TPU v7x, 32 devices: a whole 2x2x4 slice. The times are simulated.
32 devices in a mesh: dp: 8 (over y, x, core), mp: 4 (over z).
Axes of the slice: x: 2, y: 2, z: 4, core: 2. Of those that a mesh axis runs over, the one named last changes fastest.
Arguments:
- tokens: bfloat16 [2, 8192, 2560], P(None, ('dp', 'mp')), may hold values from -6 to 6
- cotangent: bfloat16 [2, 8192, 2560], P(None, ('dp', 'mp')), may hold values from -6 to 6
- parents: int32 [2, 8, 8], P(None, 'dp'), may hold values from 0 to 6, as said below
- latent_weight: float32 [2560, 1056], P('dp', 'mp'), may hold values from -0.125 to 0.125
- latent_first: float32 [2560, 1056], P('dp', 'mp')
- latent_second: float32 [2560, 1056], P('dp', 'mp'), as said below
- latent_stat: float32 [160, 16, 16], P('dp'), as said below
- latent_basis: float32 [160, 16, 16], P('dp'), as said below
- query_weight: float32 [768, 3840], P('dp', 'mp'), may hold values from -0.3125 to 0.3125
- query_first: float32 [768, 3840], P('dp', 'mp')
- query_second: float32 [768, 3840], P('dp', 'mp'), as said below
- query_stat: float32 [48, 16, 16], P('dp'), as said below
- query_basis: float32 [48, 16, 16], P('dp'), as said below
- keyval_weight: float32 [256, 5120], P('dp', 'mp'), may hold values from -0.375 to 0.375
- keyval_first: float32 [256, 5120], P('dp', 'mp')
- keyval_second: float32 [256, 5120], P('dp', 'mp'), as said below
- keyval_stat: float32 [16, 16, 16], P('dp'), as said below
- keyval_basis: float32 [16, 16, 16], P('dp'), as said below
- project_weight: float32 [2560, 2560], P('dp', 'mp'), may hold values from -4 to 4
- project_first: float32 [2560, 2560], P('dp', 'mp')
- project_second: float32 [2560, 2560], P('dp', 'mp'), as said below
- project_stat: float32 [160, 16, 16], P('dp'), as said below
- project_basis: float32 [160, 16, 16], P('dp'), as said below
- gateup_weight: float32 [2560, 2, 6400], P('dp', None, 'mp'), may hold values from -0.125 to 0.125
- gateup_first: float32 [2560, 2, 6400], P('dp', None, 'mp')
- gateup_second: float32 [2560, 2, 6400], P('dp', None, 'mp'), as said below
- gateup_stat: float32 [160, 16, 16], P('dp'), as said below
- gateup_basis: float32 [160, 16, 16], P('dp'), as said below
- down_weight: float32 [2560, 6400], P('dp', 'mp'), may hold values from -0.8 to 0.8
- down_first: float32 [2560, 6400], P('dp', 'mp')
- down_second: float32 [2560, 6400], P('dp', 'mp'), as said below
- down_stat: float32 [160, 16, 16], P('dp'), as said below
- down_basis: float32 [160, 16, 16], P('dp'), as said below
- gains: float32 [6144], P('dp'), may hold values from 0.5 to 1.5
- gains_first: float32 [6144], P('dp')
- gains_second: float32 [6144], P('dp'), as said below
Outputs:
- layer_out: bfloat16 [2, 8192, 2560], P(None, ('dp', 'mp'))
- input_grad: float32 [2, 8192, 2560], P(None, ('dp', 'mp'))
- latent_new: float32 [2560, 1056], P('dp', 'mp')
- latent_copy: bfloat16 [2560, 1056], P('dp', 'mp')
- latent_first_new: float32 [2560, 1056], P('dp', 'mp')
- latent_second_new: float32 [2560, 1056], P('dp', 'mp')
- latent_stat_new: float32 [160, 16, 16], P('dp')
- latent_basis_new: float32 [160, 16, 16], P('dp')
- query_new: float32 [768, 3840], P('dp', 'mp')
- query_copy: bfloat16 [768, 3840], P('dp', 'mp')
- query_first_new: float32 [768, 3840], P('dp', 'mp')
- query_second_new: float32 [768, 3840], P('dp', 'mp')
- query_stat_new: float32 [48, 16, 16], P('dp')
- query_basis_new: float32 [48, 16, 16], P('dp')
- keyval_new: float32 [256, 5120], P('dp', 'mp')
- keyval_copy: bfloat16 [256, 5120], P('dp', 'mp')
- keyval_first_new: float32 [256, 5120], P('dp', 'mp')
- keyval_second_new: float32 [256, 5120], P('dp', 'mp')
- keyval_stat_new: float32 [16, 16, 16], P('dp')
- keyval_basis_new: float32 [16, 16, 16], P('dp')
- project_new: float32 [2560, 2560], P('dp', 'mp')
- project_copy: bfloat16 [2560, 2560], P('dp', 'mp')
- project_first_new: float32 [2560, 2560], P('dp', 'mp')
- project_second_new: float32 [2560, 2560], P('dp', 'mp')
- project_stat_new: float32 [160, 16, 16], P('dp')
- project_basis_new: float32 [160, 16, 16], P('dp')
- gateup_new: float32 [2560, 2, 6400], P('dp', None, 'mp')
- gateup_copy: bfloat16 [2560, 2, 6400], P('dp', None, 'mp')
- gateup_first_new: float32 [2560, 2, 6400], P('dp', None, 'mp')
- gateup_second_new: float32 [2560, 2, 6400], P('dp', None, 'mp')
- gateup_stat_new: float32 [160, 16, 16], P('dp')
- gateup_basis_new: float32 [160, 16, 16], P('dp')
- down_new: float32 [2560, 6400], P('dp', 'mp')
- down_copy: bfloat16 [2560, 6400], P('dp', 'mp')
- down_first_new: float32 [2560, 6400], P('dp', 'mp')
- down_second_new: float32 [2560, 6400], P('dp', 'mp')
- down_stat_new: float32 [160, 16, 16], P('dp')
- down_basis_new: float32 [160, 16, 16], P('dp')
- gains_new: float32 [6144], P('dp')
- gains_first_new: float32 [6144], P('dp')
- gains_second_new: float32 [6144], P('dp')
Inputs may be any that keep to these rules, and one draw needn't show every extreme that they name: parents[m, d, 0] is 0 and parents[m, d, b] < b for b >= 1, so every block's path ends at block 0; the last block of every tree has block 6 as its parent. `latent_second`: positive. `latent_stat`: each block is symmetric positive definite. `latent_basis`: each block is orthogonal. `query_second`: positive. `query_stat`: each block is symmetric positive definite. `query_basis`: each block is orthogonal. `keyval_second`: positive. `keyval_stat`: each block is symmetric positive definite. `keyval_basis`: each block is orthogonal. `project_second`: positive. `project_stat`: each block is symmetric positive definite. `project_basis`: each block is orthogonal. `gateup_second`: positive. `gateup_stat`: each block is symmetric positive definite. `gateup_basis`: each block is orthogonal. `down_second`: positive. `down_stat`: each block is symmetric positive definite. `down_basis`: each block is orthogonal. `gains_second`: positive.
All inputs are finite; a program needn't handle non-finite values.
Results may differ from a plain program's by a relative error of at most 0.028.
Values may be sent and summed in bfloat16 or wider, within the bound.
No kernel may reach another device: no remote copies, remote signals or barrier semaphores. Data moves between devices by JAX's collectives and lax.ppermute only.
A program may use at most 512 MiB of HBM per device.

v0:
```python
import math

import jax
import jax.numpy as jnp
from jax import lax
from jax.sharding import PartitionSpec as P

WIDTH = 2560
HEADS = 40
QUERY_RANK = 768
LATENT_RANK = 256
NOPE_DIM = 64
ROPE_DIM = 32
VALUE_DIM = 64
BLOCK = 128
ROTATE_ROWS = 16
STEP_COUNT = 10


HIGHEST = lax.Precision.HIGHEST
NORM_EPS = 1e-05
RESIDUAL = 1.4 / math.sqrt(62.0)
ROPE_BASE = 10000.0
BETA_FIRST = 0.95
BETA_SECOND = 0.95
ADAM_EPS = 1e-08
DECAY = 0.01
RATES = (0.08, 0.2, 0.25, 3.2, 0.08, 0.56)
GAIN_RATE = 0.8


def rms_parts(values, scale_gain):
    inverse = lax.rsqrt(jnp.mean(values * values, axis=-1, keepdims=True) + NORM_EPS)
    return (values * inverse * scale_gain, inverse)


def rms_back(values, inverse, scale_gain, upstream):
    weighted = upstream * scale_gain
    inner = jnp.mean(weighted * values, axis=-1, keepdims=True)
    return inverse * weighted - values * (inverse * inverse * inverse) * inner


def rotate(values, cosine, sine_part):
    half_dim = values.shape[-1] // 2
    first_half = values[..., :half_dim]
    second_half = values[..., half_dim:]
    return jnp.concatenate(
        [
            first_half * cosine - second_half * sine_part,
            second_half * cosine + first_half * sine_part,
        ],
        axis=-1,
    )


def rotate_back(grad_in, cosine, sine_part):
    half_dim = grad_in.shape[-1] // 2
    first_half = grad_in[..., :half_dim]
    second_half = grad_in[..., half_dim:]
    return jnp.concatenate(
        [
            first_half * cosine + second_half * sine_part,
            second_half * cosine - first_half * sine_part,
        ],
        axis=-1,
    )


def tree_layout(parent):
    block_count = parent.shape[0]
    identity = jnp.eye(block_count, dtype=jnp.float32)
    blocks = jnp.arange(block_count)
    parent_of = ((parent[:, None] == blocks[None, :]) & (blocks[:, None] > 0)).astype(jnp.float32)
    reached = identity
    for unused in range(block_count):
        reached = jnp.minimum(1.0, identity + jnp.dot(parent_of, reached, precision=HIGHEST))
    depths = jnp.sum(reached, axis=1) - 1.0
    length = block_count * BLOCK
    ancestor = (
        jnp.broadcast_to(
            reached[:, None, :, None], (block_count, BLOCK, block_count, BLOCK)
        ).reshape(length, length)
        > 0.5
    )
    tokens_at = jnp.arange(length)
    same_block = tokens_at[:, None] // BLOCK == tokens_at[None, :] // BLOCK
    visible = ancestor & (jnp.logical_not(same_block) | (tokens_at[None, :] <= tokens_at[:, None]))
    position = jnp.repeat(depths, BLOCK) * BLOCK + (tokens_at % BLOCK).astype(jnp.float32)
    frequency = ROPE_BASE ** (-(jnp.arange(ROPE_DIM // 2).astype(jnp.float32) * 2.0 / ROPE_DIM))
    angles = position[:, None] * frequency[None, :]
    return (visible, jnp.cos(angles), jnp.sin(angles))


def dot_first(first_arg, second_arg):
    return lax.dot_general(
        first_arg, second_arg, (((0,), (0,)), ((), ())), preferred_element_type=jnp.float32
    )


def dot_last(first_arg, second_arg):
    return lax.dot_general(
        first_arg, second_arg, (((1,), (1,)), ((), ())), preferred_element_type=jnp.float32
    )


def gram_of(grad_w):
    blocks = grad_w.reshape(grad_w.shape[0] // ROTATE_ROWS, ROTATE_ROWS, -1)
    return jnp.einsum("bic,bjc->bij", blocks, blocks, precision=HIGHEST)


def renew(stat_m, basis_m):
    product = jnp.einsum("bij,bjk->bik", stat_m, basis_m, precision=HIGHEST)
    inner = jnp.einsum("bij,bik->bjk", product, product, precision=HIGHEST)
    factor = jnp.linalg.cholesky(inner)
    solved = jax.scipy.linalg.solve_triangular(factor, jnp.swapaxes(product, 1, 2), lower=True)
    return jnp.swapaxes(solved, 1, 2)


def rotated_update(weight, grad_w, first_m, second_m, stat_m, basis_m, gram_sum, step_rate):
    blocks = grad_w.reshape(basis_m.shape[0], basis_m.shape[1], -1)
    turned = jnp.einsum("bij,bic->bjc", basis_m, blocks, precision=HIGHEST).reshape(grad_w.shape)
    new_first = BETA_FIRST * first_m + (1.0 - BETA_FIRST) * turned
    new_second = BETA_SECOND * second_m + (1.0 - BETA_SECOND) * turned * turned
    normal_step = (
        new_first
        / (1.0 - BETA_FIRST**STEP_COUNT)
        / (jnp.sqrt(new_second / (1.0 - BETA_SECOND**STEP_COUNT)) + ADAM_EPS)
    )
    rotated_back = jnp.einsum(
        "bij,bjc->bic", basis_m, normal_step.reshape(blocks.shape), precision=HIGHEST
    ).reshape(grad_w.shape)
    new_weight = weight - step_rate * (rotated_back + DECAY * weight)
    new_stat = BETA_SECOND * stat_m + (1.0 - BETA_SECOND) * gram_sum
    return (new_weight, new_first, new_second, new_stat, renew(new_stat, basis_m))


def clip_columns(new_weight, clip_factor, head_width, rope_scaled):
    rows = new_weight.shape[0]
    root_factor = jnp.sqrt(clip_factor)
    tail_factor = clip_factor if rope_scaled else jnp.ones_like(clip_factor)
    column_scale = jnp.concatenate(
        [
            jnp.broadcast_to(root_factor[:, None], (clip_factor.shape[0], NOPE_DIM)),
            jnp.broadcast_to(tail_factor[:, None], (clip_factor.shape[0], head_width - NOPE_DIM)),
        ],
        axis=1,
    )
    return (
        new_weight.reshape(rows, clip_factor.shape[0], head_width) * column_scale[None]
    ).reshape(new_weight.shape)


def gather_weights(
    sent_latent, sent_query, sent_keyval, sent_project, sent_gateup, sent_down, sent_gains
):
    return (
        lax.all_gather(sent_latent, "dp", axis=0, tiled=True),
        lax.all_gather(sent_query, "dp", axis=0, tiled=True),
        lax.all_gather(sent_keyval, "dp", axis=0, tiled=True),
        lax.all_gather(sent_project, "dp", axis=0, tiled=True),
        lax.all_gather(sent_gateup, "dp", axis=0, tiled=True),
        lax.all_gather(sent_down, "dp", axis=0, tiled=True),
        lax.all_gather(sent_gains, "dp", axis=0, tiled=True),
    )


def on_device(
    tokens,
    cotangent,
    parents,
    latent_weight,
    latent_first,
    latent_second,
    latent_stat,
    latent_basis,
    query_weight,
    query_first,
    query_second,
    query_stat,
    query_basis,
    keyval_weight,
    keyval_first,
    keyval_second,
    keyval_stat,
    keyval_basis,
    project_weight,
    project_first,
    project_second,
    project_stat,
    project_basis,
    gateup_weight,
    gateup_first,
    gateup_second,
    gateup_stat,
    gateup_basis,
    down_weight,
    down_first,
    down_second,
    down_stat,
    down_basis,
    gains,
    gains_first,
    gains_second,
):
    matrices = (
        latent_weight,
        query_weight,
        keyval_weight,
        project_weight,
        gateup_weight,
        down_weight,
    )
    states = (
        (latent_first, latent_second, latent_stat, latent_basis),
        (query_first, query_second, query_stat, query_basis),
        (keyval_first, keyval_second, keyval_stat, keyval_basis),
        (project_first, project_second, project_stat, project_basis),
        (gateup_first, gateup_second, gateup_stat, gateup_basis),
        (down_first, down_second, down_stat, down_basis),
    )
    sent_latent = latent_weight.astype(jnp.bfloat16)
    sent_query = query_weight.astype(jnp.bfloat16)
    sent_keyval = keyval_weight.astype(jnp.bfloat16)
    sent_project = project_weight.astype(jnp.bfloat16)
    sent_gateup = gateup_weight.astype(jnp.bfloat16)
    sent_down = down_weight.astype(jnp.bfloat16)
    sent_gains = gains.astype(jnp.bfloat16)
    data_count = lax.axis_size("dp")
    share_rows = tokens.shape[1]
    model_index = lax.axis_index("mp")
    own_start = model_index * share_rows
    scale_attn = float(NOPE_DIM + ROPE_DIM) ** (-0.5)
    own_heads = query_weight.shape[1] // (NOPE_DIM + ROPE_DIM)
    shard_list = (
        sent_latent,
        sent_query,
        sent_keyval,
        sent_project,
        sent_gateup,
        sent_down,
        sent_gains,
    )
    running = tuple(
        (
            jnp.zeros((shard.shape[0] * data_count,) + shard.shape[1:], jnp.float32)
            for shard in shard_list
        )
    )
    peak_run = jnp.full((own_heads,), -1e30, jnp.float32)
    outputs = []
    input_grads = []
    for micro_index in range(tokens.shape[0]):
        gathered = gather_weights(
            sent_latent, sent_query, sent_keyval, sent_project, sent_gateup, sent_down, sent_gains
        )
        lat_w, query_w, keyval_w, output_w, gateup_w, down_w, gain_sent = gathered
        gain_all = gain_sent.astype(jnp.float32)
        gain_one = gain_all[:WIDTH]
        gain_two = gain_all[WIDTH : 2 * WIDTH]
        gain_query = gain_all[2 * WIDTH : 2 * WIDTH + QUERY_RANK]
        gain_keyval = gain_all[2 * WIDTH + QUERY_RANK :]
        tok_share = tokens[micro_index].astype(jnp.float32)
        normed, inverse_one = rms_parts(tok_share, gain_one)
        normed_full = lax.all_gather(normed.astype(jnp.bfloat16), "mp", axis=0, tiled=True)
        latent_part = jnp.dot(normed_full, lat_w, preferred_element_type=jnp.float32).astype(
            jnp.bfloat16
        )
        latent = lax.all_gather(latent_part, "mp", axis=1, tiled=True).astype(jnp.float32)
        length = latent.shape[0]
        query_raw = latent[:, :QUERY_RANK]
        keyval_raw = latent[:, QUERY_RANK : QUERY_RANK + LATENT_RANK]
        key_rope = latent[:, QUERY_RANK + LATENT_RANK :]
        query_normed, inverse_query = rms_parts(query_raw, gain_query)
        query_latent = query_normed.astype(jnp.bfloat16)
        keyval_normed, inverse_keyval = rms_parts(keyval_raw, gain_keyval)
        keyval_latent = keyval_normed.astype(jnp.bfloat16)
        local_heads = query_w.shape[1] // (NOPE_DIM + ROPE_DIM)
        query_all = jnp.dot(query_latent, query_w, preferred_element_type=jnp.float32).reshape(
            length, local_heads, NOPE_DIM + ROPE_DIM
        )
        keyval = jnp.dot(keyval_latent, keyval_w, preferred_element_type=jnp.float32).reshape(
            length, local_heads, NOPE_DIM + VALUE_DIM
        )
        visible, cosine, sine_part = tree_layout(parents[micro_index, 0])
        head_cos = cosine[:, None, :]
        head_sin = sine_part[:, None, :]
        queries = jnp.concatenate(
            [query_all[..., :NOPE_DIM], rotate(query_all[..., NOPE_DIM:], head_cos, head_sin)],
            axis=-1,
        ).astype(jnp.bfloat16)
        shared = rotate(key_rope, cosine, sine_part)
        keys_all = jnp.concatenate(
            [
                keyval[..., :NOPE_DIM],
                jnp.broadcast_to(shared[:, None, :], (length, local_heads, ROPE_DIM)),
            ],
            axis=-1,
        ).astype(jnp.bfloat16)
        values_all = keyval[..., NOPE_DIM:].astype(jnp.bfloat16)
        scores = (
            jnp.einsum("qhd,khd->hqk", queries, keys_all, preferred_element_type=jnp.float32)
            * scale_attn
        )
        scores = jnp.where(visible[None], scores, -1e30)
        row_top = jnp.max(scores, axis=-1, keepdims=True)
        peak_run = jnp.maximum(peak_run, jnp.max(row_top[..., 0], axis=-1))
        weights = jnp.exp(scores - row_top)
        row_sum = jnp.sum(weights, axis=-1, keepdims=True)
        log_total = row_top + jnp.log(row_sum)
        probs = weights / row_sum
        attended = (
            jnp.einsum(
                "hqk,khd->qhd",
                probs.astype(jnp.bfloat16),
                values_all,
                preferred_element_type=jnp.float32,
            )
            .astype(jnp.bfloat16)
            .reshape(length, local_heads * VALUE_DIM)
        )
        branch = lax.psum_scatter(
            dot_last(attended, output_w).astype(jnp.bfloat16), "mp", scatter_dimension=0, tiled=True
        ).astype(jnp.float32)
        hidden = tok_share + RESIDUAL * branch
        normed_two, inverse_two = rms_parts(hidden, gain_two)
        normed_two_full = lax.all_gather(normed_two.astype(jnp.bfloat16), "mp", axis=0, tiled=True)
        gateup = jnp.einsum(
            "ld,dkf->lkf", normed_two_full, gateup_w, preferred_element_type=jnp.float32
        )
        gate_part = gateup[:, 0]
        up_part = gateup[:, 1]
        sigmoid_gate = jax.nn.sigmoid(gate_part)
        silu_gate = gate_part * sigmoid_gate
        activated = (silu_gate * up_part).astype(jnp.bfloat16)
        mixed_out = lax.psum_scatter(
            dot_last(activated, down_w).astype(jnp.bfloat16), "mp", scatter_dimension=0, tiled=True
        ).astype(jnp.float32)
        outputs.append((hidden + RESIDUAL * mixed_out).astype(jnp.bfloat16))
        gathered = gather_weights(
            sent_latent, sent_query, sent_keyval, sent_project, sent_gateup, sent_down, sent_gains
        )
        lat_w, query_w, keyval_w, output_w, gateup_w, down_w, gain_sent = gathered
        grad_out = cotangent[micro_index].astype(jnp.float32)
        mixed_full = lax.all_gather(
            (RESIDUAL * grad_out).astype(jnp.bfloat16), "mp", axis=0, tiled=True
        )
        grad_act = jnp.dot(mixed_full, down_w, preferred_element_type=jnp.float32)
        grad_down = dot_first(mixed_full, activated)
        grad_gate = grad_act * up_part * sigmoid_gate * (1.0 + gate_part * (1.0 - sigmoid_gate))
        grad_up = grad_act * silu_gate
        grad_gateup = jnp.stack([grad_gate, grad_up], axis=1).astype(jnp.bfloat16)
        grad_gateup_w = jnp.einsum(
            "ld,lkf->dkf", normed_two_full, grad_gateup, preferred_element_type=jnp.float32
        )
        grad_normed_two = lax.psum_scatter(
            jnp.einsum(
                "lkf,dkf->ld", grad_gateup, gateup_w, preferred_element_type=jnp.float32
            ).astype(jnp.bfloat16),
            "mp",
            scatter_dimension=0,
            tiled=True,
        ).astype(jnp.float32)
        grad_hidden = grad_out + rms_back(hidden, inverse_two, gain_two, grad_normed_two)
        grad_gain_two = jnp.sum(grad_normed_two * hidden * inverse_two, axis=0)
        branch_full = lax.all_gather(
            (RESIDUAL * grad_hidden).astype(jnp.bfloat16), "mp", axis=0, tiled=True
        )
        grad_output_w = dot_first(branch_full, attended)
        grad_attended = (
            jnp.dot(branch_full, output_w, preferred_element_type=jnp.float32)
            .astype(jnp.bfloat16)
            .reshape(length, local_heads, VALUE_DIM)
        )
        scores_again = (
            jnp.einsum("qhd,khd->hqk", queries, keys_all, preferred_element_type=jnp.float32)
            * scale_attn
        )
        probs_again = jnp.exp(jnp.where(visible[None], scores_again, -1e30) - log_total)
        grad_probs = jnp.einsum(
            "qhd,khd->hqk", grad_attended, values_all, preferred_element_type=jnp.float32
        )
        grad_scores = (
            probs_again * (grad_probs - jnp.sum(probs_again * grad_probs, axis=-1, keepdims=True))
        ).astype(jnp.bfloat16)
        grad_queries = (
            jnp.einsum("hqk,khd->qhd", grad_scores, keys_all, preferred_element_type=jnp.float32)
            * scale_attn
        )
        grad_keys = (
            jnp.einsum("hqk,qhd->khd", grad_scores, queries, preferred_element_type=jnp.float32)
            * scale_attn
        )
        grad_values = jnp.einsum(
            "hqk,qhd->khd",
            probs_again.astype(jnp.bfloat16),
            grad_attended,
            preferred_element_type=jnp.float32,
        )
        grad_query_all = (
            jnp.concatenate(
                [
                    grad_queries[..., :NOPE_DIM],
                    rotate_back(grad_queries[..., NOPE_DIM:], head_cos, head_sin),
                ],
                axis=-1,
            )
            .astype(jnp.bfloat16)
            .reshape(length, local_heads * (NOPE_DIM + ROPE_DIM))
        )
        grad_keyval = (
            jnp.concatenate([grad_keys[..., :NOPE_DIM], grad_values], axis=-1)
            .astype(jnp.bfloat16)
            .reshape(length, local_heads * (NOPE_DIM + VALUE_DIM))
        )
        grad_shared = rotate_back(jnp.sum(grad_keys[..., NOPE_DIM:], axis=1), cosine, sine_part)
        grad_query_w = dot_first(query_latent, grad_query_all)
        grad_keyval_w = dot_first(keyval_latent, grad_keyval)
        latent_terms = jnp.concatenate(
            [dot_last(grad_query_all, query_w), dot_last(grad_keyval, keyval_w), grad_shared],
            axis=1,
        )
        grad_latent_all = lax.psum(latent_terms.astype(jnp.bfloat16), "mp").astype(jnp.float32)
        grad_query_up = grad_latent_all[:, :QUERY_RANK]
        grad_keyval_up = grad_latent_all[:, QUERY_RANK : QUERY_RANK + LATENT_RANK]
        grad_latent = jnp.concatenate(
            [
                rms_back(query_raw, inverse_query, gain_query, grad_query_up),
                rms_back(keyval_raw, inverse_keyval, gain_keyval, grad_keyval_up),
                grad_latent_all[:, QUERY_RANK + LATENT_RANK :],
            ],
            axis=1,
        ).astype(jnp.bfloat16)
        grad_gain_query = jnp.sum(
            lax.dynamic_slice_in_dim(
                grad_query_up * query_raw * inverse_query, own_start, share_rows, 0
            ),
            axis=0,
        )
        grad_gain_keyval = jnp.sum(
            lax.dynamic_slice_in_dim(
                grad_keyval_up * keyval_raw * inverse_keyval, own_start, share_rows, 0
            ),
            axis=0,
        )
        column_count = latent_part.shape[1]
        grad_columns = lax.dynamic_slice_in_dim(
            grad_latent, model_index * column_count, column_count, 1
        )
        grad_latent_w = dot_first(normed_full, grad_columns)
        grad_normed = lax.psum_scatter(
            dot_last(grad_columns, lat_w).astype(jnp.bfloat16),
            "mp",
            scatter_dimension=0,
            tiled=True,
        ).astype(jnp.float32)
        input_grads.append(grad_hidden + rms_back(tok_share, inverse_one, gain_one, grad_normed))
        grad_gain_one = jnp.sum(grad_normed * tok_share * inverse_one, axis=0)
        grad_gains = jnp.concatenate(
            [grad_gain_one, grad_gain_two, grad_gain_query, grad_gain_keyval]
        )
        micro_grads = (
            grad_latent_w,
            grad_query_w,
            grad_keyval_w,
            grad_output_w,
            grad_gateup_w,
            grad_down,
            grad_gains,
        )
        running = tuple((sum_old + sum_new for sum_old, sum_new in zip(running, micro_grads)))
    head_top = lax.pmax(peak_run, "dp")
    peak_row = lax.dynamic_update_slice(
        jnp.zeros((HEADS,), jnp.float32), head_top, (model_index * own_heads,)
    )
    reduced = (
        lax.psum_scatter(
            running[0].astype(jnp.bfloat16), "dp", scatter_dimension=0, tiled=True
        ).astype(jnp.float32),
        lax.psum_scatter(
            running[1].astype(jnp.bfloat16), "dp", scatter_dimension=0, tiled=True
        ).astype(jnp.float32),
        lax.psum_scatter(
            running[2].astype(jnp.bfloat16), "dp", scatter_dimension=0, tiled=True
        ).astype(jnp.float32),
        lax.psum_scatter(
            running[3].astype(jnp.bfloat16), "dp", scatter_dimension=0, tiled=True
        ).astype(jnp.float32),
        lax.psum_scatter(
            running[4].astype(jnp.bfloat16), "dp", scatter_dimension=0, tiled=True
        ).astype(jnp.float32),
        lax.psum_scatter(
            running[5].astype(jnp.bfloat16), "dp", scatter_dimension=0, tiled=True
        ).astype(jnp.float32),
        lax.psum_scatter(
            running[6].astype(jnp.bfloat16), "dp", scatter_dimension=0, tiled=True
        ).astype(jnp.float32),
    )
    grams = [gram_of(reduced[mat_index]) for mat_index in range(6)]
    summed = (
        lax.psum(grams[0].astype(jnp.bfloat16), "mp").astype(jnp.float32),
        lax.psum(grams[1].astype(jnp.bfloat16), "mp").astype(jnp.float32),
        lax.psum(grams[2].astype(jnp.bfloat16), "mp").astype(jnp.float32),
        lax.psum(grams[3].astype(jnp.bfloat16), "mp").astype(jnp.float32),
        lax.psum(grams[4].astype(jnp.bfloat16), "mp").astype(jnp.float32),
        lax.psum(grams[5].astype(jnp.bfloat16), "mp").astype(jnp.float32),
        lax.psum(reduced[6].astype(jnp.bfloat16), "mp").astype(jnp.float32),
        lax.psum(peak_row.astype(jnp.bfloat16), "mp").astype(jnp.float32),
    )
    all_peaks = summed[7]
    threshold = jnp.mean(all_peaks)
    clip_all = jnp.minimum(1.0, threshold / jnp.maximum(all_peaks, 1.0))
    clip_own = lax.dynamic_slice_in_dim(clip_all, model_index * own_heads, own_heads, 0)
    results = [jnp.stack(outputs), jnp.stack(input_grads)]
    for mat_index in range(6):
        first_m, second_m, stat_m, basis_m = states[mat_index]
        new_weight, new_first, new_second, new_stat, new_basis = rotated_update(
            matrices[mat_index],
            reduced[mat_index],
            first_m,
            second_m,
            stat_m,
            basis_m,
            summed[mat_index],
            RATES[mat_index],
        )
        if mat_index == 1:
            new_weight = clip_columns(new_weight, clip_own, NOPE_DIM + ROPE_DIM, True)
        if mat_index == 2:
            new_weight = clip_columns(new_weight, clip_own, NOPE_DIM + VALUE_DIM, False)
        results.extend(
            [
                new_weight,
                new_weight.astype(jnp.bfloat16),
                new_first,
                new_second,
                new_stat,
                new_basis,
            ]
        )
    gains_grad = summed[6]
    gains_first_new = BETA_FIRST * gains_first + (1.0 - BETA_FIRST) * gains_grad
    gains_second_new = BETA_SECOND * gains_second + (1.0 - BETA_SECOND) * gains_grad * gains_grad
    gains_step = (
        gains_first_new
        / (1.0 - BETA_FIRST**STEP_COUNT)
        / (jnp.sqrt(gains_second_new / (1.0 - BETA_SECOND**STEP_COUNT)) + ADAM_EPS)
    )
    results.extend(
        [gains - GAIN_RATE * (gains_step + DECAY * gains), gains_first_new, gains_second_new]
    )
    return (
        results[0],
        results[1],
        results[2],
        results[3],
        results[4],
        results[5],
        results[6],
        results[7],
        results[8],
        results[9],
        results[10],
        results[11],
        results[12],
        results[13],
        results[14],
        results[15],
        results[16],
        results[17],
        results[18],
        results[19],
        results[20],
        results[21],
        results[22],
        results[23],
        results[24],
        results[25],
        results[26],
        results[27],
        results[28],
        results[29],
        results[30],
        results[31],
        results[32],
        results[33],
        results[34],
        results[35],
        results[36],
        results[37],
        results[38],
        results[39],
        results[40],
    )


def solution(mesh):
    placed = (
        P(None, ("dp", "mp"), None),
        P(None, ("dp", "mp"), None),
        P(None, "dp", None),
        P("dp", "mp"),
        P("dp", "mp"),
        P("dp", "mp"),
        P("dp", None, None),
        P("dp", None, None),
        P("dp", "mp"),
        P("dp", "mp"),
        P("dp", "mp"),
        P("dp", None, None),
        P("dp", None, None),
        P("dp", "mp"),
        P("dp", "mp"),
        P("dp", "mp"),
        P("dp", None, None),
        P("dp", None, None),
        P("dp", "mp"),
        P("dp", "mp"),
        P("dp", "mp"),
        P("dp", None, None),
        P("dp", None, None),
        P("dp", None, "mp"),
        P("dp", None, "mp"),
        P("dp", None, "mp"),
        P("dp", None, None),
        P("dp", None, None),
        P("dp", "mp"),
        P("dp", "mp"),
        P("dp", "mp"),
        P("dp", None, None),
        P("dp", None, None),
        P("dp"),
        P("dp"),
        P("dp"),
    )
    return jax.shard_map(
        on_device,
        mesh=mesh,
        in_specs=placed,
        out_specs=(
            P(None, ("dp", "mp"), None),
            P(None, ("dp", "mp"), None),
            P("dp", "mp"),
            P("dp", "mp"),
            P("dp", "mp"),
            P("dp", "mp"),
            P("dp", None, None),
            P("dp", None, None),
            P("dp", "mp"),
            P("dp", "mp"),
            P("dp", "mp"),
            P("dp", "mp"),
            P("dp", None, None),
            P("dp", None, None),
            P("dp", "mp"),
            P("dp", "mp"),
            P("dp", "mp"),
            P("dp", "mp"),
            P("dp", None, None),
            P("dp", None, None),
            P("dp", "mp"),
            P("dp", "mp"),
            P("dp", "mp"),
            P("dp", "mp"),
            P("dp", None, None),
            P("dp", None, None),
            P("dp", None, "mp"),
            P("dp", None, "mp"),
            P("dp", None, "mp"),
            P("dp", None, "mp"),
            P("dp", None, None),
            P("dp", None, None),
            P("dp", "mp"),
            P("dp", "mp"),
            P("dp", "mp"),
            P("dp", "mp"),
            P("dp", None, None),
            P("dp", None, None),
            P("dp"),
            P("dp"),
            P("dp"),
        ),
        check_vma=False,
    )
```

profile of v0, /device:TPU:0, one launch (start us, length us, event | category | flops | bytes accessed | tf_op | source)
XLA Modules:
  0.0 2998.1 jit_solution(512008654507779151)
XLA Ops:
  41.9 97.5 %all-gather.32.cloned.1.call-done = bf16[1024,2560]{1,0:T(8,128)(2,1)} async-done(((bf16[256,2560]{1,0:T(8,128)(2,1)}), bf16[1024,2560]{1,0:T(8,128)(2,1)}) %all-gather.32.cloned.1.call-update) | async-done | bytes 5242896 | tf_op jit(solution)/shard_map/all_gather | solution.py:264
  144.4 93.6 %all-gather.18.cloned.1.call-done = bf16[1024,2560]{1,0:T(8,128)(2,1)} async-done(((bf16[256,2560]{1,0:T(8,128)(2,1)}), bf16[1024,2560]{1,0:T(8,128)(2,1)}) %all-gather.18.cloned.1.call-update) | async-done | bytes 5242896 | tf_op jit(solution)/shard_map/all_gather | solution.py:264
  290.2 43.5 %all-gather.20.cloned.1.call-done = bf16[1024,1056]{0,1:T(8,128)(2,1)} async-done(((bf16[1024,264]{0,1:T(8,128)(2,1)}), bf16[1024,1056]{0,1:T(8,128)(2,1)}) %all-gather.20.cloned.1.call-update) | async-done | bytes 2162704 | tf_op jit(solution)/shard_map/all_gather | solution.py:268
  527.3 97.2 %reduce-scatter.17.cloned.1.call-done = bf16[256,2560]{1,0:T(8,128)(2,1)} async-done(((bf16[1024,2560]{1,0:T(8,128)(2,1)}), bf16[256,2560]{1,0:T(8,128)(2,1)}) %reduce-scatter.17.cloned.1.call-update) | async-done | bytes 1310736 | tf_op jit(solution)/shard_map/reduce_scatter | solution.py:321
  638.0 80.3 %all-gather.28.cloned.1.call-done = bf16[2560,2,1600]{2,0,1:T(8,128)(2,1)} async-done(((bf16[320,2,1600]{2,0,1:T(8,128)(2,1)}), bf16[2560,2,1600]{2,0,1:T(8,128)(2,1)}) %all-gather.28.cloned.1.call-update) | async-done | bytes 16384016 | tf_op jit(solution)/shard_map/all_gather | solution.py:161
  718.3 100.2 %all-gather.36.cloned.1.call-done = bf16[1024,2560]{1,0:T(8,128)(2,1)} async-done(((bf16[256,2560]{1,0:T(8,128)(2,1)}), bf16[1024,2560]{1,0:T(8,128)(2,1)}) %all-gather.36.cloned.1.call-update) | async-done | bytes 5242896 | tf_op jit(solution)/shard_map/all_gather | solution.py:326
  843.9 73.1 %all-gather.42.cloned.1.call-done = bf16[1024,2560]{1,0:T(8,128)(2,1)} async-done(((bf16[256,2560]{1,0:T(8,128)(2,1)}), bf16[1024,2560]{1,0:T(8,128)(2,1)}) %all-gather.42.cloned.1.call-update) | async-done | bytes 5242896 | tf_op jit(solution)/shard_map/all_gather | solution.py:344
  917.0 55.8 %all-gather.30.cloned.1.call-done = bf16[2560,1600]{1,0:T(8,128)(2,1)} async-done(((bf16[320,1600]{1,0:T(8,128)(2,1)}), bf16[2560,1600]{1,0:T(8,128)(2,1)}) %all-gather.30.cloned.1.call-update) | async-done | bytes 8192016 | tf_op jit(solution)/shard_map/all_gather | solution.py:162
  1017.5 55.4 %all-gather.26.cloned.1.call-done = bf16[1024,2560]{1,0:T(8,128)(2,1)} async-done(((bf16[256,2560]{1,0:T(8,128)(2,1)}), bf16[1024,2560]{1,0:T(8,128)(2,1)}) %all-gather.26.cloned.1.call-update) | async-done | bytes 5242896 | tf_op jit(solution)/shard_map/all_gather | solution.py:326
  1098.3 73.1 %all-gather.38.cloned.1.call-done = bf16[1024,2560]{1,0:T(8,128)(2,1)} async-done(((bf16[256,2560]{1,0:T(8,128)(2,1)}), bf16[1024,2560]{1,0:T(8,128)(2,1)}) %all-gather.38.cloned.1.call-update) | async-done | bytes 5242896 | tf_op jit(solution)/shard_map/all_gather | solution.py:344
  1265.7 97.0 %reduce-scatter.25.cloned.1.call-done = bf16[256,2560]{1,0:T(8,128)(2,1)} async-done(((bf16[1024,2560]{1,0:T(8,128)(2,1)}), bf16[256,2560]{1,0:T(8,128)(2,1)}) %reduce-scatter.25.cloned.1.call-update) | async-done | bytes 1310736 | tf_op jit(solution)/shard_map/reduce_scatter | solution.py:355
  1367.7 91.5 %reduce-scatter.23.cloned.1.call-done = bf16[256,2560]{1,0:T(8,128)(2,1)} async-done(((bf16[1024,2560]{1,0:T(8,128)(2,1)}), bf16[256,2560]{1,0:T(8,128)(2,1)}) %reduce-scatter.23.cloned.1.call-update) | async-done | bytes 1310736 | tf_op jit(solution)/shard_map/reduce_scatter | solution.py:335
  1459.1 96.6 %reduce-scatter.19.cloned.1.call-done = bf16[256,2560]{1,0:T(8,128)(2,1)} async-done(((bf16[1024,2560]{1,0:T(8,128)(2,1)}), bf16[256,2560]{1,0:T(8,128)(2,1)}) %reduce-scatter.19.cloned.1.call-update) | async-done | bytes 1310736 | tf_op jit(solution)/shard_map/reduce_scatter | solution.py:335
  1564.7 97.9 %all-gather.40.cloned.1.call-done = bf16[1024,2560]{1,0:T(8,128)(2,1)} async-done(((bf16[256,2560]{1,0:T(8,128)(2,1)}), bf16[1024,2560]{1,0:T(8,128)(2,1)}) %all-gather.40.cloned.1.call-update) | async-done | bytes 5242896 | tf_op jit(solution)/shard_map/all_gather | solution.py:365
  1669.7 29.6 fusion.265
  1699.3 34.5 %multiply_convert_fusion.1 = bf16[10,1024,1024]{1,2,0:T(8,128)(2,1)} fusion(f32[10,1024,1024]{1,2,0:T(8,128)} %get-tuple-element.449, f32[10,1024,1024]{1,2,0:T(8,128)} %get-tuple-element.445, f32[10,1024]{1,0:T(8,128)S(1)} %get-tuple-element.290, f32[10,1024]{1,0:T(8,128)S(1)} %log_add_fusion.1), kind=kLoop, calls=%fused_computation.3 | loop fusion | flops 41943040 | bytes 104939520 | tf_op jit(solution)/shard_map/convert_element_type | solution.py:384
  1803.3 28.8 fusion.266
  1832.1 33.8 %multiply_convert_fusion = bf16[10,1024,1024]{1,2,0:T(8,128)(2,1)} fusion(f32[10,1024,1024]{1,2,0:T(8,128)} %get-tuple-element.448, f32[10,1024,1024]{1,2,0:T(8,128)} %get-tuple-element.447, f32[10,1024]{1,0:T(8,128)S(1)} %get-tuple-element.292, f32[10,1024]{1,0:T(8,128)S(1)} %log_add_fusion), kind=kLoop, calls=%fused_computation | loop fusion | flops 41943040 | bytes 104939520 | tf_op jit(solution)/shard_map/convert_element_type | solution.py:384
  1994.4 27.4 add_convert_fusion
  2022.0 40.7 %all-reduce.6.cloned.1.call-done = (bf16[1024,1056]{0,1:T(8,128)(2,1)}, bf16[1024,1056]{0,1:T(8,128)(2,1)}) async-done(((bf16[1024,1056]{0,1:T(8,128)(2,1)}, bf16[1024,1056]{0,1:T(8,128)(2,1)}), (bf16[1024,1056]{0,1:T(8,128)(2,1)}, bf16[1024,1056]{0,1:T(8,128)(2,1)})) %all-reduce.6.cloned.1.call-update) | async-done | bytes 4325392 | tf_op jit(solution)/shard_map/psum | solution.py:422
  2187.4 30.0 %reduce-scatter.33.cloned.1.call-done = bf16[96,960]{1,0:T(8,128)(2,1)} async-done(((bf16[768,960]{1,0:T(8,128)(2,1)}), bf16[96,960]{1,0:T(8,128)(2,1)}) %reduce-scatter.33.cloned.1.call-update) | async-done | bytes 184336 | tf_op jit(solution)/shard_map/reduce_scatter | solution.py:479
  2232.1 36.1 %reduce-scatter.37.cloned.1.call-done = bf16[320,640]{1,0:T(8,128)(2,1)} async-done(((bf16[2560,640]{1,0:T(8,128)(2,1)}), bf16[320,640]{1,0:T(8,128)(2,1)}) %reduce-scatter.37.cloned.1.call-update) | async-done | bytes 409616 | tf_op jit(solution)/shard_map/reduce_scatter | solution.py:485
  2275.4 113.6 %reduce-scatter.39.cloned.1.call-done = bf16[320,2,1600]{2,0,1:T(8,128)(2,1)} async-done(((bf16[2560,2,1600]{2,0,1:T(8,128)(2,1)}), bf16[320,2,1600]{2,0,1:T(8,128)(2,1)}) %reduce-scatter.39.cloned.1.call-update) | async-done | bytes 2048016 | tf_op jit(solution)/shard_map/reduce_scatter | solution.py:488
  2468.8 60.2 %reduce-scatter.31.cloned.1.call-done = bf16[256,2560]{1,0:T(8,128)(2,1)} async-done(((bf16[1024,2560]{1,0:T(8,128)(2,1)}), bf16[256,2560]{1,0:T(8,128)(2,1)}) %reduce-scatter.31.cloned.1.call-update) | async-done | bytes 1310736 | tf_op jit(solution)/shard_map/reduce_scatter | solution.py:450
  2529.0 97.1 %reduce-scatter.27.cloned.1.call-done = bf16[256,2560]{1,0:T(8,128)(2,1)} async-done(((bf16[1024,2560]{1,0:T(8,128)(2,1)}), bf16[256,2560]{1,0:T(8,128)(2,1)}) %reduce-scatter.27.cloned.1.call-update) | async-done | bytes 1310736 | tf_op jit(solution)/shard_map/reduce_scatter | solution.py:450
  2736.9 30.6 %custom-call.36 = f32[20,16,16]{2,1,0:T(8,128)} custom-call(f32[20,16,16]{2,1,0:T(8,128)} %fusion.135), custom_call_target="Cholesky" | custom-call | tf_op jit(solution)/shard_map/jit(cholesky)/cholesky | solution.py:114
  2770.9 30.6 %custom-call.34 = f32[20,16,16]{2,1,0:T(8,128)} custom-call(f32[20,16,16]{2,1,0:T(8,128)} %fusion.138), custom_call_target="Cholesky" | custom-call | tf_op jit(solution)/shard_map/jit(cholesky)/cholesky | solution.py:114
  2804.9 30.6 %custom-call.32 = f32[20,16,16]{2,1,0:T(8,128)} custom-call(f32[20,16,16]{2,1,0:T(8,128)} %fusion.141), custom_call_target="Cholesky" | custom-call | tf_op jit(solution)/shard_map/jit(cholesky)/cholesky | solution.py:114
  2837.9 30.0 %custom-call.38 = f32[20,16,16]{2,1,0:T(8,128)S(1)} custom-call(f32[20,16,16]{2,1,0:T(8,128)} %fusion.132), custom_call_target="Cholesky" | custom-call | tf_op jit(solution)/shard_map/jit(cholesky)/cholesky | solution.py:114
  2872.9 26.1 custom-call.39
  2901.2 25.4 custom-call.37
  2928.0 25.4 custom-call.35
  (733 shorter events, 1096.2 us)
Async XLA Ops:
  7.2 2211.6 %copy-start = (f32[6,16,16]{2,1,0:T(8,128)S(1)}, f32[6,16,16]{2,1,0:T(8,128)}, u32[]{:S(2)}) copy-start(f32[6,16,16]{2,1,0:T(8,128)} %param.51) | copy-start | bytes 18436
  7.3 31.9 %all-gather.46.cloned.1.call-start = ((), (), s32[]{:S(2)}) async-start(), calls=%async_computation.41 | async-start | bytes 1824768 | tf_op jit(solution)/shard_map/all_gather | solution.py:157
  9.2 130.2 %all-gather.32.cloned.1.call-start = ((), (), s32[]{:S(2)}) async-start(), calls=%async_computation.23 | async-start | bytes 6553600 | tf_op jit(solution)/shard_map/all_gather | solution.py:264
  26.2 211.8 %all-gather.18.cloned.1.call-start = ((), (), s32[]{:S(2)}) async-start(), calls=%async_computation.14 | async-start | bytes 6553600 | tf_op jit(solution)/shard_map/all_gather | solution.py:264
  27.0 258.8 %all-gather.34.cloned.1.call-start = ((), (), s32[]{:S(2)}) async-start(), calls=%async_computation.24 | async-start | bytes 2703360 | tf_op jit(solution)/shard_map/all_gather | solution.py:268
  144.4 189.3 %all-gather.20.cloned.1.call-start = ((), (), s32[]{:S(2)}) async-start(), calls=%async_computation.15 | async-start | bytes 2703360 | tf_op jit(solution)/shard_map/all_gather | solution.py:268
  243.0 119.5 %all-gather.22.cloned.1.call-start = ((), (), s32[]{:S(2)}) async-start(), calls=%async_computation.16 | async-start | bytes 1769472 | tf_op jit(solution)/shard_map/all_gather | solution.py:158
  243.8 181.9 %all-gather.24.cloned.1.call-start = ((), (), s32[]{:S(2)}) async-start(), calls=%async_computation.17 | async-start | bytes 3686400 | tf_op jit(solution)/shard_map/all_gather | solution.py:160
  244.6 282.6 %reduce-scatter.21.cloned.1.call-start = ((), (), s32[]{:S(2)}) async-start(), calls=%async_computation.25 | async-start | bytes 6553600 | tf_op jit(solution)/shard_map/reduce_scatter | solution.py:321
  434.6 189.9 %reduce-scatter.17.cloned.1.call-start = ((), (), s32[]{:S(2)}) async-start(), calls=%async_computation.18 | async-start | bytes 6553600 | tf_op jit(solution)/shard_map/reduce_scatter | solution.py:321
  498.9 219.4 %all-gather.28.cloned.1.call-start = ((), (), s32[]{:S(2)}) async-start(), calls=%async_computation.20 | async-start | bytes 19169280 | tf_op jit(solution)/shard_map/all_gather | solution.py:161
  502.9 315.6 %all-gather.36.cloned.1.call-start = ((), (), s32[]{:S(2)}) async-start(), calls=%async_computation.26 | async-start | bytes 6553600 | tf_op jit(solution)/shard_map/all_gather | solution.py:326
  631.4 285.6 %all-gather.42.cloned.1.call-start = ((), (), s32[]{:S(2)}) async-start(), calls=%async_computation.32 | async-start | bytes 6553600 | tf_op jit(solution)/shard_map/all_gather | solution.py:344
  635.2 337.6 %all-gather.30.cloned.1.call-start = ((), (), s32[]{:S(2)}) async-start(), calls=%async_computation.21 | async-start | bytes 9584640 | tf_op jit(solution)/shard_map/all_gather | solution.py:162
  636.4 436.5 %all-gather.26.cloned.1.call-start = ((), (), s32[]{:S(2)}) async-start(), calls=%async_computation.19 | async-start | bytes 6553600 | tf_op jit(solution)/shard_map/all_gather | solution.py:326
  637.0 534.4 %all-gather.38.cloned.1.call-start = ((), (), s32[]{:S(2)}) async-start(), calls=%async_computation.28 | async-start | bytes 6553600 | tf_op jit(solution)/shard_map/all_gather | solution.py:344
  637.6 628.1 %reduce-scatter.29.cloned.1.call-start = ((), (), s32[]{:S(2)}) async-start(), calls=%async_computation.33 | async-start | bytes 6553600 | tf_op jit(solution)/shard_map/reduce_scatter | solution.py:355
  1017.5 345.2 %reduce-scatter.25.cloned.1.call-start = ((), (), s32[]{:S(2)}) async-start(), calls=%async_computation.29 | async-start | bytes 6553600 | tf_op jit(solution)/shard_map/reduce_scatter | solution.py:355
  1217.4 241.7 %reduce-scatter.23.cloned.1.call-start = ((), (), s32[]{:S(2)}) async-start(), calls=%async_computation.27 | async-start | bytes 6553600 | tf_op jit(solution)/shard_map/reduce_scatter | solution.py:335
  1232.2 323.5 %reduce-scatter.19.cloned.1.call-start = ((), (), s32[]{:S(2)}) async-start(), calls=%async_computation.22 | async-start | bytes 6553600 | tf_op jit(solution)/shard_map/reduce_scatter | solution.py:335
  1246.4 309.3 %copy-start.147 = (f32[256]{0:T(256)S(1)}, f32[256]{0:T(256)}, u32[]{:S(2)}) copy-start(f32[256]{0:T(256)} %get-tuple-element.428) | copy-start | bytes 3076
  1246.5 416.1 %all-gather.40.cloned.1.call-start = ((), (), s32[]{:S(2)}) async-start(), calls=%async_computation.30 | async-start | bytes 6553600 | tf_op jit(solution)/shard_map/all_gather | solution.py:365
  1563.9 214.1 %all-gather.44.cloned.1.call-start = ((), (), s32[]{:S(2)}) async-start(), calls=%async_computation.34 | async-start | bytes 6553600 | tf_op jit(solution)/shard_map/all_gather | solution.py:365
  1564.6 498.1 %all-reduce.6.cloned.1.call-start = ((), (), s32[]{:S(2)}) async-start(), calls=%async_computation.43 | async-start | bytes 8650752 | tf_op jit(solution)/shard_map/psum | solution.py:422
  1904.5 232.8 %reduce-scatter.41.cloned.1.call-start = ((), (), s32[]{:S(2)}) async-start(), calls=%async_computation.40 | async-start | bytes 9584640 | tf_op jit(solution)/shard_map/reduce_scatter | solution.py:491
  1938.0 237.4 %reduce-scatter.35.cloned.1.call-start = ((), (), s32[]{:S(2)}) async-start(), calls=%async_computation.37 | async-start | bytes 737280 | tf_op jit(solution)/shard_map/reduce_scatter | solution.py:482
  1944.2 273.3 %reduce-scatter.33.cloned.1.call-start = ((), (), s32[]{:S(2)}) async-start(), calls=%async_computation.36 | async-start | bytes 1769472 | tf_op jit(solution)/shard_map/reduce_scatter | solution.py:479
  1953.4 314.7 %reduce-scatter.37.cloned.1.call-start = ((), (), s32[]{:S(2)}) async-start(), calls=%async_computation.38 | async-start | bytes 3686400 | tf_op jit(solution)/shard_map/reduce_scatter | solution.py:485
  1968.7 420.4 %reduce-scatter.39.cloned.1.call-start = ((), (), s32[]{:S(2)}) async-start(), calls=%async_computation.39 | async-start | bytes 19169280 | tf_op jit(solution)/shard_map/reduce_scatter | solution.py:488
  2021.8 433.2 %reduce-scatter.43.cloned.1.call-start = ((), (), s32[]{:S(2)}) async-start(), calls=%async_computation.42 | async-start | bytes 2211840 | tf_op jit(solution)/shard_map/reduce_scatter | solution.py:476
  2085.1 443.9 %reduce-scatter.31.cloned.1.call-start = ((), (), s32[]{:S(2)}) async-start(), calls=%async_computation.35 | async-start | bytes 6553600 | tf_op jit(solution)/shard_map/reduce_scatter | solution.py:450
  2092.3 533.8 %reduce-scatter.27.cloned.1.call-start = ((), (), s32[]{:S(2)}) async-start(), calls=%async_computation.31 | async-start | bytes 6553600 | tf_op jit(solution)/shard_map/reduce_scatter | solution.py:450
  (170 other events, 3898.0 us)
Sparse Core Ops, SparseCore 0:
  10.5 28.5 all-gather.45
  41.3 98.0 all-gather.31
  141.6 96.4 all-gather.17
  240.0 45.7 all-gather.33
  287.8 45.8 all-gather.19
  336.0 24.4 all-gather.21
  362.9 32.8 all-gather.23
  434.7 92.5 reduce-scatter.20
  530.1 94.2 reduce-scatter.16
  626.8 91.4 all-gather.27
  720.4 98.0 all-gather.35
  820.5 96.4 all-gather.41
  919.4 53.3 all-gather.29
  974.8 98.0 all-gather.25
  1074.9 96.4 all-gather.37
  1173.5 92.1 reduce-scatter.28
  1268.4 94.2 reduce-scatter.24
  1364.9 94.2 reduce-scatter.22
  1461.4 94.2 reduce-scatter.18
  1564.0 98.5 all-gather.39
  1664.7 96.4 all-gather.43
  1904.6 158.0 all-reduce.5
  2066.2 71.0 reduce-scatter.40
  2140.9 34.5 reduce-scatter.34
  2178.7 38.6 reduce-scatter.32
  2221.3 46.8 reduce-scatter.36
  2271.6 117.4 reduce-scatter.38
  2392.5 40.2 reduce-scatter.42
  2435.2 93.7 reduce-scatter.30
  2531.9 94.2 reduce-scatter.26
where the time goes:
time: 3010 us; the launch traced here: 3000 us
  waiting for transfers between devices  1640 us (54%)
  matrix products  623 us (21%)
  other arithmetic  503 us (17%)
  local copies, waits for them, and re-layouts  128 us (4%)
  blocking collectives  82.9 us (3%)
    all_gather x2, waiting for transfers between devices, on_device(): lax.all_gather(normed.astype(jnp.bfloat16), 'mp', axis=0, tiled=True)  191 us
    reduce_scatter x2, waiting for transfers between devices, on_device(): lax.psum_scatter(dot_last(activated, down_w).astype(jnp.bfloat16), 'mp',...  188 us
    reduce_scatter x2, waiting for transfers between devices, on_device(): lax.psum_scatter(dot_last(grad_columns, lat_w).astype(jnp.bfloat16), 'mp'...  157 us
    all_gather x2, waiting for transfers between devices, on_device(): lax.all_gather(normed_two.astype(jnp.bfloat16), 'mp', axis=0, tiled=True)  156 us
    all_gather x2, waiting for transfers between devices, on_device(): lax.all_gather((RESIDUAL * grad_out).astype(jnp.bfloat16), 'mp', axis=0,...  146 us
    another operation x16, other arithmetic, renew(): factor = jnp.linalg.cholesky(inner)  137 us
    reduce_scatter x2, waiting for transfers between devices, on_device(): lax.psum_scatter(dot_last(attended, output_w).astype(jnp.bfloat16), 'mp',...  122 us
    another operation x10, other arithmetic, renew(): jax.scipy.linalg.solve_triangular(factor, jnp.swapaxes(product, 1, 2), lo...  116 us
  transfers between devices with their start and end apart: 30, of which 26 were waited for; matrix products, arithmetic and copies ran while one was open for 26% of the time, Pallas kernels for 0%

commit v1 on v0

v1 whole, which is shorter than its diff:
```python
import functools
import math

import jax
import jax.numpy as jnp
from jax import lax
from jax.experimental import pallas as pl
from jax.experimental.pallas import tpu as pltpu
from jax.sharding import PartitionSpec as P

WIDTH = 2560
HEADS = 40
QUERY_RANK = 768
LATENT_RANK = 256
NOPE_DIM = 64
ROPE_DIM = 32
VALUE_DIM = 64
BLOCK = 128
ROTATE_ROWS = 16
STEP_COUNT = 10


HIGHEST = lax.Precision.HIGHEST
NORM_EPS = 1e-05
RESIDUAL = 1.4 / math.sqrt(62.0)
ROPE_BASE = 10000.0
BETA_FIRST = 0.95
BETA_SECOND = 0.95
ADAM_EPS = 1e-08
DECAY = 0.01
RATES = (0.08, 0.2, 0.25, 3.2, 0.08, 0.56)
GAIN_RATE = 0.8


def rms_parts(values, scale_gain):
    inverse = lax.rsqrt(jnp.mean(values * values, axis=-1, keepdims=True) + NORM_EPS)
    return (values * inverse * scale_gain, inverse)


def rms_back(values, inverse, scale_gain, upstream):
    weighted = upstream * scale_gain
    inner = jnp.mean(weighted * values, axis=-1, keepdims=True)
    return inverse * weighted - values * (inverse * inverse * inverse) * inner


def rotate(values, cosine, sine_part):
    half_dim = values.shape[-1] // 2
    first_half = values[..., :half_dim]
    second_half = values[..., half_dim:]
    return jnp.concatenate(
        [
            first_half * cosine - second_half * sine_part,
            second_half * cosine + first_half * sine_part,
        ],
        axis=-1,
    )


def rotate_back(grad_in, cosine, sine_part):
    half_dim = grad_in.shape[-1] // 2
    first_half = grad_in[..., :half_dim]
    second_half = grad_in[..., half_dim:]
    return jnp.concatenate(
        [
            first_half * cosine + second_half * sine_part,
            second_half * cosine - first_half * sine_part,
        ],
        axis=-1,
    )


def tree_layout(parent):
    block_count = parent.shape[0]
    identity = jnp.eye(block_count, dtype=jnp.float32)
    blocks = jnp.arange(block_count)
    parent_of = ((parent[:, None] == blocks[None, :]) & (blocks[:, None] > 0)).astype(jnp.float32)
    reached = identity
    for unused in range(block_count):
        reached = jnp.minimum(1.0, identity + jnp.dot(parent_of, reached, precision=HIGHEST))
    depths = jnp.sum(reached, axis=1) - 1.0
    length = block_count * BLOCK
    ancestor = (
        jnp.broadcast_to(
            reached[:, None, :, None], (block_count, BLOCK, block_count, BLOCK)
        ).reshape(length, length)
        > 0.5
    )
    tokens_at = jnp.arange(length)
    same_block = tokens_at[:, None] // BLOCK == tokens_at[None, :] // BLOCK
    visible = ancestor & (jnp.logical_not(same_block) | (tokens_at[None, :] <= tokens_at[:, None]))
    position = jnp.repeat(depths, BLOCK) * BLOCK + (tokens_at % BLOCK).astype(jnp.float32)
    frequency = ROPE_BASE ** (-(jnp.arange(ROPE_DIM // 2).astype(jnp.float32) * 2.0 / ROPE_DIM))
    angles = position[:, None] * frequency[None, :]
    return (visible, jnp.cos(angles), jnp.sin(angles))


def dot_first(first_arg, second_arg):
    return lax.dot_general(
        first_arg, second_arg, (((0,), (0,)), ((), ())), preferred_element_type=jnp.float32
    )


def dot_last(first_arg, second_arg):
    return lax.dot_general(
        first_arg, second_arg, (((1,), (1,)), ((), ())), preferred_element_type=jnp.float32
    )


def gram_of(grad_w):
    blocks = grad_w.reshape(grad_w.shape[0] // ROTATE_ROWS, ROTATE_ROWS, -1)
    return jnp.einsum("bic,bjc->bij", blocks, blocks, precision=HIGHEST)


def rotated_update(weight, grad_w, first_m, second_m, basis_m, step_rate):
    blocks = grad_w.reshape(basis_m.shape[0], basis_m.shape[1], -1)
    turned = jnp.einsum("bij,bic->bjc", basis_m, blocks, precision=HIGHEST).reshape(grad_w.shape)
    new_first = BETA_FIRST * first_m + (1.0 - BETA_FIRST) * turned
    new_second = BETA_SECOND * second_m + (1.0 - BETA_SECOND) * turned * turned
    normal_step = (
        new_first
        / (1.0 - BETA_FIRST**STEP_COUNT)
        / (jnp.sqrt(new_second / (1.0 - BETA_SECOND**STEP_COUNT)) + ADAM_EPS)
    )
    rotated_back = jnp.einsum(
        "bij,bjc->bic", basis_m, normal_step.reshape(blocks.shape), precision=HIGHEST
    ).reshape(grad_w.shape)
    new_weight = weight - step_rate * (rotated_back + DECAY * weight)
    return (new_weight, new_first, new_second)


def clip_columns(new_weight, clip_factor, head_width, rope_scaled):
    rows = new_weight.shape[0]
    root_factor = jnp.sqrt(clip_factor)
    tail_factor = clip_factor if rope_scaled else jnp.ones_like(clip_factor)
    column_scale = jnp.concatenate(
        [
            jnp.broadcast_to(root_factor[:, None], (clip_factor.shape[0], NOPE_DIM)),
            jnp.broadcast_to(tail_factor[:, None], (clip_factor.shape[0], head_width - NOPE_DIM)),
        ],
        axis=1,
    )
    return (
        new_weight.reshape(rows, clip_factor.shape[0], head_width) * column_scale[None]
    ).reshape(new_weight.shape)


def groups_of(data_count, group_size):
    near = [[start + i for i in range(group_size)] for start in range(0, data_count, group_size)]
    cross = [[i + start for start in range(0, data_count, group_size)] for i in range(group_size)]
    return near, cross


def to_trees(values, group_size, near):
    micro, count, width = values.shape
    parts = values.reshape(micro, group_size, count // group_size, width)
    parts = lax.all_to_all(parts, "dp", 1, 0, axis_index_groups=near)
    parts = parts.reshape(group_size * micro, count // group_size, width)
    return lax.all_to_all(parts, "mp", 0, 0, tiled=True)


def to_owners(values, group_size, near):
    planes, count, width = values.shape
    parts = lax.all_to_all(values, "mp", 0, 0, tiled=True)
    parts = parts.reshape(group_size, planes // group_size, count, width)
    parts = lax.all_to_all(parts, "dp", 0, 1, axis_index_groups=near)
    return parts.reshape(planes // group_size, group_size * count, width)


def spread(values, axis_name, count, groups=None):
    return lax.all_to_all(
        jnp.broadcast_to(values[None], (count,) + values.shape),
        axis_name,
        0,
        0,
        tiled=True,
        axis_index_groups=groups,
    )


def swap_bit(values, bit, data_count):
    return lax.ppermute(values, "dp", [(i, i ^ bit) for i in range(data_count)])


def bits_of(group_size, data_count):
    bits = []
    bit = group_size
    while bit < data_count:
        bits.append(bit)
        bit *= 2
    return bits


def gather_tokens(values, group_size, data_count):
    rows = values.shape[0] // 2
    bits = bits_of(group_size, data_count)
    pieces = {}
    for half in range(2):
        got = {0: values[half * rows : (half + 1) * rows]}
        for bit in bits if half == 0 else bits[::-1]:
            for index in sorted(got):
                got[index ^ bit] = swap_bit(got[index], bit, data_count)
        for index in sorted(got):
            pieces[(index, half)] = got[index]
            for near in range(1, group_size):
                pieces[(index ^ near, half)] = swap_bit(got[index], near, data_count)
    return pieces


def add_low(first_arg, second_arg):
    return (first_arg.astype(jnp.float32) + second_arg.astype(jnp.float32)).astype(jnp.bfloat16)


def scatter_tokens(pieces, group_size, data_count):
    bits = bits_of(group_size, data_count)
    halves = []
    for half in range(2):
        held = {}
        for index in range(0, data_count, group_size):
            total = pieces[(index, half)]
            for near in range(1, group_size):
                total = add_low(total, swap_bit(pieces[(index ^ near, half)], near, data_count))
            held[index] = total
        for bit in bits if half == 0 else bits[::-1]:
            for index in sorted(held):
                if not index & bit:
                    held[index] = add_low(held[index], swap_bit(held[index ^ bit], bit, data_count))
            held = {index: held[index] for index in held if not index & bit}
        halves.append(held[0])
    return jnp.concatenate(halves, axis=0)


def gather_far(block, group_size, data_count, data_index):
    far_count = data_count // group_size
    rows = block.shape[0] // 2
    own = data_index // group_size
    bits = bits_of(group_size, data_count)
    out = jnp.zeros((far_count,) + block.shape, block.dtype)
    for half in range(2):
        got = {0: block[half * rows : (half + 1) * rows]}
        for bit in bits if half == 0 else bits[::-1]:
            for index in sorted(got):
                got[index ^ bit] = swap_bit(got[index], bit, data_count)
        for index in sorted(got):
            out = lax.dynamic_update_slice(
                out, got[index][None], (own ^ (index // group_size), half * rows, 0)
            )
    return out


def gather_rows(block, group_size, data_count, data_index):
    far = gather_far(block, group_size, data_count, data_index)
    own = data_index % group_size
    out = jnp.zeros((far.shape[0], group_size) + block.shape, block.dtype)
    for near in range(group_size):
        part = far if near == 0 else swap_bit(far, near, data_count)
        out = lax.dynamic_update_slice(out, part[:, None], (0, own ^ near, 0, 0))
    return out.reshape((data_count * block.shape[0],) + block.shape[1:])


def after(values, *others):
    return lax.optimization_barrier((values,) + others)[0]


def scatter_rows(grad_w, group_size, data_count, near, cross):
    far_count = data_count // group_size
    rows = grad_w.shape[0] // data_count
    parts = grad_w.astype(jnp.bfloat16).reshape(far_count, group_size, rows, -1)
    parts = lax.all_to_all(parts, "dp", 1, 0, axis_index_groups=near)
    parts = jnp.sum(parts.astype(jnp.float32), axis=0).astype(jnp.bfloat16)
    parts = lax.all_to_all(parts, "dp", 0, 0, tiled=True, axis_index_groups=cross)
    return jnp.sum(parts.astype(jnp.float32), axis=0)


def scatter_columns(grad_w, model_count):
    rows, width = grad_w.shape
    parts = grad_w.astype(jnp.bfloat16).reshape(rows, model_count, width // model_count)
    parts = lax.all_to_all(jnp.swapaxes(parts, 0, 1), "mp", 0, 0, tiled=True)
    return jnp.sum(parts.astype(jnp.float32), axis=0)


def basis_kernel(stat_ref, basis_ref, out_ref):
    size = stat_ref.shape[0]
    columns = jnp.zeros(stat_ref.shape, jnp.float32)
    for j in range(size):
        columns = columns + basis_ref[j][:, None, :] * stat_ref[j][None, :, :]
    for j in range(size):
        column = columns[j]
        norm = jnp.sum(column * column, axis=0, keepdims=True)
        column = column * lax.rsqrt(norm)
        out_ref[j] = column
        shares = jnp.sum(columns * column[None], axis=1, keepdims=True)
        columns = columns - shares * column[None]


def renew_all(stats, bases):
    counts = [stat_m.shape[0] for stat_m in stats]
    total = sum(counts)
    padded = -(-total // 128) * 128
    stat_t = jnp.concatenate([jnp.transpose(s, (2, 1, 0)) for s in stats], axis=2)
    basis_t = jnp.concatenate([jnp.transpose(b, (1, 2, 0)) for b in bases], axis=2)
    pad = ((0, 0), (0, 0), (0, padded - total))
    stat_t = jnp.pad(stat_t, pad, constant_values=1.0)
    basis_t = jnp.pad(basis_t, pad, constant_values=1.0)
    out = pl.pallas_call(
        basis_kernel,
        out_shape=jax.ShapeDtypeStruct((ROTATE_ROWS, ROTATE_ROWS, padded), jnp.float32),
    )(stat_t, basis_t)
    results = []
    start = 0
    for count in counts:
        results.append(jnp.transpose(out[:, :, start : start + count], (2, 1, 0)))
        start += count
    return results


LOG2E = 1.4426950408889634


def exp_rows(query, keys, bias, scale):
    scores = lax.dot_general(
        query, keys, (((1,), (1,)), ((), ())), preferred_element_type=jnp.float32
    )
    scores = scores * (scale * LOG2E) + bias
    top = jnp.max(scores, axis=-1, keepdims=True)
    raised = jnp.exp2(scores - top)
    return raised, top, 1.0 / jnp.sum(raised, axis=-1, keepdims=True)


def attend_kernel(
    scale,
    rows,
    query_latent_ref,
    keyval_latent_ref,
    query_w_ref,
    keyval_w_ref,
    key_ref,
    bias_ref,
    cos_ref,
    left_ref,
    right_ref,
    out_ref,
    query_ref,
    keyval_ref,
    peak_ref,
):
    bf16 = jnp.bfloat16
    length = key_ref.shape[0]
    raw = jnp.dot(query_latent_ref[...], query_w_ref[...], preferred_element_type=jnp.float32)
    both = jnp.dot(keyval_latent_ref[...], keyval_w_ref[...], preferred_element_type=jnp.float32)
    keyval_ref[...] = both.astype(bf16)
    lane = lax.broadcasted_iota(jnp.int32, (1, 128), 1)
    for head in range(2):
        at = slice(head * 128, head * 128 + 128)
        part = raw[:, at]
        query_ref[:, at] = (
            part * cos_ref[...]
            + pltpu.roll(part, 128 - ROPE_DIM // 2, 1) * left_ref[...]
            + pltpu.roll(part, ROPE_DIM // 2, 1) * right_ref[...]
        ).astype(bf16)
    for first in range(0, length, rows):
        last = first + rows
        outs = []
        for head in range(2):
            at = slice(head * 128, head * 128 + 128)
            keyval = keyval_ref[:last, at]
            keys = jnp.where(lane < NOPE_DIM, keyval, key_ref[:last, :])
            raised, top, inverse = exp_rows(
                query_ref[first:last, at], keys, bias_ref[first:last, :last], scale
            )
            outs.append(
                jnp.dot(raised.astype(bf16), keyval, preferred_element_type=jnp.float32) * inverse
            )
            tops = jnp.max(top) * (1.0 / LOG2E)
            spot = slice(head * 8, head * 8 + 8)
            if first == 0:
                peak_ref[0, spot, :] = jnp.full((8, 128), tops, jnp.float32)
            else:
                peak_ref[0, spot, :] = jnp.maximum(peak_ref[0, spot, :], tops)
        out_ref[first:last, :] = jnp.where(
            lane < VALUE_DIM, pltpu.roll(outs[0], VALUE_DIM, 1), outs[1]
        ).astype(bf16)


def attend_back_kernel(
    scale,
    rows,
    query_ref,
    keyval_ref,
    grad_ref,
    key_ref,
    bias_ref,
    cos_ref,
    left_ref,
    right_ref,
    query_out_ref,
    keyval_out_ref,
    shared_out_ref,
    pair_ref,
    total_ref,
):
    bf16 = jnp.bfloat16
    length = key_ref.shape[0]
    lane = lax.broadcasted_iota(jnp.int32, (1, 128), 1)
    low_lanes = lane < NOPE_DIM

    @pl.when(pl.program_id(0) == 0)
    def clear():
        total_ref[...] = jnp.zeros_like(total_ref)

    for head in range(2):
        at = slice(head * 128, head * 128 + 128)
        pair_ref[...] = jnp.zeros_like(pair_ref)
        for first in range(0, length, rows):
            last = first + rows
            keyval = keyval_ref[:last, at]
            keys = jnp.where(low_lanes, keyval, key_ref[:last, :])
            query = query_ref[first:last, at]
            grad = grad_ref[first:last, :].astype(jnp.float32)
            if head == 0:
                grad = pltpu.roll(grad, VALUE_DIM, 1)
            grad = jnp.where(low_lanes, 0.0, grad).astype(bf16)
            raised, _, inverse = exp_rows(query, keys, bias_ref[first:last, :last], scale)
            probs = raised * inverse
            grad_probs = lax.dot_general(
                grad, keyval, (((1,), (1,)), ((), ())), preferred_element_type=jnp.float32
            )
            inner = jnp.sum(probs * grad_probs, axis=-1, keepdims=True)
            grad_scores = (probs * (grad_probs - inner)).astype(bf16)
            part = jnp.dot(grad_scores, keys, preferred_element_type=jnp.float32) * scale
            query_out_ref[first:last, at] = (
                part * cos_ref[first:last, :]
                - pltpu.roll(part, 128 - ROPE_DIM // 2, 1) * left_ref[first:last, :]
                - pltpu.roll(part, ROPE_DIM // 2, 1) * right_ref[first:last, :]
            ).astype(bf16)
            zero = jnp.zeros_like(query)
            left = jnp.concatenate([grad_scores, probs.astype(bf16)], axis=0)
            right = jnp.concatenate(
                [
                    jnp.concatenate(
                        [jnp.where(low_lanes, query, zero), jnp.where(low_lanes, zero, query)],
                        axis=1,
                    ),
                    jnp.concatenate([grad, zero], axis=1),
                ],
                axis=0,
            )
            both = lax.dot_general(
                left, right, (((0,), (0,)), ((), ())), preferred_element_type=jnp.float32
            )
            pair_ref[:last, :] += both[:, :128]
            total_ref[:last, :] += both[:, 128:]
        keyval_out_ref[:, at] = (pair_ref[...] * jnp.where(low_lanes, scale, 1.0)).astype(bf16)

    @pl.when(pl.program_id(0) == pl.num_programs(0) - 1)
    def finish():
        shared_out_ref[...] = total_ref[...] * scale


def resident(shape):
    return pl.BlockSpec(shape, lambda step: (0,) * len(shape))


def attend(query_latent, keyval_latent, query_w, keyval_w, key_lanes, bias, tables, scale, rows):
    length = bias.shape[0]
    steps = query_w.shape[1] // 256
    wide = jax.ShapeDtypeStruct((length, steps * 256), jnp.bfloat16)
    column = lambda width: pl.BlockSpec((length, width), lambda step: (0, step))
    return pl.pallas_call(
        functools.partial(attend_kernel, scale, rows),
        grid=(steps,),
        in_specs=[
            resident(query_latent.shape),
            resident(keyval_latent.shape),
            pl.BlockSpec((query_w.shape[0], 256), lambda step: (0, step)),
            pl.BlockSpec((keyval_w.shape[0], 256), lambda step: (0, step)),
            resident(key_lanes.shape),
            resident(bias.shape),
        ]
        + [resident(table.shape) for table in tables],
        out_specs=[
            column(128),
            column(256),
            column(256),
            pl.BlockSpec((1, 16, 128), lambda step: (step, 0, 0)),
        ],
        out_shape=[
            jax.ShapeDtypeStruct((length, steps * 128), jnp.bfloat16),
            wide,
            wide,
            jax.ShapeDtypeStruct((steps, 16, 128), jnp.float32),
        ],
        compiler_params=pltpu.CompilerParams(vmem_limit_bytes=56 * 1024 * 1024),
    )(query_latent, keyval_latent, query_w, keyval_w, key_lanes, bias, *tables)


def attend_back(queries, keyval, grad, key_lanes, bias, tables, scale, rows):
    length = bias.shape[0]
    steps = queries.shape[1] // 256
    wide = jax.ShapeDtypeStruct(queries.shape, jnp.bfloat16)
    column = lambda width: pl.BlockSpec((length, width), lambda step: (0, step))
    return pl.pallas_call(
        functools.partial(attend_back_kernel, scale, rows),
        grid=(steps,),
        in_specs=[
            column(256),
            column(256),
            column(128),
            resident(key_lanes.shape),
            resident(bias.shape),
        ]
        + [resident(table.shape) for table in tables],
        out_specs=[column(256), column(256), resident((length, 128))],
        out_shape=[wide, wide, jax.ShapeDtypeStruct((length, 128), jnp.float32)],
        scratch_shapes=[
            pltpu.VMEM((length, 128), jnp.float32),
            pltpu.VMEM((length, 128), jnp.float32),
        ],
        compiler_params=pltpu.CompilerParams(vmem_limit_bytes=56 * 1024 * 1024),
    )(queries, keyval, grad, key_lanes, bias, *tables)


def on_device(
    tokens,
    cotangent,
    parents,
    latent_weight,
    latent_first,
    latent_second,
    latent_stat,
    latent_basis,
    query_weight,
    query_first,
    query_second,
    query_stat,
    query_basis,
    keyval_weight,
    keyval_first,
    keyval_second,
    keyval_stat,
    keyval_basis,
    project_weight,
    project_first,
    project_second,
    project_stat,
    project_basis,
    gateup_weight,
    gateup_first,
    gateup_second,
    gateup_stat,
    gateup_basis,
    down_weight,
    down_first,
    down_second,
    down_stat,
    down_basis,
    gains,
    gains_first,
    gains_second,
):
    matrices = (
        latent_weight,
        query_weight,
        keyval_weight,
        project_weight,
        gateup_weight,
        down_weight,
    )
    states = (
        (latent_first, latent_second, latent_stat, latent_basis),
        (query_first, query_second, query_stat, query_basis),
        (keyval_first, keyval_second, keyval_stat, keyval_basis),
        (project_first, project_second, project_stat, project_basis),
        (gateup_first, gateup_second, gateup_stat, gateup_basis),
        (down_first, down_second, down_stat, down_basis),
    )
    bf16 = jnp.bfloat16
    data_count = lax.axis_size("dp")
    model_count = lax.axis_size("mp")
    micro, share, _ = tokens.shape
    group = model_count // micro
    near, cross = groups_of(data_count, group)
    data_index = lax.axis_index("dp")
    model_index = lax.axis_index("mp")
    own_part = data_index % group
    length = share * model_count
    heads = HEADS // group
    scale_attn = float(NOPE_DIM + ROPE_DIM) ** (-0.5)
    rows_attn = min(512, length)
    own_heads = query_weight.shape[1] // (NOPE_DIM + ROPE_DIM)
    latent_all = latent_weight.shape[1] * model_count

    gain_all = spread(gains.astype(bf16), "dp", data_count).reshape(-1).astype(jnp.float32)
    gain_one = gain_all[:WIDTH]
    gain_two = gain_all[WIDTH : 2 * WIDTH]
    gain_query = gain_all[2 * WIDTH : 2 * WIDTH + QUERY_RANK]
    gain_keyval = gain_all[2 * WIDTH + QUERY_RANK :]

    def columns(weight):
        return lax.all_gather(weight.astype(bf16), "mp", axis=1, tiled=True)

    def head_part(weight, width):
        rows = columns(weight)
        parts = rows.reshape(rows.shape[0], group, -1)
        parts = lax.all_to_all(parts, "dp", 1, 0, axis_index_groups=near)
        parts = parts.reshape(group * rows.shape[0], -1)
        full = gather_far(parts, group, data_count, data_index)
        full = full.reshape(data_count * rows.shape[0], heads, width)
        return jnp.pad(full, ((0, 0), (0, 0), (0, 128 - width))).reshape(full.shape[0], -1)

    lat_w = gather_rows(columns(latent_weight), group, data_count, data_index)
    query_w = head_part(query_weight, NOPE_DIM + ROPE_DIM)
    keyval_w = head_part(keyval_weight, NOPE_DIM + VALUE_DIM)
    output_w = gather_rows(columns(project_weight), group, data_count, data_index)

    unit_count = down_weight.shape[1] // data_count
    hidden_units = unit_count * model_count
    padded = -(-hidden_units // 128) * 128
    gate_t = gateup_weight.astype(bf16).reshape(-1, 2, data_count, unit_count)
    gate_t = lax.all_to_all(jnp.transpose(gate_t, (2, 1, 3, 0)), "dp", 0, 0, tiled=True)
    gate_t = jnp.transpose(gate_t, (1, 2, 0, 3)).reshape(2 * unit_count, WIDTH)
    gate_t = lax.all_gather(gate_t, "mp", axis=0)
    gate_t = jnp.transpose(gate_t.reshape(model_count, 2, unit_count, WIDTH), (1, 0, 2, 3))
    gate_t = gate_t.reshape(2, hidden_units, WIDTH)
    gate_t = jnp.pad(gate_t, ((0, 0), (0, padded - hidden_units), (0, 0))).reshape(-1, WIDTH)
    down_t = down_weight.astype(bf16).reshape(-1, data_count, unit_count)
    down_t = lax.all_to_all(jnp.transpose(down_t, (1, 2, 0)), "dp", 0, 0, tiled=True)
    down_t = jnp.transpose(down_t, (1, 0, 2)).reshape(unit_count, WIDTH)
    down_t = lax.all_gather(down_t, "mp", axis=0).reshape(hidden_units, WIDTH)
    down_t = jnp.pad(down_t, ((0, padded - hidden_units), (0, 0)))

    tok = tokens.reshape(micro * share, WIDTH).astype(jnp.float32)
    normed, inverse_one = rms_parts(tok, gain_one)
    normed = normed.astype(bf16)
    latent = jnp.dot(normed, lat_w, preferred_element_type=jnp.float32).astype(bf16)
    latent = latent.astype(jnp.float32)
    query_raw = latent[:, :QUERY_RANK]
    keyval_raw = latent[:, QUERY_RANK : QUERY_RANK + LATENT_RANK]
    key_rope = latent[:, QUERY_RANK + LATENT_RANK :]
    query_normed, inverse_query = rms_parts(query_raw, gain_query)
    keyval_normed, inverse_keyval = rms_parts(keyval_raw, gain_keyval)
    sent = jnp.concatenate([query_normed, keyval_normed, key_rope], axis=1).astype(bf16)

    mid = to_trees(sent.reshape(micro, share, latent_all), group, near)
    tree = spread(mid, "dp", group, near)
    tree = jnp.swapaxes(tree, 0, 1).reshape(length, latent_all)
    tree_parents = spread(parents[:, 0], "dp", group, near).reshape(group * micro, -1)
    visible, cosine, sine_part = tree_layout(
        lax.dynamic_index_in_dim(tree_parents, model_index, 0, keepdims=False)
    )
    query_latent = tree[:, :QUERY_RANK]
    keyval_latent = tree[:, QUERY_RANK : QUERY_RANK + LATENT_RANK]
    shared = rotate(
        tree[:, QUERY_RANK + LATENT_RANK :].astype(jnp.float32), cosine, sine_part
    )
    key_lanes = jnp.pad(shared, ((0, 0), (NOPE_DIM, 128 - NOPE_DIM - ROPE_DIM))).astype(bf16)
    bias = jnp.where(visible, 0.0, -1e30).astype(jnp.float32)
    half_rope = ROPE_DIM // 2
    tail_lanes = 128 - NOPE_DIM - ROPE_DIM
    tables = (
        jnp.concatenate(
            [jnp.ones((length, NOPE_DIM)), cosine, cosine, jnp.zeros((length, tail_lanes))], axis=1
        ).astype(jnp.float32),
        jnp.pad(-sine_part, ((0, 0), (NOPE_DIM, half_rope + tail_lanes))),
        jnp.pad(sine_part, ((0, 0), (NOPE_DIM + half_rope, tail_lanes))),
    )
    attended, queries, keyval, peaks = attend(
        query_latent, keyval_latent, query_w, keyval_w, key_lanes, bias, tables, scale_attn, rows_attn
    )
    peak_own = peaks.reshape(heads, 8, 128)[:, 0, 0]

    def heads_out(values):
        parts = values.reshape(model_count, group, share // group, -1)
        parts = lax.all_to_all(parts, "dp", 1, 2, axis_index_groups=near)
        return to_owners(
            parts.reshape(model_count, share // group, -1), group, near
        ).reshape(micro * share, -1)

    def heads_in(values):
        parts = to_trees(values.reshape(micro, share, -1), group, near)
        parts = parts.reshape(model_count, share // group, group, -1)
        parts = lax.all_to_all(parts, "dp", 2, 1, axis_index_groups=near)
        return parts.reshape(length, -1)

    attended_own = heads_out(attended)
    branch = dot_last(attended_own, output_w)
    hidden = tok + RESIDUAL * branch
    normed_two, inverse_two = rms_parts(hidden, gain_two)
    normed_two = normed_two.astype(bf16)

    far_count = data_count // group
    half_rows = micro * share // 2
    order = [
        [(far * group + place, half) for place in range(group) for half in range(2)]
        for far in range(far_count)
    ]

    def joined(values):
        pieces = gather_tokens(values, group, data_count)
        return [jnp.concatenate([pieces[key] for key in keys], axis=0) for keys in order]

    def parted(blocks):
        pieces = {}
        for keys, block in zip(order, blocks):
            for at, key in enumerate(keys):
                pieces[key] = block[at * half_rows : (at + 1) * half_rows]
        return scatter_tokens(pieces, group, data_count).astype(jnp.float32)

    grad_out = cotangent.reshape(micro * share, WIDTH).astype(jnp.float32)
    mixed_blocks = joined(after((RESIDUAL * grad_out).astype(bf16), tree))
    normed_blocks = joined(normed_two)
    active_blocks = []
    grad_gateup_blocks = []
    for mixed_block, normed_block in zip(mixed_blocks, normed_blocks):
        gateup = dot_last(normed_block, gate_t)
        gate_part = gateup[:, :padded]
        up_part = gateup[:, padded:]
        sigmoid_gate = jax.nn.sigmoid(gate_part)
        silu_gate = gate_part * sigmoid_gate
        active_blocks.append((silu_gate * up_part).astype(bf16))
        grad_act = dot_last(mixed_block, down_t)
        grad_gate = grad_act * up_part * sigmoid_gate * (1.0 + gate_part * (1.0 - sigmoid_gate))
        grad_up = grad_act * silu_gate
        grad_gateup_blocks.append(jnp.concatenate([grad_gate, grad_up], axis=1).astype(bf16))
    grad_normed_blocks = [
        jnp.dot(block, gate_t, preferred_element_type=jnp.float32).astype(bf16)
        for block in grad_gateup_blocks
    ]
    grad_normed_two = parted(grad_normed_blocks)
    activated = jnp.concatenate(active_blocks, axis=0)
    grad_down_t = dot_first(activated, jnp.concatenate(mixed_blocks, axis=0)).astype(bf16)
    grad_gate_t = dot_first(
        jnp.concatenate(grad_gateup_blocks, axis=0), jnp.concatenate(normed_blocks, axis=0)
    ).astype(bf16)
    active_late = [after(block, grad_normed_two) for block in active_blocks]
    mixed_out = parted(
        [
            jnp.dot(block, down_t, preferred_element_type=jnp.float32).astype(bf16)
            for block in active_late
        ]
    )
    layer_out = (hidden + RESIDUAL * mixed_out).astype(bf16)
    grad_down_t = grad_down_t[:hidden_units]

    down_sum = lax.psum_scatter(
        grad_down_t.reshape(model_count, unit_count, WIDTH), "mp", scatter_dimension=0, tiled=True
    )
    down_sum = jnp.transpose(down_sum.reshape(unit_count, data_count, -1), (1, 0, 2))
    down_sum = lax.all_to_all(down_sum, "dp", 0, 0, tiled=True)
    down_sum = jnp.transpose(down_sum, (2, 0, 1)).reshape(down_weight.shape)
    gate_sum = grad_gate_t.reshape(2, padded, WIDTH)[:, :hidden_units]
    gate_sum = jnp.transpose(
        gate_sum.reshape(2, model_count, unit_count, WIDTH), (1, 0, 2, 3)
    ).reshape(model_count, 2 * unit_count, WIDTH)
    gate_sum = lax.psum_scatter(gate_sum, "mp", scatter_dimension=0, tiled=True)
    gate_sum = jnp.transpose(gate_sum.reshape(2 * unit_count, data_count, -1), (1, 0, 2))
    gate_sum = lax.all_to_all(gate_sum, "dp", 0, 0, tiled=True)
    gate_sum = jnp.transpose(
        gate_sum.reshape(data_count, 2, unit_count, -1), (3, 1, 0, 2)
    ).reshape(gateup_weight.shape)

    grad_hidden = grad_out + rms_back(hidden, inverse_two, gain_two, grad_normed_two)
    grad_gain_two = jnp.sum(grad_normed_two * hidden * inverse_two, axis=0)
    grad_branch = (RESIDUAL * grad_hidden).astype(bf16)
    grad_branch = after(grad_branch, grad_gate_t, grad_down_t)
    grad_attended = heads_in(
        jnp.dot(grad_branch, output_w, preferred_element_type=jnp.float32).astype(bf16)
    )
    grad_project = dot_first(grad_branch, attended_own)
    grad_query_all, grad_keyval, grad_shared = attend_back(
        queries, keyval, grad_attended, key_lanes, bias, tables, scale_attn, rows_attn
    )
    grad_shared = rotate_back(
        grad_shared[:, NOPE_DIM : NOPE_DIM + ROPE_DIM], cosine, sine_part
    )
    latent_terms = jnp.concatenate(
        [dot_last(grad_query_all, query_w), dot_last(grad_keyval, keyval_w), grad_shared], axis=1
    ).astype(bf16)
    parts = latent_terms.reshape(model_count, group, share // group, latent_all)
    parts = lax.all_to_all(parts, "dp", 1, 0, axis_index_groups=near)
    parts = jnp.sum(parts.astype(jnp.float32), axis=0).astype(bf16)
    grad_latent_all = (
        to_owners(parts, group, near).reshape(micro * share, latent_all).astype(jnp.float32)
    )
    grad_query_w = dot_first(query_latent, grad_query_all)
    grad_keyval_w = dot_first(keyval_latent, grad_keyval)

    grad_query_up = grad_latent_all[:, :QUERY_RANK]
    grad_keyval_up = grad_latent_all[:, QUERY_RANK : QUERY_RANK + LATENT_RANK]
    grad_latent = jnp.concatenate(
        [
            rms_back(query_raw, inverse_query, gain_query, grad_query_up),
            rms_back(keyval_raw, inverse_keyval, gain_keyval, grad_keyval_up),
            grad_latent_all[:, QUERY_RANK + LATENT_RANK :],
        ],
        axis=1,
    ).astype(bf16)
    grad_gain_query = jnp.sum(grad_query_up * query_raw * inverse_query, axis=0)
    grad_gain_keyval = jnp.sum(grad_keyval_up * keyval_raw * inverse_keyval, axis=0)
    grad_normed = dot_last(grad_latent, lat_w)
    grad_latent_w = dot_first(normed, grad_latent)
    input_grad = grad_hidden + rms_back(tok, inverse_one, gain_one, grad_normed)
    grad_gain_one = jnp.sum(grad_normed * tok * inverse_one, axis=0)
    grad_gains = jnp.concatenate(
        [grad_gain_one, grad_gain_two, grad_gain_query, grad_gain_keyval]
    )

    def head_grads(grad_w):
        rows = grad_w.shape[0] // data_count
        parts = grad_w.astype(bf16).reshape(data_count // group, group * rows, -1)
        parts = lax.all_to_all(parts, "dp", 0, 0, tiled=True, axis_index_groups=cross)
        parts = jnp.sum(parts.astype(jnp.float32), axis=0).astype(bf16)
        parts = lax.all_to_all(
            parts.reshape(group, rows, -1), "dp", 0, 1, axis_index_groups=near
        )
        return scatter_columns(parts.reshape(rows, -1), model_count)

    reduced = [
        scatter_columns(
            scatter_rows(grad_latent_w, group, data_count, near, cross), model_count
        ),
        head_grads(grad_query_w)
        .reshape(query_weight.shape[0], own_heads, 128)[:, :, : NOPE_DIM + ROPE_DIM]
        .reshape(query_weight.shape),
        head_grads(grad_keyval_w),
        scatter_columns(
            scatter_rows(grad_project, group, data_count, near, cross), model_count
        ),
        gate_sum.astype(jnp.float32),
        down_sum.astype(jnp.float32),
    ]
    gain_parts = lax.all_to_all(
        grad_gains.reshape(data_count, -1), "dp", 0, 0, tiled=True
    )
    gain_parts = jnp.sum(gain_parts, axis=0)
    gains_grad = jnp.sum(spread(gain_parts, "mp", model_count), axis=0)

    peak_all = jnp.max(spread(peak_own, "mp", model_count), axis=0)
    peak_all = jnp.max(spread(peak_all, "dp", data_count // group, cross), axis=0)
    all_peaks = spread(peak_all, "dp", group, near).reshape(HEADS)
    threshold = jnp.mean(all_peaks)
    clip_all = jnp.minimum(1.0, threshold / jnp.maximum(all_peaks, 1.0))
    clip_own = lax.dynamic_slice_in_dim(clip_all, model_index * own_heads, own_heads, 0)

    grams = jnp.concatenate([gram_of(grad_w) for grad_w in reduced], axis=0)
    grams = jnp.sum(spread(grams, "mp", model_count), axis=0)
    results = [
        layer_out.reshape(tokens.shape),
        input_grad.reshape(tokens.shape),
    ]
    new_stats = []
    start = 0
    for mat_index in range(6):
        stat_m = states[mat_index][2]
        gram_sum = grams[start : start + stat_m.shape[0]]
        start += stat_m.shape[0]
        new_stats.append(BETA_SECOND * stat_m + (1.0 - BETA_SECOND) * gram_sum)
    new_bases = renew_all(new_stats, [state[3] for state in states])
    for mat_index in range(6):
        first_m, second_m, stat_m, basis_m = states[mat_index]
        new_weight, new_first, new_second = rotated_update(
            matrices[mat_index],
            reduced[mat_index],
            first_m,
            second_m,
            basis_m,
            RATES[mat_index],
        )
        if mat_index == 1:
            new_weight = clip_columns(new_weight, clip_own, NOPE_DIM + ROPE_DIM, True)
        if mat_index == 2:
            new_weight = clip_columns(new_weight, clip_own, NOPE_DIM + VALUE_DIM, False)
        results.extend(
            [
                new_weight,
                new_weight.astype(jnp.bfloat16),
                new_first,
                new_second,
                new_stats[mat_index],
                new_bases[mat_index],
            ]
        )
    gains_first_new = BETA_FIRST * gains_first + (1.0 - BETA_FIRST) * gains_grad
    gains_second_new = BETA_SECOND * gains_second + (1.0 - BETA_SECOND) * gains_grad * gains_grad
    gains_step = (
        gains_first_new
        / (1.0 - BETA_FIRST**STEP_COUNT)
        / (jnp.sqrt(gains_second_new / (1.0 - BETA_SECOND**STEP_COUNT)) + ADAM_EPS)
    )
    results.extend(
        [gains - GAIN_RATE * (gains_step + DECAY * gains), gains_first_new, gains_second_new]
    )
    return tuple(results)


def solution(mesh):
    placed = (
        P(None, ("dp", "mp"), None),
        P(None, ("dp", "mp"), None),
        P(None, "dp", None),
        P("dp", "mp"),
        P("dp", "mp"),
        P("dp", "mp"),
        P("dp", None, None),
        P("dp", None, None),
        P("dp", "mp"),
        P("dp", "mp"),
        P("dp", "mp"),
        P("dp", None, None),
        P("dp", None, None),
        P("dp", "mp"),
        P("dp", "mp"),
        P("dp", "mp"),
        P("dp", None, None),
        P("dp", None, None),
        P("dp", "mp"),
        P("dp", "mp"),
        P("dp", "mp"),
        P("dp", None, None),
        P("dp", None, None),
        P("dp", None, "mp"),
        P("dp", None, "mp"),
        P("dp", None, "mp"),
        P("dp", None, None),
        P("dp", None, None),
        P("dp", "mp"),
        P("dp", "mp"),
        P("dp", "mp"),
        P("dp", None, None),
        P("dp", None, None),
        P("dp"),
        P("dp"),
        P("dp"),
    )
    return jax.shard_map(
        on_device,
        mesh=mesh,
        in_specs=placed,
        out_specs=(
            P(None, ("dp", "mp"), None),
            P(None, ("dp", "mp"), None),
            P("dp", "mp"),
            P("dp", "mp"),
            P("dp", "mp"),
            P("dp", "mp"),
            P("dp", None, None),
            P("dp", None, None),
            P("dp", "mp"),
            P("dp", "mp"),
            P("dp", "mp"),
            P("dp", "mp"),
            P("dp", None, None),
            P("dp", None, None),
            P("dp", "mp"),
            P("dp", "mp"),
            P("dp", "mp"),
            P("dp", "mp"),
            P("dp", None, None),
            P("dp", None, None),
            P("dp", "mp"),
            P("dp", "mp"),
            P("dp", "mp"),
            P("dp", "mp"),
            P("dp", None, None),
            P("dp", None, None),
            P("dp", None, "mp"),
            P("dp", None, "mp"),
            P("dp", None, "mp"),
            P("dp", None, "mp"),
            P("dp", None, None),
            P("dp", None, None),
            P("dp", "mp"),
            P("dp", "mp"),
            P("dp", "mp"),
            P("dp", "mp"),
            P("dp", None, None),
            P("dp", None, None),
            P("dp"),
            P("dp"),
            P("dp"),
        ),
        check_vma=False,
    )
```

time: 3010 us -> 3630 us (1.21)
  local copies, waits for them, and re-layouts: 128 us -> 2010 us
  waiting for transfers between devices: 1640 us -> 584 us
  other arithmetic: 503 us -> 185 us
  matrix products: 623 us -> 394 us
  starting transfers between devices: 2.65 us -> 164 us
  Pallas kernels: 0 us -> 115 us
  blocking collectives: 82.9 us -> 153 us
    dynamic_update_slice x1 -> x36, local copies, waits for them, and re-layouts: 0.23 us -> 1620 us  [the longest x32 1600 us: gather_far(): lax.dynamic_update_slice(out, got[index][None], (own ^ index // group_siz...]
    all_gather x15 -> x3, waiting for transfers between devices: 803 us -> 0.02 us  [the longest x1 0.02 us: columns(): return lax.all_gather(weight.astype(bf16), 'mp', axis=1, tiled=True)]
    reduce_scatter x14 -> x2, waiting for transfers between devices: 793 us -> 0.01 us  [the longest x1 0.01 us: on_device(): lax.psum_scatter(grad_down_t.reshape(model_count, unit_count, WIDTH), 'mp...]
    ppermute x0 -> x82, waiting for transfers between devices: none -> 391 us  [swap_bit(): return lax.ppermute(values, 'dp', [(i, i ^ bit) for i in range(data_count)])]
    dot_general x40 -> x10, matrix products: 445 us -> 90.6 us  [the longest x4 49.7 us: on_device(): jnp.dot(block, gate_t, preferred_element_type=jnp.float32).astype(bf16)]
    another operation x38 -> x5, other arithmetic: 270 us -> 5.93 us  [the longest x16 137 us: renew(): factor = jnp.linalg.cholesky(inner)]
    all_to_all x0 -> x26, waiting for transfers between devices: none -> 194 us  [the longest x2 114 us: to_trees(): return lax.all_to_all(parts, 'mp', 0, 0, tiled=True)]
    pallas_call x0 -> x3, Pallas kernels: none -> 115 us  [the longest x1 70 us: attend_back(): pl.pallas_call(functools.partial(attend_back_kernel, scale, rows), grid=(...]
  transfers between devices with their start and end apart: 30 -> 113, of which waited for: 26 -> 33; matrix products, arithmetic and copies ran while one was open for 26% -> 70% of each run, Pallas kernels for 0% -> 3%
where the time goes in v1:
time: 3630 us; the launch traced here: 3620 us
  local copies, waits for them, and re-layouts  2010 us (55%)
  waiting for transfers between devices  584 us (16%)
  matrix products  394 us (11%)
  other arithmetic  185 us (5%)
  starting transfers between devices  164 us (5%)
  blocking collectives  153 us (4%)
  Pallas kernels  115 us (3%)
    dynamic_update_slice x32, local copies, waits for them, and re-layouts, gather_far(): lax.dynamic_update_slice(out, got[index][None], (own ^ index // group_siz...  1600 us
    ppermute x82, waiting for transfers between devices, swap_bit(): return lax.ppermute(values, 'dp', [(i, i ^ bit) for i in range(data_count)])  391 us
    dot_general x12, matrix products, dot_last(): lax.dot_general(first_arg, second_arg, (((1,), (1,)), ((), ())), preferre...  156 us
    dot_general x6, matrix products, dot_first(): lax.dot_general(first_arg, second_arg, (((0,), (0,)), ((), ())), preferre...  114 us
    all_to_all x2, waiting for transfers between devices, to_trees(): return lax.all_to_all(parts, 'mp', 0, 0, tiled=True)  114 us
    unnamed x373, local copies, waits for them, and re-layouts  95.9 us
  transfers between devices with their start and end apart: 113, of which 33 were waited for; matrix products, arithmetic and copies ran while one was open for 70% of the time, Pallas kernels for 3%

profile of v1, /device:TPU:0, one launch (start us, length us, event | category | flops | bytes accessed | tf_op | source)
XLA Modules:
  0.0 3619.4 jit_solution(1135996362634442901)
XLA Ops:
  8.3 21.7 all_gather.18
  73.0 18.1 all-gather
  161.3 67.6 %dynamic_update_slice.118 = bf16[4,192,1920]{1,0,2:T(4,128)(2,1)} dynamic-update-slice(bf16[4,192,1920]{1,0,2:T(4,128)(2,1)} %broadcast_in_dim.256, bf16[1,96,1920]{1,0,2:T(2,128)(2,1)} %copy.904, s32[]{:T(128)S(6)} %select_n.104, s32[]{:T(128)} %constant.107.clone.1, s32[]{:T(128)} %constant.107.clone.1) | dynamic-update-slice | bytes 737284 | tf_op jit(solution)/shard_map/dynamic_update_slice | solution.py:244
  239.7 26.6 collective-permute-done.14
  401.8 18.7 all-to-all-done.2
  456.1 67.6 %dynamic_update_slice.119 = bf16[4,192,1920]{1,0,2:T(4,128)(2,1)} dynamic-update-slice(bf16[4,192,1920]{1,0,2:T(4,128)(2,1)} %dynamic_update_slice.118, bf16[1,96,1920]{1,0,2:T(2,128)(2,1)} %copy.905, s32[]{:T(128)S(6)} %select_n.105, s32[]{:T(128)} %constant.107.clone.1, s32[]{:T(128)} %constant.107.clone.1) | dynamic-update-slice | bytes 737284 | tf_op jit(solution)/shard_map/dynamic_update_slice | solution.py:244
  523.8 67.6 %dynamic_update_slice.120 = bf16[4,192,1920]{1,0,2:T(4,128)(2,1)} dynamic-update-slice(bf16[4,192,1920]{1,0,2:T(4,128)(2,1)} %dynamic_update_slice.119, bf16[1,96,1920]{1,0,2:T(2,128)(2,1)} %copy.906, s32[]{:T(128)S(6)} %select_n.106, s32[]{:T(128)} %constant.107.clone.1, s32[]{:T(128)} %constant.107.clone.1) | dynamic-update-slice | bytes 737284 | tf_op jit(solution)/shard_map/dynamic_update_slice | solution.py:244
  596.4 67.6 %dynamic_update_slice.121 = bf16[4,192,1920]{1,0,2:T(4,128)(2,1)} dynamic-update-slice(bf16[4,192,1920]{1,0,2:T(4,128)(2,1)} %dynamic_update_slice.120, bf16[1,96,1920]{1,0,2:T(2,128)(2,1)} %copy.907, s32[]{:T(128)S(6)} %select_n.107, s32[]{:T(128)} %constant.107.clone.1, s32[]{:T(128)} %constant.107.clone.1) | dynamic-update-slice | bytes 737284 | tf_op jit(solution)/shard_map/dynamic_update_slice | solution.py:244
  664.1 325.9 %dynamic_update_slice.122 = bf16[4,192,1920]{1,0,2:T(4,128)(2,1)} dynamic-update-slice(bf16[4,192,1920]{1,0,2:T(4,128)(2,1)} %dynamic_update_slice.121, bf16[1,96,1920]{1,0,2:T(2,128)(2,1)} %copy.908, s32[]{:T(128)S(6)} %select_n.104, s32[]{:T(128)} %constant.211.clone.1, s32[]{:T(128)} %constant.107.clone.1) | dynamic-update-slice | bytes 737284 | tf_op jit(solution)/shard_map/dynamic_update_slice | solution.py:244
  990.0 325.9 %dynamic_update_slice.123 = bf16[4,192,1920]{1,0,2:T(4,128)(2,1)} dynamic-update-slice(bf16[4,192,1920]{1,0,2:T(4,128)(2,1)} %dynamic_update_slice.122, bf16[1,96,1920]{1,0,2:T(2,128)(2,1)} %copy.909, s32[]{:T(128)S(6)} %select_n.105, s32[]{:T(128)} %constant.211.clone.1, s32[]{:T(128)} %constant.107.clone.1) | dynamic-update-slice | bytes 737284 | tf_op jit(solution)/shard_map/dynamic_update_slice | solution.py:244
  1315.9 325.9 %dynamic_update_slice.124 = bf16[4,192,1920]{1,0,2:T(4,128)(2,1)} dynamic-update-slice(bf16[4,192,1920]{1,0,2:T(4,128)(2,1)} %dynamic_update_slice.123, bf16[1,96,1920]{1,0,2:T(2,128)(2,1)} %copy.910, s32[]{:T(128)S(6)} %select_n.106, s32[]{:T(128)} %constant.211.clone.1, s32[]{:T(128)} %constant.107.clone.1) | dynamic-update-slice | bytes 737284 | tf_op jit(solution)/shard_map/dynamic_update_slice | solution.py:244
  1641.9 325.9 %dynamic_update_slice.125 = bf16[4,192,1920]{1,0,2:T(4,128)(2,1)} dynamic-update-slice(bf16[4,192,1920]{1,0,2:T(4,128)(2,1)} %dynamic_update_slice.124, bf16[1,96,1920]{1,0,2:T(2,128)(2,1)} %copy.911, s32[]{:T(128)S(6)} %select_n.107, s32[]{:T(128)} %constant.211.clone.1, s32[]{:T(128)} %constant.107.clone.1) | dynamic-update-slice | bytes 737284 | tf_op jit(solution)/shard_map/dynamic_update_slice | solution.py:244
  2003.3 43.3 %shard_map.659 = (bf16[1024,1280]{1,0:T(8,128)(2,1)}, bf16[1024,2560]{1,0:T(8,128)(2,1)}, bf16[1024,2560]{1,0:T(8,128)(2,1)}, f32[10,16,128]{2,1,0:T(8,128)}) custom-call(bf16[1024,768]{1,0:T(8,128)(2,1)} %slice.373.query_latent_ref, bf16[1024,256]{1,0:T(8,128)(2,1)} %slice.374.keyval_latent_ref, bf16[768,2560]{1,0:T(8,128)(2,1)} %copy.918.query_w_ref, ...), custom_call_target="tpu_custom_call" | custom-call | tf_op jit(solution)/shard_map/pallas_call | solution.py:468
  2088.9 28.1 collective-permute-done.42
  2126.6 18.0 collective-permute-done.50
  2231.5 23.5 collective-permute-done.36
  2259.1 25.6 collective-permute-done.54
  2313.3 17.5 fusion.48
  2361.0 18.3 fusion.64
  2440.3 18.8 fusion.80
  2505.7 27.8 fusion.19
  2551.6 18.3 collective-permute-done.59
  2577.1 55.2 %fusion.16 = bf16[1792,2560]{1,0:T(8,128)(2,1)} fusion(bf16[4096,2560]{1,0:T(8,128)(2,1)} %constant_dynamic-update-slice_fusion, bf16[1024,896]{1,0:T(8,128)(2,1)} %get-tuple-element.488, bf16[1024,896]{1,0:T(8,128)(2,1)} %get-tuple-element.487, bf16[1024,896]{1,0:T(8,128)(2,1)} %copy-done.140, bf16[1024,896]{1,0:T(8,128)(2,1)} %copy-done.139, ...), kind=kOutput, calls=%fused_computation.18 | convolution fusion | flops 37702991872 | bytes 44826624 | tf_op jit(solution)/shard_map/dot_general | solution.py:98
  2702.8 95.1 %all-to-all-done.13 = bf16[4,128,2560]{2,1,0:T(8,128)(2,1)} async-done(((bf16[4,128,2560]{2,1,0:T(8,128)(2,1)}), bf16[4,128,2560]{2,1,0:T(8,128)(2,1)}, u32[]{:S(2)}, u32[]{:S(2)}) %all-to-all-start.13) | async-done | bytes 2621472 | tf_op jit(solution)/shard_map/all_to_all | solution.py:158
  2809.9 70.0 %shard_map.660 = (bf16[1024,2560]{1,0:T(8,128)(2,1)}, bf16[1024,2560]{1,0:T(8,128)(2,1)}, f32[1024,128]{1,0:T(8,128)}) custom-call(bf16[1024,2560]{1,0:T(8,128)(2,1)} %get-tuple-element.60.query_ref, bf16[1024,2560]{1,0:T(8,128)(2,1)} %get-tuple-element.61.keyval_ref, bf16[1024,1280]{1,0:T(8,128)(2,1)} %bitcast.469, bf16[1024,128]{1,0:T(8,128)(2,1)} %pad.34.key_ref, ...), custom_call_target="tpu_custom_call" | custom-call | tf_op jit(solution)/shard_map/pallas_call | solution.py:501
  2940.5 25.8 all_to_all.312
  3027.8 84.5 %collective-permute-done.80 = bf16[256,2560]{1,0:T(8,128)(2,1)S(1)} collective-permute-done((bf16[256,2560]{1,0:T(8,128)(2,1)S(1)}, bf16[256,2560]{1,0:T(8,128)(2,1)S(1)}, u32[]{:S(2)}, u32[]{:S(2)}) %collective-permute-start.80) | collective-permute-done | bytes 1310752 | tf_op jit(solution)/shard_map/ppermute | solution.py:181
  3240.1 28.1 collective-permute-done.81
  3269.1 47.5 %collective-permute-done.77 = bf16[256,2560]{1,0:T(8,128)(2,1)} collective-permute-done((bf16[256,2560]{1,0:T(8,128)(2,1)}, bf16[256,2560]{1,0:T(8,128)(2,1)}, u32[]{:S(2)}, u32[]{:S(2)}) %collective-permute-start.77) | collective-permute-done | bytes 1310752 | tf_op jit(solution)/shard_map/ppermute | solution.py:181
  3377.0 21.2 all-to-all-done.29
  3418.1 18.2 all-to-all-done.19
  3550.2 17.3 add_divide_fusion
  (936 shorter events, 1240.6 us)
Async XLA Ops:
  7.2 300.2 %all-gather.5.cloned.1.call-start = ((), (), s32[]{:S(2)}) async-start(), calls=%async_computation.40 | async-start | bytes 2048000 | tf_op jit(solution)/shard_map/all_gather | solution.py:599
  32.2 248.2 %collective-permute-start = (bf16[160,1056]{1,0:T(8,128)(2,1)}, bf16[160,1056]{1,0:T(8,128)(2,1)}, u32[]{:S(2)}, u32[]{:S(2)}) collective-permute-start(bf16[160,1056]{1,0:T(8,128)(2,1)} %copy.892), channel_id=1, source_target_pairs={{0,8},{4,12},{8,0},{12,4},{16,24},{20,28},{24,16},{28,20},{1,9},{5... | collective-permute-start | bytes 1013768 | tf_op jit(solution)/shard_map/ppermute | solution.py:181
  33.7 248.7 %collective-permute-start.1 = (bf16[160,1056]{1,0:T(8,128)(2,1)}, bf16[160,1056]{1,0:T(8,128)(2,1)}, u32[]{:S(2)}, u32[]{:S(2)}) collective-permute-start(bf16[160,1056]{1,0:T(8,128)(2,1)} %copy.892), channel_id=1, source_target_pairs={{0,16},{4,20},{8,24},{12,28},{16,0},{20,4},{24,8},{28,12},{1,17},{... | collective-permute-start | bytes 1013768 | tf_op jit(solution)/shard_map/ppermute | solution.py:181
  36.2 262.1 %collective-permute-start.3 = (bf16[160,1056]{1,0:T(8,128)(2,1)}, bf16[160,1056]{1,0:T(8,128)(2,1)}, u32[]{:S(2)}, u32[]{:S(2)}) collective-permute-start(bf16[160,1056]{1,0:T(8,128)(2,1)} %copy.895), channel_id=1, source_target_pairs={{0,8},{4,12},{8,0},{12,4},{16,24},{20,28},{24,16},{28,20},{1,9},{5... | collective-permute-start | bytes 1013768 | tf_op jit(solution)/shard_map/ppermute | solution.py:181
  36.7 247.4 %collective-permute-start.4 = (bf16[160,1056]{1,0:T(8,128)(2,1)}, bf16[160,1056]{1,0:T(8,128)(2,1)}, u32[]{:S(2)}, u32[]{:S(2)}) collective-permute-start(bf16[160,1056]{1,0:T(8,128)(2,1)} %copy.895), channel_id=1, source_target_pairs={{0,16},{4,20},{8,24},{12,28},{16,0},{20,4},{24,8},{28,12},{1,17},{... | collective-permute-start | bytes 1013768 | tf_op jit(solution)/shard_map/ppermute | solution.py:181
  63.6 172.5 %collective-permute-start.13 = (bf16[32,2560]{1,0:T(8,128)(2,1)}, bf16[32,2560]{1,0:T(8,128)(2,1)}, u32[]{:S(2)}, u32[]{:S(2)}) collective-permute-start(bf16[32,2560]{1,0:T(8,128)(2,1)} %get-tuple-element.547), channel_id=1, source_target_pairs={{0,8},{4,12},{8,0},{12,4},{16,24},{20,28},{24,16},{28,20},{1,9},{5... | collective-permute-start | bytes 491528 | tf_op jit(solution)/shard_map/ppermute | solution.py:181
  103.1 125.8 %all-to-all-start = ((bf16[8,2,384]{2,1,0:T(2,128)(2,1)}), bf16[8,2,384]{2,1,0:T(2,128)(2,1)S(1)}, u32[]{:S(2)}, u32[]{:S(2)}) async-start(bf16[8,2,384]{2,1,0:T(2,128)(2,1)} %reshape.733), calls=%async_computation | async-start | bytes 24576 | tf_op jit(solution)/shard_map/all_to_all | solution.py:170
  233.3 2065.2 %all-gather.7.cloned.1.call-start = ((), (), s32[]{:S(2)}) async-start(), calls=%async_computation.41 | async-start | bytes 10240000 | tf_op jit(solution)/shard_map/all_gather | solution.py:621
  277.9 160.1 %collective-permute-start.7 = (bf16[96,1920]{1,0:T(8,128)(2,1)}, bf16[96,1920]{1,0:T(8,128)(2,1)}, u32[]{:S(2)}, u32[]{:S(2)}) collective-permute-start(bf16[96,1920]{1,0:T(8,128)(2,1)} %get-tuple-element.539), channel_id=1, source_target_pairs={{0,8},{4,12},{8,0},{12,4},{16,24},{20,28},{24,16},{28,20},{1,9},{5... | collective-permute-start | bytes 1105928 | tf_op jit(solution)/shard_map/ppermute | solution.py:181
  280.4 157.9 %collective-permute-start.8 = (bf16[96,1920]{1,0:T(8,128)(2,1)}, bf16[96,1920]{1,0:T(8,128)(2,1)}, u32[]{:S(2)}, u32[]{:S(2)}) collective-permute-start(bf16[96,1920]{1,0:T(8,128)(2,1)} %get-tuple-element.539), channel_id=1, source_target_pairs={{0,16},{4,20},{8,24},{12,28},{16,0},{20,4},{24,8},{28,12},{1,17},{... | collective-permute-start | bytes 1105928 | tf_op jit(solution)/shard_map/ppermute | solution.py:181
  427.1 1558.9 %all-to-all-start.11 = ((bf16[8,200,320]{2,1,0:T(8,128)(2,1)}), bf16[8,200,320]{2,1,0:T(8,128)(2,1)}, u32[]{:S(2)}, u32[]{:S(2)}) async-start(bf16[8,200,320]{2,1,0:T(8,128)(2,1)} %copy.928), calls=%async_computation.11 | async-start | bytes 2457600 | tf_op jit(solution)/shard_map/all_to_all | solution.py:626
  431.7 1899.1 %all-gather.9.cloned.1.call-start = ((), (), s32[]{:S(2)}) async-start(), calls=%async_computation.42 | async-start | bytes 5120000 | tf_op jit(solution)/shard_map/all_gather | solution.py:628
  437.8 1736.1 %collective-permute-start.25 = (bf16[4,320,2560]{2,1,0:T(8,128)(2,1)}, bf16[4,320,2560]{2,1,0:T(8,128)(2,1)}, u32[]{:S(2)}, u32[]{:S(2)}) collective-permute-start(bf16[4,320,2560]{2,1,0:T(8,128)(2,1)} %bitcast_dynamic-update-slice_fusion.4), channel_id=1, source_target_pairs={{0,4},{4,0},{8,12},{12,8},{16,20},{20,16},{24,28},{28,24},{1,5},{5... | collective-permute-start | bytes 19660808 | tf_op jit(solution)/shard_map/ppermute | solution.py:181
  438.1 1618.9 %collective-permute-start.28 = (bf16[256,2560]{1,0:T(8,128)(2,1)}, bf16[256,2560]{1,0:T(8,128)(2,1)}, u32[]{:S(2)}, u32[]{:S(2)}) collective-permute-start(bf16[256,2560]{1,0:T(8,128)(2,1)} %get-tuple-element.528), channel_id=1, source_target_pairs={{0,4},{4,0},{8,12},{12,8},{16,20},{20,16},{24,28},{28,24},{1,5},{5... | collective-permute-start | bytes 3932168 | tf_op jit(solution)/shard_map/ppermute | solution.py:181
  438.3 1619.1 %collective-permute-start.29 = (bf16[256,2560]{1,0:T(8,128)(2,1)}, bf16[256,2560]{1,0:T(8,128)(2,1)}, u32[]{:S(2)}, u32[]{:S(2)}) collective-permute-start(bf16[256,2560]{1,0:T(8,128)(2,1)} %get-tuple-element.529), channel_id=1, source_target_pairs={{0,4},{4,0},{8,12},{12,8},{16,20},{20,16},{24,28},{28,24},{1,5},{5... | collective-permute-start | bytes 3932168 | tf_op jit(solution)/shard_map/ppermute | solution.py:181
  440.2 151.2 %collective-permute-start.9 = (bf16[96,1920]{1,0:T(8,128)(2,1)}, bf16[96,1920]{1,0:T(8,128)(2,1)}, u32[]{:S(2)}, u32[]{:S(2)}) collective-permute-start(bf16[96,1920]{1,0:T(8,128)(2,1)} %collective-permute-done.7), channel_id=1, source_target_pairs={{0,16},{4,20},{8,24},{12,28},{16,0},{20,4},{24,8},{28,12},{1,17},{... | collective-permute-start | bytes 1105928 | tf_op jit(solution)/shard_map/ppermute | solution.py:181
  441.9 152.6 %collective-permute-start.12 = (bf16[96,1920]{1,0:T(8,128)(2,1)}, bf16[96,1920]{1,0:T(8,128)(2,1)S(1)}, u32[]{:S(2)}, u32[]{:S(2)}) collective-permute-start(bf16[96,1920]{1,0:T(8,128)(2,1)} %collective-permute-done.11), channel_id=1, source_target_pairs={{0,8},{4,12},{8,0},{12,4},{16,24},{20,28},{24,16},{28,20},{1,9},{5... | collective-permute-start | bytes 1105928 | tf_op jit(solution)/shard_map/ppermute | solution.py:181
  2169.8 487.4 %all-to-all-start.34 = ((f32[4,1,20]{2,1,0:T(1,128)}), f32[4,1,20]{2,1,0:T(1,128)}, u32[]{:S(2)}, u32[]{:S(2)}) async-start(f32[4,1,20]{2,1,0:T(1,128)} %broadcast_in_dim.297), calls=%async_computation.36 | async-start | bytes 4096 | tf_op jit(solution)/shard_map/all_to_all | solution.py:170
  2173.6 943.7 %reduce-scatter.5.cloned.1.call-start = ((), (), s32[]{:S(2)}) async-start(), calls=%async_computation.44 | async-start | bytes 5120000 | tf_op jit(solution)/shard_map/reduce_scatter | solution.py:744
  2284.7 155.6 %collective-permute-start.56 = (bf16[256,2560]{1,0:T(8,128)(2,1)}, bf16[256,2560]{1,0:T(8,128)(2,1)}, u32[]{:S(2)}, u32[]{:S(2)}) collective-permute-start(bf16[256,2560]{1,0:T(8,128)(2,1)} %collective-permute-done.54), channel_id=1, source_target_pairs={{0,4},{4,0},{8,12},{12,8},{16,20},{20,16},{24,28},{28,24},{1,5},{5... | collective-permute-start | bytes 3932168 | tf_op jit(solution)/shard_map/ppermute | solution.py:181
  2284.7 155.6 %collective-permute-start.57 = (bf16[256,2560]{1,0:T(8,128)(2,1)}, bf16[256,2560]{1,0:T(8,128)(2,1)}, u32[]{:S(2)}, u32[]{:S(2)}) collective-permute-start(bf16[256,2560]{1,0:T(8,128)(2,1)} %collective-permute-done.55), channel_id=1, source_target_pairs={{0,4},{4,0},{8,12},{12,8},{16,20},{20,16},{24,28},{28,24},{1,5},{5... | collective-permute-start | bytes 3932168 | tf_op jit(solution)/shard_map/ppermute | solution.py:181
  2360.5 177.5 %collective-permute-start.39 = (bf16[256,2560]{1,0:T(8,128)(2,1)}, bf16[256,2560]{1,0:T(8,128)(2,1)}, u32[]{:S(2)}, u32[]{:S(2)}) collective-permute-start(bf16[256,2560]{1,0:T(8,128)(2,1)} %get-tuple-element.517), channel_id=1, source_target_pairs={{0,4},{4,0},{8,12},{12,8},{16,20},{20,16},{24,28},{28,24},{1,5},{5... | collective-permute-start | bytes 3932168 | tf_op jit(solution)/shard_map/ppermute | solution.py:181
  2360.5 183.4 %collective-permute-start.64 = (bf16[256,2560]{1,0:T(8,128)(2,1)}, bf16[256,2560]{1,0:T(8,128)(2,1)}, u32[]{:S(2)}, u32[]{:S(2)}) collective-permute-start(bf16[256,2560]{1,0:T(8,128)(2,1)} %get-tuple-element.518), channel_id=1, source_target_pairs={{0,4},{4,0},{8,12},{12,8},{16,20},{20,16},{24,28},{28,24},{1,5},{5... | collective-permute-start | bytes 3932168 | tf_op jit(solution)/shard_map/ppermute | solution.py:181
  2409.8 139.8 %collective-permute-start.49 = (bf16[256,2560]{1,0:T(8,128)(2,1)}, bf16[256,2560]{1,0:T(8,128)(2,1)}, u32[]{:S(2)}, u32[]{:S(2)}) collective-permute-start(bf16[256,2560]{1,0:T(8,128)(2,1)} %get-tuple-element.521), channel_id=1, source_target_pairs={{0,4},{4,0},{8,12},{12,8},{16,20},{20,16},{24,28},{28,24},{1,5},{5... | collective-permute-start | bytes 3932168 | tf_op jit(solution)/shard_map/ppermute | solution.py:181
  2664.0 133.8 %all-to-all-start.13 = ((bf16[4,128,2560]{2,1,0:T(8,128)(2,1)}), bf16[4,128,2560]{2,1,0:T(8,128)(2,1)}, u32[]{:S(2)}, u32[]{:S(2)}) async-start(bf16[4,128,2560]{2,1,0:T(8,128)(2,1)} %bitcast.91), calls=%async_computation.13 | async-start | bytes 5242880 | tf_op jit(solution)/shard_map/all_to_all | solution.py:158
  2668.8 804.2 %reduce-scatter.3.cloned.1.call-start = ((), (), s32[]{:S(2)}) async-start(), calls=%async_computation.43 | async-start | bytes 10240000 | tf_op jit(solution)/shard_map/reduce_scatter | solution.py:754
  2691.0 547.8 %collective-permute-start.75 = (bf16[256,2560]{1,0:T(8,128)(2,1)}, bf16[256,2560]{1,0:T(8,128)(2,1)}, u32[]{:S(2)}, u32[]{:S(2)}) collective-permute-start(bf16[256,2560]{1,0:T(8,128)(2,1)} %get-tuple-element.498), channel_id=1, source_target_pairs={{0,4},{4,0},{8,12},{12,8},{16,20},{20,16},{24,28},{28,24},{1,5},{5... | collective-permute-start | bytes 3932168 | tf_op jit(solution)/shard_map/ppermute | solution.py:181
  2931.2 291.8 %collective-permute-start.68 = (bf16[256,2560]{1,0:T(8,128)(2,1)}, bf16[256,2560]{1,0:T(8,128)(2,1)}, u32[]{:S(2)}, u32[]{:S(2)}) collective-permute-start(bf16[256,2560]{1,0:T(8,128)(2,1)} %get-tuple-element.497), channel_id=1, source_target_pairs={{0,4},{4,0},{8,12},{12,8},{16,20},{20,16},{24,28},{28,24},{1,5},{5... | collective-permute-start | bytes 3932168 | tf_op jit(solution)/shard_map/ppermute | solution.py:181
  3005.4 129.7 %all-to-all-start.28 = ((bf16[4,320,2560]{2,1,0:T(8,128)(2,1)}), bf16[4,320,2560]{2,1,0:T(8,128)(2,1)}, u32[]{:S(2)}, u32[]{:S(2)}) async-start(bf16[4,320,2560]{2,1,0:T(8,128)(2,1)} %reduce_sum.290), calls=%async_computation.28 | async-start | bytes 13107200 | tf_op jit(solution)/shard_map/all_to_all | solution.py:270
  3027.3 181.0 %collective-permute-start.71 = (bf16[256,2560]{1,0:T(8,128)(2,1)}, bf16[256,2560]{1,0:T(8,128)(2,1)}, u32[]{:S(2)}, u32[]{:S(2)}) collective-permute-start(bf16[256,2560]{1,0:T(8,128)(2,1)} %get-tuple-element.505), channel_id=1, source_target_pairs={{0,4},{4,0},{8,12},{12,8},{16,20},{20,16},{24,28},{28,24},{1,5},{5... | collective-permute-start | bytes 3932168 | tf_op jit(solution)/shard_map/ppermute | solution.py:181
  3027.6 182.7 %collective-permute-start.76 = (bf16[256,2560]{1,0:T(8,128)(2,1)}, bf16[256,2560]{1,0:T(8,128)(2,1)}, u32[]{:S(2)}, u32[]{:S(2)}) collective-permute-start(bf16[256,2560]{1,0:T(8,128)(2,1)} %get-tuple-element.506), channel_id=1, source_target_pairs={{0,4},{4,0},{8,12},{12,8},{16,20},{20,16},{24,28},{28,24},{1,5},{5... | collective-permute-start | bytes 3932168 | tf_op jit(solution)/shard_map/ppermute | solution.py:181
  3210.4 123.6 %all-to-all-start.21 = ((bf16[4,192,2560]{2,1,0:T(8,128)(2,1)}), bf16[4,192,2560]{2,1,0:T(8,128)(2,1)}, u32[]{:S(2)}, u32[]{:S(2)}) async-start(bf16[4,192,2560]{2,1,0:T(8,128)(2,1)} %bitcast.512), calls=%async_computation.21 | async-start | bytes 7864320 | tf_op jit(solution)/shard_map/all_to_all | solution.py:810
  (240 other events, 11501.9 us)
Sparse Core Ops, SparseCore 0:
  38.2 38.5 all-gather.4
  307.6 167.4 all-gather.6
  1991.9 75.5 all-gather.8
  2538.1 71.5 reduce-scatter.4
  2677.6 181.6 reduce-scatter.2

commit v2 on v1

--- a/solution.py
+++ b/solution.py
@@ -5,6 +5,7 @@
 import jax.numpy as jnp
 from jax import lax
 from jax.experimental import pallas as pl
+from jax.experimental.layout import Layout, with_layout_constraint
 from jax.experimental.pallas import tpu as pltpu
 from jax.sharding import PartitionSpec as P
 
@@ -150,18 +151,20 @@
     return near, cross
 
 
-def to_trees(values, group_size, near):
+def near_parts(values, group_size, near):
     micro, count, width = values.shape
     parts = values.reshape(micro, group_size, count // group_size, width)
     parts = lax.all_to_all(parts, "dp", 1, 0, axis_index_groups=near)
-    parts = parts.reshape(group_size * micro, count // group_size, width)
-    return lax.all_to_all(parts, "mp", 0, 0, tiled=True)
+    return parts.reshape(group_size * micro, count // group_size, width)
+
+
+def to_trees(values, group_size, near):
+    return lax.all_to_all(near_parts(values, group_size, near), "mp", 0, 0, tiled=True)
 
 
 def to_owners(values, group_size, near):
     planes, count, width = values.shape
-    parts = lax.all_to_all(values, "mp", 0, 0, tiled=True)
-    parts = parts.reshape(group_size, planes // group_size, count, width)
+    parts = values.reshape(group_size, planes // group_size, count, width)
     parts = lax.all_to_all(parts, "dp", 0, 1, axis_index_groups=near)
     return parts.reshape(planes // group_size, group_size * count, width)
 
@@ -210,14 +213,14 @@
     return (first_arg.astype(jnp.float32) + second_arg.astype(jnp.float32)).astype(jnp.bfloat16)
 
 
-def scatter_tokens(pieces, group_size, data_count):
+def scatter_tokens(pieces, group_size, data_count, near_count):
     bits = bits_of(group_size, data_count)
     halves = []
     for half in range(2):
         held = {}
         for index in range(0, data_count, group_size):
             total = pieces[(index, half)]
-            for near in range(1, group_size):
+            for near in range(1, near_count):
                 total = add_low(total, swap_bit(pieces[(index ^ near, half)], near, data_count))
             held[index] = total
         for bit in bits if half == 0 else bits[::-1]:
@@ -229,46 +232,96 @@
     return jnp.concatenate(halves, axis=0)
 
 
-def gather_far(block, group_size, data_count, data_index):
-    far_count = data_count // group_size
-    rows = block.shape[0] // 2
-    own = data_index // group_size
-    bits = bits_of(group_size, data_count)
-    out = jnp.zeros((far_count,) + block.shape, block.dtype)
-    for half in range(2):
-        got = {0: block[half * rows : (half + 1) * rows]}
-        for bit in bits if half == 0 else bits[::-1]:
-            for index in sorted(got):
-                got[index ^ bit] = swap_bit(got[index], bit, data_count)
-        for index in sorted(got):
-            out = lax.dynamic_update_slice(
-                out, got[index][None], (own ^ (index // group_size), half * rows, 0)
+def spread_planes(values, model_count, model_index):
+    out = jnp.zeros((model_count,) + values.shape, values.dtype)
+    for shift in range(model_count):
+        part = values
+        if shift:
+            part = lax.ppermute(
+                values, "mp", [(i, (i + shift) % model_count) for i in range(model_count)]
             )
+        place = (model_index + model_count - shift) % model_count
+        out = lax.dynamic_update_slice(out, part[None], (place,) + (0,) * values.ndim)
     return out
 
 
-def gather_rows(block, group_size, data_count, data_index):
-    far = gather_far(block, group_size, data_count, data_index)
+def row_major(values):
+    return with_layout_constraint(values, Layout(major_to_minor=tuple(range(values.ndim))))
+
+
+def far_parts(block, group_size, data_count):
+    return [block] + [
+        swap_bit(block, far, data_count) for far in range(group_size, data_count, group_size)
+    ]
+
+
+def in_order(parts, own):
+    out = jnp.zeros((len(parts),) + parts[0].shape, parts[0].dtype)
+    for index, part in enumerate(parts):
+        out = lax.dynamic_update_slice(out, part[None], (own ^ index,) + (0,) * part.ndim)
+    return row_major(out)
+
+
+def rows_of(parts, group_size, data_count, data_index):
+    far = in_order(parts, data_index // group_size)
     own = data_index % group_size
-    out = jnp.zeros((far.shape[0], group_size) + block.shape, block.dtype)
+    out = jnp.zeros((len(parts), group_size) + parts[0].shape, far.dtype)
     for near in range(group_size):
         part = far if near == 0 else swap_bit(far, near, data_count)
         out = lax.dynamic_update_slice(out, part[:, None], (0, own ^ near, 0, 0))
-    return out.reshape((data_count * block.shape[0],) + block.shape[1:])
-
-
-def after(values, *others):
-    return lax.optimization_barrier((values,) + others)[0]
-
-
-def scatter_rows(grad_w, group_size, data_count, near, cross):
-    far_count = data_count // group_size
-    rows = grad_w.shape[0] // data_count
-    parts = grad_w.astype(jnp.bfloat16).reshape(far_count, group_size, rows, -1)
-    parts = lax.all_to_all(parts, "dp", 1, 0, axis_index_groups=near)
-    parts = jnp.sum(parts.astype(jnp.float32), axis=0).astype(jnp.bfloat16)
-    parts = lax.all_to_all(parts, "dp", 0, 0, tiled=True, axis_index_groups=cross)
-    return jnp.sum(parts.astype(jnp.float32), axis=0)
+    return out.reshape((data_count * parts[0].shape[0],) + parts[0].shape[1:])
+
+
+def blocks_of(parts, group_size, data_count):
+    blocks = []
+    for part in parts:
+        blocks.append(part)
+        for near in range(1, group_size):
+            blocks.append(swap_bit(part, near, data_count))
+    return jnp.concatenate(blocks, axis=0)
+
+
+def scatter_blocks(values, group_size, data_count):
+    parts = values.reshape(data_count // group_size, group_size, -1, values.shape[-1])
+    total = parts[:, 0].astype(jnp.float32)
+    for near in range(1, group_size):
+        total = total + swap_bit(parts[:, near], near, data_count).astype(jnp.float32)
+    total = total.astype(jnp.bfloat16)
+    result = total[0].astype(jnp.float32)
+    for far in range(1, data_count // group_size):
+        result = result + swap_bit(total[far], far * group_size, data_count).astype(jnp.float32)
+    return result
+
+
+def tie(*values):
+    return lax.optimization_barrier(values)
+
+
+def far_sum(parts, group_size, data_count, data_index):
+    own = data_index // group_size
+
+    def part_of(far):
+        return lax.dynamic_index_in_dim(parts, own ^ far, 0, keepdims=False)
+
+    total = part_of(0).astype(jnp.float32)
+    for far in range(1, data_count // group_size):
+        total = total + swap_bit(part_of(far), far * group_size, data_count).astype(jnp.float32)
+    return total
+
+
+def near_sum(grad_w, group_size, data_count, data_index):
+    own = data_index % group_size
+    parts = grad_w.astype(jnp.bfloat16).reshape(
+        data_count // group_size, group_size, -1, grad_w.shape[-1]
+    )
+
+    def part_of(near):
+        return lax.dynamic_index_in_dim(parts, own ^ near, 1, keepdims=False)
+
+    total = part_of(0).astype(jnp.float32)
+    for near in range(1, group_size):
+        total = total + swap_bit(part_of(near), near, data_count).astype(jnp.float32)
+    return total.astype(jnp.bfloat16)
 
 
 def scatter_columns(grad_w, model_count):
@@ -456,6 +509,14 @@
         shared_out_ref[...] = total_ref[...] * scale
 
 
+def attend_cost(length, steps, products):
+    return pl.CostEstimate(
+        flops=int(products * 2 * steps * 2 * length * length * 256),
+        bytes_accessed=steps * length * 256 * 8,
+        transcendentals=steps * 2 * length * length,
+    )
+
+
 def resident(shape):
     return pl.BlockSpec(shape, lambda step: (0,) * len(shape))
 
@@ -490,6 +551,7 @@
             jax.ShapeDtypeStruct((steps, 16, 128), jnp.float32),
         ],
         compiler_params=pltpu.CompilerParams(vmem_limit_bytes=56 * 1024 * 1024),
+        cost_estimate=attend_cost(length, steps, 2.0),
     )(query_latent, keyval_latent, query_w, keyval_w, key_lanes, bias, *tables)
 
 
@@ -516,6 +578,7 @@
             pltpu.VMEM((length, 128), jnp.float32),
         ],
         compiler_params=pltpu.CompilerParams(vmem_limit_bytes=56 * 1024 * 1024),
+        cost_estimate=attend_cost(length, steps, 4.0),
     )(queries, keyval, grad, key_lanes, bias, *tables)
 
 
@@ -589,44 +652,51 @@
     own_heads = query_weight.shape[1] // (NOPE_DIM + ROPE_DIM)
     latent_all = latent_weight.shape[1] * model_count
 
-    gain_all = spread(gains.astype(bf16), "dp", data_count).reshape(-1).astype(jnp.float32)
+    def columns(far):
+        return jnp.swapaxes(far, 0, 1).reshape(far.shape[1], -1)
+
+    def exchange_units(values):
+        return lax.all_to_all(values, "dp", 0, 0, tiled=True)
+
+    query_rows = query_weight.shape[0]
+    keyval_rows = keyval_weight.shape[0]
+    unit_count = down_weight.shape[1] // data_count
+    hidden_units = unit_count * model_count
+    padded = -(-hidden_units // 128) * 128
+    gain_all = spread(gains.astype(bf16), "dp", data_count)
+    output_w = lax.all_gather(project_weight.astype(bf16), "mp", axis=0)
+    lat_w = spread_planes(row_major(latent_weight.astype(bf16)), model_count, model_index)
+    query_pad = jnp.pad(
+        query_weight.astype(bf16).reshape(query_rows, own_heads, NOPE_DIM + ROPE_DIM),
+        ((0, 0), (0, 0), (0, 128 - NOPE_DIM - ROPE_DIM)),
+    ).reshape(query_rows, own_heads * 128)
+    both_w = jnp.concatenate([query_pad, keyval_weight.astype(bf16)], axis=0)
+    both_w, lat_w = tie(row_major(both_w), lat_w)
+    both_w = spread_planes(both_w, model_count, model_index)
+    units = jnp.concatenate(
+        [
+            jnp.transpose(
+                gateup_weight.astype(bf16).reshape(-1, 2, data_count, unit_count), (2, 1, 3, 0)
+            ),
+            jnp.transpose(
+                down_weight.astype(bf16).reshape(-1, 1, data_count, unit_count), (2, 1, 3, 0)
+            ),
+        ],
+        axis=1,
+    )
+    units, gain_all = tie(units, gain_all)
+    units = exchange_units(units)
+    lat_w = far_parts(row_major(columns(lat_w)), group, data_count)
+    both_w, *lat_w = tie(both_w, *lat_w)
+    lat_w = rows_of(lat_w, group, data_count, data_index)
+    both_w = columns(both_w).reshape(query_rows + keyval_rows, group, -1)
+    both_w = lax.all_to_all(both_w, "dp", 1, 0, axis_index_groups=near)
+    both_w = in_order(far_parts(row_major(both_w), group, data_count), data_index // group)
+    gain_all = gain_all.reshape(-1).astype(jnp.float32)
     gain_one = gain_all[:WIDTH]
     gain_two = gain_all[WIDTH : 2 * WIDTH]
     gain_query = gain_all[2 * WIDTH : 2 * WIDTH + QUERY_RANK]
     gain_keyval = gain_all[2 * WIDTH + QUERY_RANK :]
-
-    def columns(weight):
-        return lax.all_gather(weight.astype(bf16), "mp", axis=1, tiled=True)
-
-    def head_part(weight, width):
-        rows = columns(weight)
-        parts = rows.reshape(rows.shape[0], group, -1)
-        parts = lax.all_to_all(parts, "dp", 1, 0, axis_index_groups=near)
-        parts = parts.reshape(group * rows.shape[0], -1)
-        full = gather_far(parts, group, data_count, data_index)
-        full = full.reshape(data_count * rows.shape[0], heads, width)
-        return jnp.pad(full, ((0, 0), (0, 0), (0, 128 - width))).reshape(full.shape[0], -1)
-
-    lat_w = gather_rows(columns(latent_weight), group, data_count, data_index)
-    query_w = head_part(query_weight, NOPE_DIM + ROPE_DIM)
-    keyval_w = head_part(keyval_weight, NOPE_DIM + VALUE_DIM)
-    output_w = gather_rows(columns(project_weight), group, data_count, data_index)
-
-    unit_count = down_weight.shape[1] // data_count
-    hidden_units = unit_count * model_count
-    padded = -(-hidden_units // 128) * 128
-    gate_t = gateup_weight.astype(bf16).reshape(-1, 2, data_count, unit_count)
-    gate_t = lax.all_to_all(jnp.transpose(gate_t, (2, 1, 3, 0)), "dp", 0, 0, tiled=True)
-    gate_t = jnp.transpose(gate_t, (1, 2, 0, 3)).reshape(2 * unit_count, WIDTH)
-    gate_t = lax.all_gather(gate_t, "mp", axis=0)
-    gate_t = jnp.transpose(gate_t.reshape(model_count, 2, unit_count, WIDTH), (1, 0, 2, 3))
-    gate_t = gate_t.reshape(2, hidden_units, WIDTH)
-    gate_t = jnp.pad(gate_t, ((0, 0), (0, padded - hidden_units), (0, 0))).reshape(-1, WIDTH)
-    down_t = down_weight.astype(bf16).reshape(-1, data_count, unit_count)
-    down_t = lax.all_to_all(jnp.transpose(down_t, (1, 2, 0)), "dp", 0, 0, tiled=True)
-    down_t = jnp.transpose(down_t, (1, 0, 2)).reshape(unit_count, WIDTH)
-    down_t = lax.all_gather(down_t, "mp", axis=0).reshape(hidden_units, WIDTH)
-    down_t = jnp.pad(down_t, ((0, padded - hidden_units), (0, 0)))
 
     tok = tokens.reshape(micro * share, WIDTH).astype(jnp.float32)
     normed, inverse_one = rms_parts(tok, gain_one)
@@ -640,10 +710,29 @@
     keyval_normed, inverse_keyval = rms_parts(keyval_raw, gain_keyval)
     sent = jnp.concatenate([query_normed, keyval_normed, key_rope], axis=1).astype(bf16)
 
-    mid = to_trees(sent.reshape(micro, share, latent_all), group, near)
+    mid, units = tie(
+        near_parts(sent.reshape(micro, share, latent_all), group, near), units
+    )
+    mid = lax.all_to_all(mid, "mp", 0, 0, tiled=True)
+    units = jnp.transpose(units, (1, 2, 0, 3)).reshape(3, unit_count, WIDTH)
+    gate_first = lax.all_gather(units[0], "mp", axis=0)
+    gate_pad = jnp.zeros((padded - hidden_units, WIDTH), bf16)
     tree = spread(mid, "dp", group, near)
+    tree, both_w, output_w = tie(tree, both_w, output_w)
+    tree, gate_first = tie(tree, gate_first)
+    query_w = both_w[:, :, :query_rows].reshape(data_count * query_rows, -1)
+    keyval_w = both_w[:, :, query_rows:].reshape(data_count * keyval_rows, -1)
+    gate_halves = [gate_first, lax.all_gather(units[1], "mp", axis=0)]
+    output_parts = far_parts(row_major(columns(output_w)), group, data_count)
     tree = jnp.swapaxes(tree, 0, 1).reshape(length, latent_all)
-    tree_parents = spread(parents[:, 0], "dp", group, near).reshape(group * micro, -1)
+    tree_parents = jnp.zeros((group, micro, parents.shape[2]), parents.dtype)
+    own_parents, normed = tie(parents[:, 0], normed)
+    for place in range(group):
+        part = own_parents if place == 0 else swap_bit(own_parents, place, data_count)
+        tree_parents = lax.dynamic_update_slice(
+            tree_parents, part[None], (own_part ^ place, 0, 0)
+        )
+    tree_parents = tree_parents.reshape(group * micro, -1)
     visible, cosine, sine_part = tree_layout(
         lax.dynamic_index_in_dim(tree_parents, model_index, 0, keepdims=False)
     )
@@ -668,20 +757,30 @@
     )
     peak_own = peaks.reshape(heads, 8, 128)[:, 0, 0]
 
-    def heads_out(values):
+    def heads_near(values):
         parts = values.reshape(model_count, group, share // group, -1)
         parts = lax.all_to_all(parts, "dp", 1, 2, axis_index_groups=near)
-        return to_owners(
-            parts.reshape(model_count, share // group, -1), group, near
-        ).reshape(micro * share, -1)
+        return parts.reshape(model_count, share // group, -1)
 
     def heads_in(values):
-        parts = to_trees(values.reshape(micro, share, -1), group, near)
-        parts = parts.reshape(model_count, share // group, group, -1)
+        parts = values.reshape(model_count, share // group, group, -1)
         parts = lax.all_to_all(parts, "dp", 2, 1, axis_index_groups=near)
         return parts.reshape(length, -1)
 
-    attended_own = heads_out(attended)
+    grad_out = cotangent.reshape(micro * share, WIDTH).astype(jnp.float32)
+    mixed_own, attended, *output_parts = tie(
+        (RESIDUAL * grad_out).astype(bf16), attended, *output_parts
+    )
+    output_w = rows_of(output_parts, group, data_count, data_index)
+    mixed_parts = [mixed_own] + [
+        swap_bit(mixed_own, bit, data_count) for bit in bits_of(group, data_count)
+    ]
+    attended, gate_halves[1] = tie(attended, gate_halves[1])
+    attended = heads_near(attended)
+    attended = lax.all_to_all(attended, "mp", 0, 0, tiled=True)
+    down_t, attended, *mixed_parts = tie(units[2], attended, *mixed_parts)
+    down_t = lax.all_gather(down_t, "mp", axis=0).reshape(hidden_units, WIDTH)
+    attended_own = to_owners(attended, group, near).reshape(micro * share, -1)
     branch = dot_last(attended_own, output_w)
     hidden = tok + RESIDUAL * branch
     normed_two, inverse_two = rms_parts(hidden, gain_two)
@@ -696,93 +795,129 @@
 
     def joined(values):
         pieces = gather_tokens(values, group, data_count)
-        return [jnp.concatenate([pieces[key] for key in keys], axis=0) for keys in order]
-
-    def parted(blocks):
+        return jnp.concatenate([pieces[key] for keys in order for key in keys], axis=0)
+
+    def parted(values):
         pieces = {}
-        for keys, block in zip(order, blocks):
-            for at, key in enumerate(keys):
-                pieces[key] = block[at * half_rows : (at + 1) * half_rows]
-        return scatter_tokens(pieces, group, data_count).astype(jnp.float32)
-
-    grad_out = cotangent.reshape(micro * share, WIDTH).astype(jnp.float32)
-    mixed_blocks = joined(after((RESIDUAL * grad_out).astype(bf16), tree))
-    normed_blocks = joined(normed_two)
-    active_blocks = []
-    grad_gateup_blocks = []
-    for mixed_block, normed_block in zip(mixed_blocks, normed_blocks):
-        gateup = dot_last(normed_block, gate_t)
-        gate_part = gateup[:, :padded]
-        up_part = gateup[:, padded:]
-        sigmoid_gate = jax.nn.sigmoid(gate_part)
-        silu_gate = gate_part * sigmoid_gate
-        active_blocks.append((silu_gate * up_part).astype(bf16))
-        grad_act = dot_last(mixed_block, down_t)
-        grad_gate = grad_act * up_part * sigmoid_gate * (1.0 + gate_part * (1.0 - sigmoid_gate))
-        grad_up = grad_act * silu_gate
-        grad_gateup_blocks.append(jnp.concatenate([grad_gate, grad_up], axis=1).astype(bf16))
-    grad_normed_blocks = [
-        jnp.dot(block, gate_t, preferred_element_type=jnp.float32).astype(bf16)
-        for block in grad_gateup_blocks
+        for at, key in enumerate([key for keys in order for key in keys]):
+            pieces[key] = values[at * half_rows : (at + 1) * half_rows]
+        return scatter_tokens(pieces, group, data_count, group).astype(jnp.float32)
+
+    down_t = jnp.concatenate([down_t, gate_pad], axis=0)
+    normed_full, *mixed_parts = tie(joined(normed_two), *mixed_parts)
+    early = [0] + [bit // group for bit in bits_of(group, data_count)]
+    mixed_parts = [
+        mixed_parts[early.index(far)]
+        if far in early
+        else swap_bit(mixed_parts[0], far * group, data_count)
+        for far in range(far_count)
     ]
-    grad_normed_two = parted(grad_normed_blocks)
-    activated = jnp.concatenate(active_blocks, axis=0)
-    grad_down_t = dot_first(activated, jnp.concatenate(mixed_blocks, axis=0)).astype(bf16)
-    grad_gate_t = dot_first(
-        jnp.concatenate(grad_gateup_blocks, axis=0), jnp.concatenate(normed_blocks, axis=0)
-    ).astype(bf16)
-    active_late = [after(block, grad_normed_two) for block in active_blocks]
-    mixed_out = parted(
+    mixed_full = blocks_of(mixed_parts, group, data_count)
+    gate_t = jnp.concatenate(
         [
-            jnp.dot(block, down_t, preferred_element_type=jnp.float32).astype(bf16)
-            for block in active_late
-        ]
-    )
-    layer_out = (hidden + RESIDUAL * mixed_out).astype(bf16)
+            gate_halves[0].reshape(hidden_units, WIDTH),
+            gate_pad,
+            gate_halves[1].reshape(hidden_units, WIDTH),
+            gate_pad,
+        ],
+        axis=0,
+    )
+    gateup = dot_last(normed_full, gate_t)
+    gate_part = gateup[:, :padded]
+    up_part = gateup[:, padded:]
+    grad_act = dot_last(mixed_full, down_t)
+    sigmoid_gate = jax.nn.sigmoid(gate_part)
+    silu_gate = gate_part * sigmoid_gate
+    activated = (silu_gate * up_part).astype(bf16)
+    grad_gate = grad_act * up_part * sigmoid_gate * (1.0 + gate_part * (1.0 - sigmoid_gate))
+    grad_up = grad_act * silu_gate
+    grad_gateup = jnp.concatenate([grad_gate, grad_up], axis=1).astype(bf16)
+    grad_normed_two = parted(
+        jnp.dot(grad_gateup, gate_t, preferred_element_type=jnp.float32).astype(bf16)
+    )
+    grad_down_t = dot_first(activated, mixed_full).astype(bf16)
+    grad_gate_t = dot_first(grad_gateup, normed_full).astype(bf16)
     grad_down_t = grad_down_t[:hidden_units]
 
     down_sum = lax.psum_scatter(
         grad_down_t.reshape(model_count, unit_count, WIDTH), "mp", scatter_dimension=0, tiled=True
     )
-    down_sum = jnp.transpose(down_sum.reshape(unit_count, data_count, -1), (1, 0, 2))
-    down_sum = lax.all_to_all(down_sum, "dp", 0, 0, tiled=True)
-    down_sum = jnp.transpose(down_sum, (2, 0, 1)).reshape(down_weight.shape)
+
+    grad_hidden = grad_out + rms_back(hidden, inverse_two, gain_two, grad_normed_two)
+    grad_gain_two = jnp.sum(grad_normed_two * hidden * inverse_two, axis=0)
+    grad_branch, grad_gate_t = tie((RESIDUAL * grad_hidden).astype(bf16), grad_gate_t)
     gate_sum = grad_gate_t.reshape(2, padded, WIDTH)[:, :hidden_units]
     gate_sum = jnp.transpose(
         gate_sum.reshape(2, model_count, unit_count, WIDTH), (1, 0, 2, 3)
     ).reshape(model_count, 2 * unit_count, WIDTH)
     gate_sum = lax.psum_scatter(gate_sum, "mp", scatter_dimension=0, tiled=True)
+    grad_attended = jnp.dot(grad_branch, output_w, preferred_element_type=jnp.float32)
+    grad_attended = near_parts(
+        grad_attended.astype(bf16).reshape(micro, share, -1), group, near
+    )
+    tail = grad_attended.shape[1] // 2
+    early = lax.all_to_all(grad_attended[:, :tail], "mp", 0, 0, tiled=True)
+    late, early, activated = tie(grad_attended[:, tail:], early, activated)
+    late = lax.all_to_all(late, "mp", 0, 0, tiled=True)
+    mixed_out = jnp.dot(activated, down_t, preferred_element_type=jnp.float32).astype(bf16)
+    mixed_out = lax.psum_scatter(
+        in_order(list(mixed_out.reshape(data_count, -1, WIDTH)), data_index),
+        "dp",
+        scatter_dimension=0,
+        tiled=True,
+    ).reshape(hidden.shape)
+    project_sum = near_sum(
+        dot_first(grad_branch, attended_own), group, data_count, data_index
+    )
+    grad_attended = heads_in(jnp.concatenate([early, late], axis=1))
+    grad_attended, project_sum = tie(grad_attended, project_sum)
+    project_sum = far_sum(project_sum, group, data_count, data_index)
+    grad_query_all, grad_keyval, grad_shared = attend_back(
+        queries, keyval, grad_attended, key_lanes, bias, tables, scale_attn, rows_attn
+    )
+    grad_shared = rotate_back(
+        grad_shared[:, NOPE_DIM : NOPE_DIM + ROPE_DIM], cosine, sine_part
+    )
+    latent_terms = jnp.concatenate(
+        [dot_last(grad_query_all, query_w), dot_last(grad_keyval, keyval_w), grad_shared], axis=1
+    ).astype(bf16)
+    down_sum = jnp.transpose(down_sum.reshape(unit_count, data_count, -1), (1, 0, 2))
+    down_sum = lax.all_to_all(down_sum, "dp", 0, 0, tiled=True)
     gate_sum = jnp.transpose(gate_sum.reshape(2 * unit_count, data_count, -1), (1, 0, 2))
     gate_sum = lax.all_to_all(gate_sum, "dp", 0, 0, tiled=True)
+    latent_terms, project_sum, down_sum, gate_sum = tie(
+        latent_terms, project_sum, down_sum, gate_sum
+    )
+    down_sum = jnp.transpose(down_sum, (2, 0, 1)).reshape(down_weight.shape)
     gate_sum = jnp.transpose(
         gate_sum.reshape(data_count, 2, unit_count, -1), (3, 1, 0, 2)
     ).reshape(gateup_weight.shape)
 
-    grad_hidden = grad_out + rms_back(hidden, inverse_two, gain_two, grad_normed_two)
-    grad_gain_two = jnp.sum(grad_normed_two * hidden * inverse_two, axis=0)
-    grad_branch = (RESIDUAL * grad_hidden).astype(bf16)
-    grad_branch = after(grad_branch, grad_gate_t, grad_down_t)
-    grad_attended = heads_in(
-        jnp.dot(grad_branch, output_w, preferred_element_type=jnp.float32).astype(bf16)
-    )
-    grad_project = dot_first(grad_branch, attended_own)
-    grad_query_all, grad_keyval, grad_shared = attend_back(
-        queries, keyval, grad_attended, key_lanes, bias, tables, scale_attn, rows_attn
-    )
-    grad_shared = rotate_back(
-        grad_shared[:, NOPE_DIM : NOPE_DIM + ROPE_DIM], cosine, sine_part
-    )
-    latent_terms = jnp.concatenate(
-        [dot_last(grad_query_all, query_w), dot_last(grad_keyval, keyval_w), grad_shared], axis=1
-    ).astype(bf16)
+    layer_out = (hidden + RESIDUAL * mixed_out).astype(bf16)
     parts = latent_terms.reshape(model_count, group, share // group, latent_all)
     parts = lax.all_to_all(parts, "dp", 1, 0, axis_index_groups=near)
     parts = jnp.sum(parts.astype(jnp.float32), axis=0).astype(bf16)
+    grad_both = jnp.concatenate(
+        [
+            dot_first(query_latent, grad_query_all)
+            .astype(bf16)
+            .reshape(data_count // group, group, query_rows, -1),
+            dot_first(keyval_latent, grad_keyval)
+            .astype(bf16)
+            .reshape(data_count // group, group, keyval_rows, -1),
+        ],
+        axis=2,
+    )
+    parts, grad_both = tie(lax.all_to_all(parts, "mp", 0, 0, tiled=True), grad_both)
+    grad_both = far_sum(
+        grad_both.reshape(data_count // group, group * (query_rows + keyval_rows), -1),
+        group,
+        data_count,
+        data_index,
+    )
     grad_latent_all = (
         to_owners(parts, group, near).reshape(micro * share, latent_all).astype(jnp.float32)
     )
-    grad_query_w = dot_first(query_latent, grad_query_all)
-    grad_keyval_w = dot_first(keyval_latent, grad_keyval)
 
     grad_query_up = grad_latent_all[:, :QUERY_RANK]
     grad_keyval_up = grad_latent_all[:, QUERY_RANK : QUERY_RANK + LATENT_RANK]
@@ -797,52 +932,66 @@
     grad_gain_query = jnp.sum(grad_query_up * query_raw * inverse_query, axis=0)
     grad_gain_keyval = jnp.sum(grad_keyval_up * keyval_raw * inverse_keyval, axis=0)
     grad_normed = dot_last(grad_latent, lat_w)
-    grad_latent_w = dot_first(normed, grad_latent)
+    latent_sum = near_sum(dot_first(normed, grad_latent), group, data_count, data_index)
     input_grad = grad_hidden + rms_back(tok, inverse_one, gain_one, grad_normed)
     grad_gain_one = jnp.sum(grad_normed * tok * inverse_one, axis=0)
     grad_gains = jnp.concatenate(
         [grad_gain_one, grad_gain_two, grad_gain_query, grad_gain_keyval]
     )
 
-    def head_grads(grad_w):
-        rows = grad_w.shape[0] // data_count
-        parts = grad_w.astype(bf16).reshape(data_count // group, group * rows, -1)
-        parts = lax.all_to_all(parts, "dp", 0, 0, tiled=True, axis_index_groups=cross)
-        parts = jnp.sum(parts.astype(jnp.float32), axis=0).astype(bf16)
-        parts = lax.all_to_all(
-            parts.reshape(group, rows, -1), "dp", 0, 1, axis_index_groups=near
-        )
-        return scatter_columns(parts.reshape(rows, -1), model_count)
-
+    grad_both = lax.all_to_all(
+        grad_both.astype(bf16).reshape(group, query_rows + keyval_rows, -1),
+        "dp",
+        0,
+        1,
+        axis_index_groups=near,
+    )
+    grad_both = scatter_columns(
+        grad_both.reshape(query_rows + keyval_rows, -1), model_count
+    )
     reduced = [
         scatter_columns(
-            scatter_rows(grad_latent_w, group, data_count, near, cross), model_count
+            far_sum(latent_sum, group, data_count, data_index), model_count
         ),
-        head_grads(grad_query_w)
-        .reshape(query_weight.shape[0], own_heads, 128)[:, :, : NOPE_DIM + ROPE_DIM]
+        grad_both[:query_rows]
+        .reshape(query_rows, own_heads, 128)[:, :, : NOPE_DIM + ROPE_DIM]
         .reshape(query_weight.shape),
-        head_grads(grad_keyval_w),
-        scatter_columns(
-            scatter_rows(grad_project, group, data_count, near, cross), model_count
-        ),
+        grad_both[query_rows:],
+        scatter_columns(project_sum, model_count),
         gate_sum.astype(jnp.float32),
         down_sum.astype(jnp.float32),
     ]
-    gain_parts = lax.all_to_all(
-        grad_gains.reshape(data_count, -1), "dp", 0, 0, tiled=True
-    )
-    gain_parts = jnp.sum(gain_parts, axis=0)
-    gains_grad = jnp.sum(spread(gain_parts, "mp", model_count), axis=0)
-
-    peak_all = jnp.max(spread(peak_own, "mp", model_count), axis=0)
-    peak_all = jnp.max(spread(peak_all, "dp", data_count // group, cross), axis=0)
-    all_peaks = spread(peak_all, "dp", group, near).reshape(HEADS)
+
+    peak_row = lax.dynamic_update_slice(
+        jnp.full((HEADS,), -1e30, jnp.float32), peak_own, (own_part * heads,)
+    )
+    small = jnp.concatenate(
+        [
+            grad_gains.reshape(data_count, -1),
+            jnp.broadcast_to(peak_row[None], (data_count, HEADS)),
+        ],
+        axis=1,
+    )
+    small = lax.all_to_all(small, "dp", 0, 0, tiled=True)
+    gain_count = gains.shape[0]
+    small = jnp.concatenate(
+        [jnp.sum(small[:, :gain_count], axis=0), jnp.max(small[:, gain_count:], axis=0)]
+    )
+    cells = ROTATE_ROWS * ROTATE_ROWS
+    small = jnp.pad(small, (0, -(gain_count + HEADS) % cells)).reshape(-1, cells)
+    grams = jnp.concatenate([gram_of(grad_w) for grad_w in reduced], axis=0)
+    gram_count = grams.shape[0]
+    packed = spread(
+        jnp.concatenate([grams.reshape(gram_count, cells), small], axis=0), "mp", model_count
+    )
+    grams = jnp.sum(packed[:, :gram_count], axis=0).reshape(grams.shape)
+    small = packed[:, gram_count:].reshape(model_count, -1)
+    gains_grad = jnp.sum(small[:, :gain_count], axis=0)
+    all_peaks = jnp.max(small[:, gain_count : gain_count + HEADS], axis=0)
     threshold = jnp.mean(all_peaks)
     clip_all = jnp.minimum(1.0, threshold / jnp.maximum(all_peaks, 1.0))
     clip_own = lax.dynamic_slice_in_dim(clip_all, model_index * own_heads, own_heads, 0)
 
-    grams = jnp.concatenate([gram_of(grad_w) for grad_w in reduced], axis=0)
-    grams = jnp.sum(spread(grams, "mp", model_count), axis=0)
     results = [
         layer_out.reshape(tokens.shape),
         input_grad.reshape(tokens.shape),

time: 3630 us -> 1730 us (0.48)
  local copies, waits for them, and re-layouts: 2010 us -> 427 us
  waiting for transfers between devices: 584 us -> 454 us
  blocking collectives: 153 us -> 59.1 us
  matrix products: 394 us -> 332 us
  starting transfers between devices: 164 us -> 123 us
    dynamic_update_slice x36 -> x35, local copies, waits for them, and re-layouts: 1620 us -> 68.6 us  [the longest x20 41.3 us: in_order(): lax.dynamic_update_slice(out, part[None], (own ^ index,) + (0,) * part.ndim)]
    ppermute x82 -> x58, waiting for transfers between devices: 391 us -> 285 us  [swap_bit(): return lax.ppermute(values, 'dp', [(i, i ^ bit) for i in range(data_count)])]
    all_gather x3 -> x0, blocking collectives: 55.6 us -> none  [columns(): return lax.all_gather(weight.astype(bf16), 'mp', axis=1, tiled=True)]
    all_to_all x13 -> x7, waiting for transfers between devices: 136 us -> 85.9 us  [the longest x1 46.3 us: on_device(): early = lax.all_to_all(grad_attended[:, :tail], 'mp', 0, 0, tiled=True)]
    dot_general x12 -> x6, matrix products: 156 us -> 116 us  [dot_last(): lax.dot_general(first_arg, second_arg, (((1,), (1,)), ((), ())), preferre...]
    all_to_all x8 -> x5, blocking collectives: 72.8 us -> 33.5 us  [the longest x2 12.8 us: near_parts(): parts = lax.all_to_all(parts, 'dp', 1, 0, axis_index_groups=near)]
    unnamed x373 -> x249, local copies, waits for them, and re-layouts: 95.9 us -> 75.9 us
    dot_general x8 -> x2, matrix products: 79.4 us -> 71.9 us  [the longest x1 46.2 us: on_device(): jnp.dot(grad_gateup, gate_t, preferred_element_type=jnp.float32)]
  transfers between devices with their start and end apart: 113 -> 86, of which waited for: 33 -> 34; matrix products, arithmetic and copies ran while one was open for 70% -> 47% of each run, Pallas kernels for 3% -> 7%
where the time goes in v2:
time: 1730 us; the launch traced here: 1710 us
  waiting for transfers between devices  454 us (26%)
  local copies, waits for them, and re-layouts  427 us (25%)
  matrix products  332 us (19%)
  other arithmetic  185 us (11%)
  starting transfers between devices  123 us (7%)
  Pallas kernels  118 us (7%)
  blocking collectives  59.1 us (3%)
    ppermute x58, waiting for transfers between devices, swap_bit(): return lax.ppermute(values, 'dp', [(i, i ^ bit) for i in range(data_count)])  285 us
    dot_general x6, matrix products, dot_last(): lax.dot_general(first_arg, second_arg, (((1,), (1,)), ((), ())), preferre...  116 us
    dot_general x6, matrix products, dot_first(): lax.dot_general(first_arg, second_arg, (((0,), (0,)), ((), ())), preferre...  95.5 us
    unnamed x249, local copies, waits for them, and re-layouts  75.9 us
    pallas_call x1, Pallas kernels, attend_back(): pl.pallas_call(functools.partial(attend_back_kernel, scale, rows), grid=(...  72.1 us
    all_to_all x1, waiting for transfers between devices, on_device(): early = lax.all_to_all(grad_attended[:, :tail], 'mp', 0, 0, tiled=True)  46.3 us
    dot_general x1, matrix products, on_device(): jnp.dot(grad_gateup, gate_t, preferred_element_type=jnp.float32)  46.2 us
    ppermute x58, starting transfers between devices, swap_bit(): return lax.ppermute(values, 'dp', [(i, i ^ bit) for i in range(data_count)])  43.6 us
  transfers between devices with their start and end apart: 86, of which 34 were waited for; matrix products, arithmetic and copies ran while one was open for 47% of the time, Pallas kernels for 7%

profile of v2, /device:TPU:0, one launch (start us, length us, event | category | flops | bytes accessed | tf_op | source)
XLA Modules:
  0.0 1713.3 jit_solution(5924782329347879350)
XLA Ops:
  151.3 19.8 %all-to-all-done.2 = bf16[8,3,200,320]{3,2,1,0:T(8,128)(2,1)} async-done(((bf16[8,3,200,320]{3,2,1,0:T(8,128)(2,1)}), bf16[8,3,200,320]{3,2,1,0:T(8,128)(2,1)}, u32[]{:S(2)}, u32[]{:S(2)}) %all-to-all-start.2) | async-done | bytes 3072032 | tf_op jit(solution)/shard_map/all_to_all | solution.py:659
  218.9 15.3 collective-permute-done.10
  236.7 28.6 %collective-permute-done.11 = bf16[2,128,2560]{2,1,0:T(8,128)(2,1)} collective-permute-done((bf16[2,128,2560]{2,1,0:T(8,128)(2,1)}, bf16[2,128,2560]{2,1,0:T(8,128)(2,1)}, u32[]{:S(2)}, u32[]{:S(2)}) %collective-permute-start.11) | collective-permute-done | bytes 1310752 | tf_op jit(solution)/shard_map/ppermute | solution.py:184
  311.7 43.3 %shard_map.659 = (bf16[1024,1280]{1,0:T(8,128)(2,1)}, bf16[1024,2560]{1,0:T(8,128)(2,1)}, bf16[1024,2560]{1,0:T(8,128)(2,1)}, f32[10,16,128]{2,1,0:T(8,128)}) custom-call(bf16[1024,768]{1,0:T(8,128)(2,1)} %slice.309.query_latent_ref, bf16[1024,256]{1,0:T(8,128)(2,1)} %slice.310.keyval_latent_ref, bf16[768,2560]{1,0:T(8,128)(2,1)} %bitcast.530, ...), custom_call_target="tpu_custom_call" | custom-call | flops 21474836480 | bytes 20971520 | tf_op jit(solution)/shard_map/pallas_call | solution.py:529
  355.1 14.4 collective-permute-done.15
  421.7 40.1 %collective-permute-done.17 = bf16[512,2560]{1,0:T(8,128)(2,1)} collective-permute-done((bf16[512,2560]{1,0:T(8,128)(2,1)}, bf16[512,2560]{1,0:T(8,128)(2,1)}, u32[]{:S(2)}, u32[]{:S(2)}) %collective-permute-start.17) | collective-permute-done | bytes 2621472 | tf_op jit(solution)/shard_map/ppermute | solution.py:184
  481.5 10.4 multiply_reduce_fusion
  499.6 27.5 %collective-permute-done.22 = bf16[256,2560]{1,0:T(8,128)(2,1)} collective-permute-done((bf16[256,2560]{1,0:T(8,128)(2,1)S(1)}, bf16[256,2560]{1,0:T(8,128)(2,1)}, u32[]{:S(2)}, u32[]{:S(2)}) %collective-permute-start.22) | collective-permute-done | bytes 1310752 | tf_op jit(solution)/shard_map/ppermute | solution.py:184
  531.5 23.6 %collective-permute-done.23 = bf16[256,2560]{1,0:T(8,128)(2,1)} collective-permute-done((bf16[256,2560]{1,0:T(8,128)(2,1)S(1)}, bf16[256,2560]{1,0:T(8,128)(2,1)}, u32[]{:S(2)}, u32[]{:S(2)}) %collective-permute-start.23) | collective-permute-done | bytes 1310752 | tf_op jit(solution)/shard_map/ppermute | solution.py:184
  563.1 20.6 %collective-permute-done.30 = bf16[256,2560]{1,0:T(8,128)(2,1)S(1)} collective-permute-done((bf16[256,2560]{1,0:T(8,128)(2,1)}, bf16[256,2560]{1,0:T(8,128)(2,1)S(1)}, u32[]{:S(2)}, u32[]{:S(2)}) %collective-permute-start.30) | collective-permute-done | bytes 1310752 | tf_op jit(solution)/shard_map/ppermute | solution.py:184
  598.9 54.2 %fusion.45 = f32[4096,1792]{0,1:T(8,128)} fusion(bf16[4096,2560]{1,0:T(8,128)(2,1)} %constant_dynamic-update-slice_fusion, bf16[96,2560]{1,0:T(8,128)(2,1)S(1)} %broadcast_in_dim.246, bf16[800,2560]{1,0:T(8,128)(2,1)} %bitcast.584, bf16[800,2560]{1,0:T(8,128)(2,1)} %bitcast.582), kind=kOutput, calls=%fused_computation.128 | convolution fusion | flops 37617664000 | bytes 59015168 | tf_op jit(solution)/shard_map/dot_general | solution.py:105
  677.7 34.8 %multiply_convert_fusion.2 = (bf16[4096,896]{0,1:T(8,128)(2,1)}, bf16[4096,896]{0,1:T(8,128)(2,1)}, bf16[4096,896]{0,1:T(8,128)(2,1)}) fusion(f32[4096,1792]{0,1:T(8,128)} %fusion.45, bf16[4096,2560]{1,0:T(8,128)(2,1)} %constant_dynamic-update-slice_fusion.15, bf16[800,2560]{1,0:T(8,128)(2,1)} %all-gather.13.cloned.1.call-done), kind=kOutput, calls=%fused_computation.6 | convolution fusion | flops 18845532160 | bytes 76447744 | tf_op jit(solution)/shard_map/dot_general | solution.py:105
  712.5 46.2 %convolution_convert_fusion = bf16[4096,2560]{1,0:T(8,128)(2,1)} fusion(bf16[4096,896]{0,1:T(8,128)(2,1)} %get-tuple-element.525, bf16[4096,896]{0,1:T(8,128)(2,1)} %get-tuple-element.524, bf16[96,2560]{1,0:T(8,128)(2,1)S(1)} %broadcast_in_dim.246, bf16[800,2560]{1,0:T(8,128)(2,1)} %bitcast.585, bf16[800,2560]{1,0:T(8,128)(2,1)} %bitcast.583), kind=kOutput, calls=%fused_computation | convolution fusion | flops 37657509888 | bytes 44335104 | tf_op jit(solution)/shard_map/dot_general | solution.py:836
  774.6 29.0 %collective-permute-done.44 = bf16[256,2560]{1,0:T(8,128)(2,1)S(1)} collective-permute-done((bf16[256,2560]{1,0:T(8,128)(2,1)S(1)}, bf16[256,2560]{1,0:T(8,128)(2,1)S(1)}, u32[]{:S(2)}, u32[]{:S(2)}) %collective-permute-start.44) | collective-permute-done | bytes 1310752 | tf_op jit(solution)/shard_map/ppermute | solution.py:184
  806.6 24.4 %collective-permute-done.41 = bf16[256,2560]{1,0:T(8,128)(2,1)S(1)} collective-permute-done((bf16[256,2560]{1,0:T(8,128)(2,1)S(1)}, bf16[256,2560]{1,0:T(8,128)(2,1)S(1)}, u32[]{:S(2)}, u32[]{:S(2)}) %collective-permute-start.41) | collective-permute-done | bytes 1310752 | tf_op jit(solution)/shard_map/ppermute | solution.py:184
  840.7 22.0 %fusion.156 = bf16[896,2560]{1,0:T(8,128)(2,1)S(1)} fusion(bf16[4096,896]{0,1:T(8,128)(2,1)S(1)} %bitcast.589, bf16[4096,2560]{1,0:T(8,128)(2,1)} %constant_dynamic-update-slice_fusion.15), kind=kOutput, calls=%fused_computation.384 | convolution fusion | flops 18790481920 | bytes 32899072 | tf_op jit(solution)/shard_map/dot_general | solution.py:99
  877.1 47.3 %convolution_convert_fusion.3 = bf16[1792,2560]{1,0:T(8,128)(2,1)} fusion(bf16[4096,2560]{1,0:T(8,128)(2,1)} %constant_dynamic-update-slice_fusion, bf16[4096,896]{0,1:T(8,128)(2,1)} %get-tuple-element.525, bf16[4096,896]{0,1:T(8,128)(2,1)} %get-tuple-element.524), kind=kOutput, calls=%fused_computation.11 | convolution fusion | flops 37614911488 | bytes 44826624 | tf_op jit(solution)/shard_map/dot_general | solution.py:99
  959.1 10.0 convolution_convert_fusion.6
  982.2 9.4 convolution_convert_fusion.2
  1001.9 46.3 %all-to-all-done.10 = bf16[4,64,2560]{2,1,0:T(8,128)(2,1)S(1)} async-done(((bf16[4,64,2560]{2,1,0:T(8,128)(2,1)}), bf16[4,64,2560]{2,1,0:T(8,128)(2,1)S(1)}, u32[]{:S(2)}, u32[]{:S(2)}) %all-to-all-start.10) | async-done | bytes 1310752 | tf_op jit(solution)/shard_map/all_to_all | solution.py:859
  1052.6 25.7 %convolution_convert_fusion.1 = bf16[4096,2560]{1,0:T(8,128)(2,1)S(1)} fusion(bf16[4096,896]{0,1:T(8,128)(2,1)} %get-tuple-element.132, bf16[800,2560]{1,0:T(8,128)(2,1)} %all-gather.13.cloned.1.call-done), kind=kOutput, calls=%fused_computation.1 | convolution fusion | flops 18800967680 | bytes 32407552 | tf_op jit(solution)/shard_map/dot_general | solution.py:862
  1099.2 19.6 %all-to-all-done.11 = bf16[4,64,2560]{2,1,0:T(8,128)(2,1)} async-done(((bf16[4,64,2560]{2,1,0:T(8,128)(2,1)}), bf16[4,64,2560]{2,1,0:T(8,128)(2,1)}, u32[]{:S(2)}, u32[]{:S(2)}) %all-to-all-start.11) | async-done | bytes 1310752 | tf_op jit(solution)/shard_map/all_to_all | solution.py:861
  1138.3 9.3 fusion.1
  1156.1 72.1 %shard_map.660 = (bf16[1024,2560]{1,0:T(8,128)(2,1)}, bf16[1024,2560]{1,0:T(8,128)(2,1)}, f32[1024,128]{1,0:T(8,128)}) custom-call(bf16[1024,2560]{1,0:T(8,128)(2,1)} %get-tuple-element.133.query_ref, bf16[1024,2560]{1,0:T(8,128)(2,1)} %get-tuple-element.134.keyval_ref, bf16[1024,1280]{1,0:T(8,128)(2,1)} %bitcast.540, bf16[1024,128]{1,0:T(8,128)(2,1)} %pad.31.key_ref, ...), custom_call_target="tpu_custom_call" | custom-call | flops 42949672960 | bytes 20971520 | tf_op jit(solution)/shard_map/pallas_call | solution.py:563
  1273.0 36.7 %all-to-all-done.14 = bf16[8,400,320]{2,1,0:T(8,128)(2,1)S(1)} async-done(((bf16[8,400,320]{2,1,0:T(8,128)(2,1)}), bf16[8,400,320]{2,1,0:T(8,128)(2,1)S(1)}, u32[]{:S(2)}, u32[]{:S(2)}) %all-to-all-start.14) | async-done | bytes 2048032 | tf_op jit(solution)/shard_map/all_to_all | solution.py:887
  1358.8 17.3 %add_divide_fusion.1 = (f32[320,2,1600]{2,1,0:T(2,128)}, f32[320,2,1600]{2,1,0:T(2,128)}, f32[320,2,1600]{2,1,0:T(2,128)}) fusion(f32[320,2,1600]{2,1,0:T(2,128)} %reshape.677, f32[320,2,1600]{2,1,0:T(2,128)} %param.60, f32[320,2,1600]{2,1,0:T(2,128)} %param.61), kind=kLoop, calls=%fused_computation.66 | loop fusion | flops 10240000 | bytes 24576000 | tf_op jit(solution)/shard_map/div | solution.py:121
  1433.8 9.0 fusion.21
  1507.7 26.4 %collective-permute-done.62 = bf16[256,2560]{1,0:T(8,128)(2,1)} collective-permute-done((bf16[256,2560]{1,0:T(8,128)(2,1)}, bf16[256,2560]{1,0:T(8,128)(2,1)}, u32[]{:S(2)}, u32[]{:S(2)}) %collective-permute-start.62) | collective-permute-done | bytes 1310752 | tf_op jit(solution)/shard_map/ppermute | solution.py:184
  1570.1 12.0 all-to-all-done.20
  1591.4 8.9 collective-permute-done.59
  1619.0 12.6 all-to-all-done.18
  1695.4 10.7 fusion.18
  (750 shorter events, 868.8 us)
Async XLA Ops:
  22.3 260.0 %all-gather.11.cloned.1.call-start = ((), (), s32[]{:S(2)}) async-start(), calls=%async_computation.32 | async-start | bytes 2048000 | tf_op jit(solution)/shard_map/all_gather | solution.py:667
  127.4 171.0 %all-gather.7.cloned.1.call-start = ((), (), s32[]{:S(2)}) async-start(), calls=%async_computation.27 | async-start | bytes 5120000 | tf_op jit(solution)/shard_map/all_gather | solution.py:718
  207.0 60.7 %collective-permute-start.12 = (bf16[2,128,2560]{2,1,0:T(8,128)(2,1)}, bf16[2,128,2560]{2,1,0:T(8,128)(2,1)}, u32[]{:S(2)}, u32[]{:S(2)}) collective-permute-start(bf16[2,128,2560]{2,1,0:T(8,128)(2,1)} %bitcast.34), channel_id=1, source_target_pairs={{0,24},{4,28},{8,16},{12,20},{16,8},{20,12},{24,0},{28,4},{1,25},{... | collective-permute-start | bytes 3932168 | tf_op jit(solution)/shard_map/ppermute | solution.py:184
  214.6 59.8 %all-to-all-start.3 = ((bf16[4,128,1056]{1,2,0:T(8,128)(2,1)}), bf16[4,128,1056]{1,2,0:T(8,128)(2,1)}, u32[]{:S(2)}, u32[]{:S(2)}) async-start(bf16[4,128,1056]{1,2,0:T(8,128)(2,1)} %bitcast.527), calls=%async_computation.3 | async-start | bytes 2162688 | tf_op jit(solution)/shard_map/all_to_all | solution.py:716
  218.9 164.8 %all-gather.9.cloned.1.call-start = ((), (), s32[]{:S(2)}) async-start(), calls=%async_computation.28 | async-start | bytes 5120000 | tf_op jit(solution)/shard_map/all_gather | solution.py:725
  294.9 60.1 %collective-permute-start.14 = (bf16[320,2560]{1,0:T(8,128)(2,1)}, bf16[320,2560]{1,0:T(8,128)(2,1)}, u32[]{:S(2)}, u32[]{:S(2)}) collective-permute-start(bf16[320,2560]{1,0:T(8,128)(2,1)} %bitcast.243), channel_id=1, source_target_pairs={{0,8},{4,12},{8,0},{12,4},{16,24},{20,28},{24,16},{28,20},{1,9},{5... | collective-permute-start | bytes 4915208 | tf_op jit(solution)/shard_map/ppermute | solution.py:184
  296.5 73.0 %collective-permute-start.15 = (bf16[320,2560]{1,0:T(8,128)(2,1)}, bf16[320,2560]{1,0:T(8,128)(2,1)}, u32[]{:S(2)}, u32[]{:S(2)}) collective-permute-start(bf16[320,2560]{1,0:T(8,128)(2,1)} %bitcast.243), channel_id=1, source_target_pairs={{0,16},{4,20},{8,24},{12,28},{16,0},{20,4},{24,8},{28,12},{1,17},{... | collective-permute-start | bytes 4915208 | tf_op jit(solution)/shard_map/ppermute | solution.py:184
  297.0 72.5 %collective-permute-start.16 = (bf16[320,2560]{1,0:T(8,128)(2,1)}, bf16[320,2560]{1,0:T(8,128)(2,1)}, u32[]{:S(2)}, u32[]{:S(2)}) collective-permute-start(bf16[320,2560]{1,0:T(8,128)(2,1)} %bitcast.243), channel_id=1, source_target_pairs={{0,24},{4,28},{8,16},{12,20},{16,8},{20,12},{24,0},{28,4},{1,25},{... | collective-permute-start | bytes 4915208 | tf_op jit(solution)/shard_map/ppermute | solution.py:184
  383.6 90.9 %collective-permute-start.19 = (bf16[4,320,2560]{2,1,0:T(8,128)(2,1)}, bf16[4,320,2560]{2,1,0:T(8,128)(2,1)}, u32[]{:S(2)}, u32[]{:S(2)}) collective-permute-start(bf16[4,320,2560]{2,1,0:T(8,128)(2,1)} %bitcast_dynamic-update-slice_fusion.4), channel_id=1, source_target_pairs={{0,4},{4,0},{8,12},{12,8},{16,20},{20,16},{24,28},{28,24},{1,5},{5... | collective-permute-start | bytes 19660808 | tf_op jit(solution)/shard_map/ppermute | solution.py:184
  397.9 64.6 %all-to-all-start.7 = ((bf16[4,128,2560]{1,2,0:T(8,128)(2,1)}), bf16[4,128,2560]{1,2,0:T(8,128)(2,1)}, u32[]{:S(2)}, u32[]{:S(2)}) async-start(bf16[4,128,2560]{1,2,0:T(8,128)(2,1)} %bitcast.501), calls=%async_computation.7 | async-start | bytes 5242880 | tf_op jit(solution)/shard_map/all_to_all | solution.py:780
  402.4 275.3 %all-gather.13.cloned.1.call-start = ((), (), s32[]{:S(2)}) async-start(), calls=%async_computation.33 | async-start | bytes 5120000 | tf_op jit(solution)/shard_map/all_gather | solution.py:782
  402.5 59.3 %collective-permute-start.17 = (bf16[512,2560]{1,0:T(8,128)(2,1)}, bf16[512,2560]{1,0:T(8,128)(2,1)}, u32[]{:S(2)}, u32[]{:S(2)}) collective-permute-start(bf16[512,2560]{1,0:T(8,128)(2,1)} %fusion.9), channel_id=1, source_target_pairs={{0,8},{4,12},{8,0},{12,4},{16,24},{20,28},{24,16},{28,20},{1,9},{5... | collective-permute-start | bytes 7864328 | tf_op jit(solution)/shard_map/ppermute | solution.py:184
  498.1 500.1 %reduce-scatter.6.cloned.1.call-start = ((), (), s32[]{:S(2)}) async-start(), calls=%async_computation.30 | async-start | bytes 5120000 | tf_op jit(solution)/shard_map/reduce_scatter | solution.py:842
  498.3 64.2 %collective-permute-start.26 = (bf16[256,2560]{1,0:T(8,128)(2,1)S(1)}, bf16[256,2560]{1,0:T(8,128)(2,1)S(1)}, u32[]{:S(2)}, u32[]{:S(2)}) collective-permute-start(bf16[256,2560]{1,0:T(8,128)(2,1)S(1)} %get-tuple-element.557), channel_id=1, source_target_pairs={{0,16},{4,20},{8,24},{12,28},{16,0},{20,4},{24,8},{28,12},{1,17},{... | collective-permute-start | bytes 3932168 | tf_op jit(solution)/shard_map/ppermute | solution.py:184
  597.2 61.9 %collective-permute-start.34 = (bf16[512,2560]{1,0:T(8,128)(2,1)S(1)}, bf16[512,2560]{1,0:T(8,128)(2,1)}, u32[]{:S(2)}, u32[]{:S(2)}) collective-permute-start(bf16[512,2560]{1,0:T(8,128)(2,1)S(1)} %copy-done.12), channel_id=1, source_target_pairs={{0,4},{4,0},{8,12},{12,8},{16,20},{20,16},{24,28},{28,24},{1,5},{5... | collective-permute-start | bytes 7864328 | tf_op jit(solution)/shard_map/ppermute | solution.py:184
  597.2 60.2 %collective-permute-start.37 = (bf16[512,2560]{1,0:T(8,128)(2,1)S(1)}, bf16[512,2560]{1,0:T(8,128)(2,1)S(1)}, u32[]{:S(2)}, u32[]{:S(2)}) collective-permute-start(bf16[512,2560]{1,0:T(8,128)(2,1)S(1)} %copy-done.12), channel_id=1, source_target_pairs={{0,24},{4,28},{8,16},{12,20},{16,8},{20,12},{24,0},{28,4},{1,25},{... | collective-permute-start | bytes 7864328 | tf_op jit(solution)/shard_map/ppermute | solution.py:184
  598.3 67.5 %collective-permute-start.35 = (bf16[512,2560]{1,0:T(8,128)(2,1)}, bf16[512,2560]{1,0:T(8,128)(2,1)}, u32[]{:S(2)}, u32[]{:S(2)}) collective-permute-start(bf16[512,2560]{1,0:T(8,128)(2,1)} %collective-permute-done.17), channel_id=1, source_target_pairs={{0,4},{4,0},{8,12},{12,8},{16,20},{20,16},{24,28},{28,24},{1,5},{5... | collective-permute-start | bytes 7864328 | tf_op jit(solution)/shard_map/ppermute | solution.py:184
  598.5 74.1 %collective-permute-start.36 = (bf16[512,2560]{1,0:T(8,128)(2,1)}, bf16[512,2560]{1,0:T(8,128)(2,1)S(1)}, u32[]{:S(2)}, u32[]{:S(2)}) collective-permute-start(bf16[512,2560]{1,0:T(8,128)(2,1)} %collective-permute-done.18), channel_id=1, source_target_pairs={{0,4},{4,0},{8,12},{12,8},{16,20},{20,16},{24,28},{28,24},{1,5},{5... | collective-permute-start | bytes 7864328 | tf_op jit(solution)/shard_map/ppermute | solution.py:184
  806.1 60.3 %collective-permute-start.49 = (bf16[256,2560]{1,0:T(8,128)(2,1)}, bf16[256,2560]{1,0:T(8,128)(2,1)}, u32[]{:S(2)}, u32[]{:S(2)}) collective-permute-start(bf16[256,2560]{1,0:T(8,128)(2,1)} %get-tuple-element.532), channel_id=1, source_target_pairs={{0,4},{4,0},{8,12},{12,8},{16,20},{20,16},{24,28},{28,24},{1,5},{5... | collective-permute-start | bytes 3932168 | tf_op jit(solution)/shard_map/ppermute | solution.py:184
  806.1 118.3 %collective-permute-start.46 = (bf16[256,2560]{1,0:T(8,128)(2,1)S(1)}, bf16[256,2560]{1,0:T(8,128)(2,1)}, u32[]{:S(2)}, u32[]{:S(2)}) collective-permute-start(bf16[256,2560]{1,0:T(8,128)(2,1)S(1)} %get-tuple-element.534), channel_id=1, source_target_pairs={{0,4},{4,0},{8,12},{12,8},{16,20},{20,16},{24,28},{28,24},{1,5},{5... | collective-permute-start | bytes 3932168 | tf_op jit(solution)/shard_map/ppermute | solution.py:184
  865.0 382.2 %reduce-scatter.8.cloned.1.call-start = ((), (), s32[]{:S(2)}) async-start(), calls=%async_computation.31 | async-start | bytes 10240000 | tf_op jit(solution)/shard_map/reduce_scatter | solution.py:853
  865.0 59.4 %collective-permute-start.48 = (bf16[256,2560]{1,0:T(8,128)(2,1)}, bf16[256,2560]{1,0:T(8,128)(2,1)}, u32[]{:S(2)}, u32[]{:S(2)}) collective-permute-start(bf16[256,2560]{1,0:T(8,128)(2,1)} %get-tuple-element.529), channel_id=1, source_target_pairs={{0,16},{4,20},{8,24},{12,28},{16,0},{20,4},{24,8},{28,12},{1,17},{... | collective-permute-start | bytes 3932168 | tf_op jit(solution)/shard_map/ppermute | solution.py:184
  976.8 71.4 %all-to-all-start.10 = ((bf16[4,64,2560]{2,1,0:T(8,128)(2,1)}), bf16[4,64,2560]{2,1,0:T(8,128)(2,1)S(1)}, u32[]{:S(2)}, u32[]{:S(2)}) async-start(bf16[4,64,2560]{2,1,0:T(8,128)(2,1)} %get-tuple-element.554), calls=%async_computation.10 | async-start | bytes 2621440 | tf_op jit(solution)/shard_map/all_to_all | solution.py:859
  998.3 140.0 %collective-permute-start.53 = (bf16[4,320,2560]{2,1,0:T(8,128)(2,1)}, bf16[4,320,2560]{2,1,0:T(8,128)(2,1)}, u32[]{:S(2)}, u32[]{:S(2)}) collective-permute-start(bf16[4,320,2560]{2,1,0:T(8,128)(2,1)} %dynamic-slice_bitcast_fusion), channel_id=1, source_target_pairs={{0,4},{4,0},{8,12},{12,8},{16,20},{20,16},{24,28},{28,24},{1,5},{5... | collective-permute-start | bytes 19660808 | tf_op jit(solution)/shard_map/ppermute | solution.py:184
  1048.2 70.6 %all-to-all-start.11 = ((bf16[4,64,2560]{2,1,0:T(8,128)(2,1)}), bf16[4,64,2560]{2,1,0:T(8,128)(2,1)}, u32[]{:S(2)}, u32[]{:S(2)}) async-start(bf16[4,64,2560]{2,1,0:T(8,128)(2,1)} %get-tuple-element.136), calls=%async_computation.12 | async-start | bytes 2621440 | tf_op jit(solution)/shard_map/all_to_all | solution.py:861
  1052.5 642.8 %reduce-scatter.4.cloned.1.call-start = ((), (), s32[]{:S(2)}) async-start(), calls=%async_computation.29 | async-start | bytes 23592960 | tf_op jit(solution)/shard_map/reduce_scatter | solution.py:863
  1131.0 121.9 %all-to-all-start.13 = ((bf16[8,200,320]{2,1,0:T(8,128)(2,1)}), bf16[8,200,320]{2,1,0:T(8,128)(2,1)}, u32[]{:S(2)}, u32[]{:S(2)}) async-start(bf16[8,200,320]{2,1,0:T(8,128)(2,1)} %copy.782), calls=%async_computation.15 | async-start | bytes 2457600 | tf_op jit(solution)/shard_map/all_to_all | solution.py:885
  1152.6 115.0 %collective-permute-start.54 = (bf16[320,2560]{1,0:T(8,128)(2,1)}, bf16[320,2560]{1,0:T(8,128)(2,1)}, u32[]{:S(2)}, u32[]{:S(2)}) collective-permute-start(bf16[320,2560]{1,0:T(8,128)(2,1)} %get-tuple-element.540), channel_id=1, source_target_pairs={{0,8},{4,12},{8,0},{12,4},{16,24},{20,28},{24,16},{28,20},{1,9},{5... | collective-permute-start | bytes 4915208 | tf_op jit(solution)/shard_map/ppermute | solution.py:184
  1154.5 113.1 %collective-permute-start.55 = (bf16[320,2560]{1,0:T(8,128)(2,1)}, bf16[320,2560]{1,0:T(8,128)(2,1)}, u32[]{:S(2)}, u32[]{:S(2)}) collective-permute-start(bf16[320,2560]{1,0:T(8,128)(2,1)} %get-tuple-element.542), channel_id=1, source_target_pairs={{0,16},{4,20},{8,24},{12,28},{16,0},{20,4},{24,8},{28,12},{1,17},{... | collective-permute-start | bytes 4915208 | tf_op jit(solution)/shard_map/ppermute | solution.py:184
  1156.0 111.7 %collective-permute-start.56 = (bf16[320,2560]{1,0:T(8,128)(2,1)}, bf16[320,2560]{1,0:T(8,128)(2,1)}, u32[]{:S(2)}, u32[]{:S(2)}) collective-permute-start(bf16[320,2560]{1,0:T(8,128)(2,1)} %get-tuple-element.541), channel_id=1, source_target_pairs={{0,24},{4,28},{8,16},{12,20},{16,8},{20,12},{24,0},{28,4},{1,25},{... | collective-permute-start | bytes 4915208 | tf_op jit(solution)/shard_map/ppermute | solution.py:184
  1329.7 84.5 %all-to-all-start.16 = ((bf16[4,128,1056]{1,2,0:T(8,128)(2,1)}), bf16[4,128,1056]{1,2,0:T(8,128)(2,1)}, u32[]{:S(2)}, u32[]{:S(2)}) async-start(bf16[4,128,1056]{1,2,0:T(8,128)(2,1)} %copy.787), calls=%async_computation.19 | async-start | bytes 2162688 | tf_op jit(solution)/shard_map/all_to_all | solution.py:911
  1495.1 65.1 %collective-permute-start.57 = (bf16[4,320,1056]{2,1,0:T(8,128)(2,1)}, bf16[4,320,1056]{2,1,0:T(8,128)(2,1)}, u32[]{:S(2)}, u32[]{:S(2)}) collective-permute-start(bf16[4,320,1056]{2,1,0:T(8,128)(2,1)} %dynamic-slice_bitcast_fusion.1), channel_id=1, source_target_pairs={{0,4},{4,0},{8,12},{12,8},{16,20},{20,16},{24,28},{28,24},{1,5},{5... | collective-permute-start | bytes 8110088 | tf_op jit(solution)/shard_map/ppermute | solution.py:184
  (152 other events, 3661.1 us)
Sparse Core Ops, SparseCore 0:
  25.3 37.5 all-gather.10
  186.3 99.6 all-gather.6
  288.1 77.5 all-gather.8
  498.3 79.4 all-gather.12
  865.1 75.6 reduce-scatter.5
  946.6 191.3 reduce-scatter.7
  1141.6 206.9 reduce-scatter.3

commit v3 on v2

--- a/solution.py
+++ b/solution.py
@@ -213,23 +213,46 @@
     return (first_arg.astype(jnp.float32) + second_arg.astype(jnp.float32)).astype(jnp.bfloat16)
 
 
-def scatter_tokens(pieces, group_size, data_count, near_count):
+def scatter_tokens(pieces, group_size, data_count, near_count, fillers):
     bits = bits_of(group_size, data_count)
-    halves = []
+    fillers = list(fillers)
+    held = [{}, {}]
+    far = range(0, data_count, group_size)
+    sent = {
+        (index, half, near): swap_bit(pieces[(index ^ near, half)], near, data_count)
+        for half in range(2)
+        for index in far
+        for near in range(1, near_count)
+    }
+    keys = sorted(sent)
+    fillers[0], *arrived = tie(fillers[0], *[sent[key] for key in keys])
+    sent = dict(zip(keys, arrived))
     for half in range(2):
-        held = {}
-        for index in range(0, data_count, group_size):
+        for index in far:
             total = pieces[(index, half)]
             for near in range(1, near_count):
-                total = add_low(total, swap_bit(pieces[(index ^ near, half)], near, data_count))
-            held[index] = total
-        for bit in bits if half == 0 else bits[::-1]:
-            for index in sorted(held):
+                total = add_low(total, sent[(index, half, near)])
+            held[half][index] = total
+    for step in range(len(bits)):
+        sent = {}
+        for half in range(2):
+            bit = bits[step] if half == 0 else bits[::-1][step]
+            for index in held[half]:
                 if not index & bit:
-                    held[index] = add_low(held[index], swap_bit(held[index ^ bit], bit, data_count))
-            held = {index: held[index] for index in held if not index & bit}
-        halves.append(held[0])
-    return jnp.concatenate(halves, axis=0)
+                    sent[(index, half)] = swap_bit(held[half][index ^ bit], bit, data_count)
+        keys = sorted(sent)
+        if step + 1 < len(fillers):
+            fillers[step + 1], *arrived = tie(fillers[step + 1], *[sent[key] for key in keys])
+            sent = dict(zip(keys, arrived))
+        held = [
+            {
+                index: add_low(held[half][index], sent[(index, half)])
+                for index in held[half]
+                if (index, half) in sent
+            }
+            for half in range(2)
+        ]
+    return jnp.concatenate([held[half][0] for half in range(2)], axis=0), fillers
 
 
 def spread_planes(values, model_count, model_index):
@@ -684,14 +707,14 @@
         ],
         axis=1,
     )
-    units, gain_all = tie(units, gain_all)
     units = exchange_units(units)
     lat_w = far_parts(row_major(columns(lat_w)), group, data_count)
-    both_w, *lat_w = tie(both_w, *lat_w)
+    both_w, *lat_w = tie(columns(both_w), *lat_w)
+    both_w = both_w.reshape(query_rows + keyval_rows, group, -1)
+    both_w = lax.all_to_all(both_w, "dp", 1, 0, axis_index_groups=near)
+    both_w, units = tie(row_major(both_w), units)
+    both_parts = far_parts(both_w, group, data_count)
     lat_w = rows_of(lat_w, group, data_count, data_index)
-    both_w = columns(both_w).reshape(query_rows + keyval_rows, group, -1)
-    both_w = lax.all_to_all(both_w, "dp", 1, 0, axis_index_groups=near)
-    both_w = in_order(far_parts(row_major(both_w), group, data_count), data_index // group)
     gain_all = gain_all.reshape(-1).astype(jnp.float32)
     gain_one = gain_all[:WIDTH]
     gain_two = gain_all[WIDTH : 2 * WIDTH]
@@ -710,10 +733,10 @@
     keyval_normed, inverse_keyval = rms_parts(keyval_raw, gain_keyval)
     sent = jnp.concatenate([query_normed, keyval_normed, key_rope], axis=1).astype(bf16)
 
-    mid, units = tie(
-        near_parts(sent.reshape(micro, share, latent_all), group, near), units
-    )
+    mid = near_parts(sent.reshape(micro, share, latent_all), group, near)
     mid = lax.all_to_all(mid, "mp", 0, 0, tiled=True)
+    mid, *both_parts = tie(mid, *both_parts)
+    both_w = in_order(both_parts, data_index // group)
     units = jnp.transpose(units, (1, 2, 0, 3)).reshape(3, unit_count, WIDTH)
     gate_first = lax.all_gather(units[0], "mp", axis=0)
     gate_pad = jnp.zeros((padded - hidden_units, WIDTH), bf16)
@@ -797,11 +820,11 @@
         pieces = gather_tokens(values, group, data_count)
         return jnp.concatenate([pieces[key] for keys in order for key in keys], axis=0)
 
-    def parted(values):
+    def parted(values, fillers):
         pieces = {}
         for at, key in enumerate([key for keys in order for key in keys]):
             pieces[key] = values[at * half_rows : (at + 1) * half_rows]
-        return scatter_tokens(pieces, group, data_count, group).astype(jnp.float32)
+        return scatter_tokens(pieces, group, data_count, group, fillers)
 
     down_t = jnp.concatenate([down_t, gate_pad], axis=0)
     normed_full, *mixed_parts = tie(joined(normed_two), *mixed_parts)
@@ -832,11 +855,14 @@
     grad_gate = grad_act * up_part * sigmoid_gate * (1.0 + gate_part * (1.0 - sigmoid_gate))
     grad_up = grad_act * silu_gate
     grad_gateup = jnp.concatenate([grad_gate, grad_up], axis=1).astype(bf16)
-    grad_normed_two = parted(
-        jnp.dot(grad_gateup, gate_t, preferred_element_type=jnp.float32).astype(bf16)
-    )
-    grad_down_t = dot_first(activated, mixed_full).astype(bf16)
-    grad_gate_t = dot_first(grad_gateup, normed_full).astype(bf16)
+    grad_normed_two, (grad_down_t, grad_gate_t) = parted(
+        jnp.dot(grad_gateup, gate_t, preferred_element_type=jnp.float32).astype(bf16),
+        [
+            dot_first(activated, mixed_full).astype(bf16),
+            dot_first(grad_gateup, normed_full).astype(bf16),
+        ],
+    )
+    grad_normed_two = grad_normed_two.astype(jnp.float32)
     grad_down_t = grad_down_t[:hidden_units]
 
     down_sum = lax.psum_scatter(
@@ -845,7 +871,7 @@
 
     grad_hidden = grad_out + rms_back(hidden, inverse_two, gain_two, grad_normed_two)
     grad_gain_two = jnp.sum(grad_normed_two * hidden * inverse_two, axis=0)
-    grad_branch, grad_gate_t = tie((RESIDUAL * grad_hidden).astype(bf16), grad_gate_t)
+    grad_branch = (RESIDUAL * grad_hidden).astype(bf16)
     gate_sum = grad_gate_t.reshape(2, padded, WIDTH)[:, :hidden_units]
     gate_sum = jnp.transpose(
         gate_sum.reshape(2, model_count, unit_count, WIDTH), (1, 0, 2, 3)
@@ -857,20 +883,21 @@
     )
     tail = grad_attended.shape[1] // 2
     early = lax.all_to_all(grad_attended[:, :tail], "mp", 0, 0, tiled=True)
-    late, early, activated = tie(grad_attended[:, tail:], early, activated)
-    late = lax.all_to_all(late, "mp", 0, 0, tiled=True)
-    mixed_out = jnp.dot(activated, down_t, preferred_element_type=jnp.float32).astype(bf16)
-    mixed_out = lax.psum_scatter(
-        in_order(list(mixed_out.reshape(data_count, -1, WIDTH)), data_index),
-        "dp",
-        scatter_dimension=0,
-        tiled=True,
-    ).reshape(hidden.shape)
     project_sum = near_sum(
         dot_first(grad_branch, attended_own), group, data_count, data_index
     )
+    activated = in_order(list(activated.reshape(data_count, -1, padded)), data_index)
+    late, early, activated, project_sum = tie(
+        grad_attended[:, tail:], early, activated, project_sum
+    )
+    late = lax.all_to_all(late, "mp", 0, 0, tiled=True)
+    mixed_out = jnp.dot(
+        activated.reshape(-1, padded), down_t, preferred_element_type=jnp.float32
+    ).astype(bf16)
+    mixed_out = lax.psum_scatter(
+        mixed_out.reshape(data_count, -1, WIDTH), "dp", scatter_dimension=0, tiled=True
+    ).reshape(hidden.shape)
     grad_attended = heads_in(jnp.concatenate([early, late], axis=1))
-    grad_attended, project_sum = tie(grad_attended, project_sum)
     project_sum = far_sum(project_sum, group, data_count, data_index)
     grad_query_all, grad_keyval, grad_shared = attend_back(
         queries, keyval, grad_attended, key_lanes, bias, tables, scale_attn, rows_attn
@@ -883,16 +910,8 @@
     ).astype(bf16)
     down_sum = jnp.transpose(down_sum.reshape(unit_count, data_count, -1), (1, 0, 2))
     down_sum = lax.all_to_all(down_sum, "dp", 0, 0, tiled=True)
-    gate_sum = jnp.transpose(gate_sum.reshape(2 * unit_count, data_count, -1), (1, 0, 2))
-    gate_sum = lax.all_to_all(gate_sum, "dp", 0, 0, tiled=True)
-    latent_terms, project_sum, down_sum, gate_sum = tie(
-        latent_terms, project_sum, down_sum, gate_sum
-    )
+    latent_terms, project_sum, down_sum = tie(latent_terms, project_sum, down_sum)
     down_sum = jnp.transpose(down_sum, (2, 0, 1)).reshape(down_weight.shape)
-    gate_sum = jnp.transpose(
-        gate_sum.reshape(data_count, 2, unit_count, -1), (3, 1, 0, 2)
-    ).reshape(gateup_weight.shape)
-
     layer_out = (hidden + RESIDUAL * mixed_out).astype(bf16)
     parts = latent_terms.reshape(model_count, group, share // group, latent_all)
     parts = lax.all_to_all(parts, "dp", 1, 0, axis_index_groups=near)
@@ -908,7 +927,16 @@
         ],
         axis=2,
     )
-    parts, grad_both = tie(lax.all_to_all(parts, "mp", 0, 0, tiled=True), grad_both)
+    gate_sum = jnp.transpose(gate_sum.reshape(2 * unit_count, data_count, -1), (1, 0, 2))
+    parts, grad_both, gate_sum = tie(
+        lax.all_to_all(parts, "mp", 0, 0, tiled=True), grad_both, gate_sum
+    )
+    gate_sum = lax.all_to_all(gate_sum, "dp", 0, 0, tiled=True)
+    project_sum, gate_sum = tie(project_sum, gate_sum)
+    gate_sum = jnp.transpose(
+        gate_sum.reshape(data_count, 2, unit_count, -1), (3, 1, 0, 2)
+    ).reshape(gateup_weight.shape)
+
     grad_both = far_sum(
         grad_both.reshape(data_count // group, group * (query_rows + keyval_rows), -1),
         group,

time: 1730 us -> 1660 us (0.960)
  local copies, waits for them, and re-layouts: 427 us -> 386 us
  other arithmetic: 185 us -> 164 us
    ppermute x58, waiting for transfers between devices: 285 us -> 319 us  [swap_bit(): return lax.ppermute(values, 'dp', [(i, i ^ bit) for i in range(data_count)])]
    all_to_all x1, waiting for transfers between devices: 19.6 us -> 0.01 us  [on_device(): late = lax.all_to_all(late, 'mp', 0, 0, tiled=True)]
    unnamed x249 -> x284, local copies, waits for them, and re-layouts: 75.9 us -> 66.2 us
  transfers between devices with their start and end apart: 86 -> 86, of which waited for: 34 -> 31; matrix products, arithmetic and copies ran while one was open for 47% -> 46% of each run, Pallas kernels for 7% -> 7%
where the time goes in v3:
time: 1660 us; the launch traced here: 1650 us
  waiting for transfers between devices  451 us (27%)
  local copies, waits for them, and re-layouts  386 us (23%)
  matrix products  332 us (20%)
  other arithmetic  164 us (10%)
  starting transfers between devices  122 us (7%)
  Pallas kernels  116 us (7%)
  blocking collectives  56.5 us (3%)
  between operations  17.6 us (1%)
    ppermute x58, waiting for transfers between devices, swap_bit(): return lax.ppermute(values, 'dp', [(i, i ^ bit) for i in range(data_count)])  319 us
    dot_general x6, matrix products, dot_last(): lax.dot_general(first_arg, second_arg, (((1,), (1,)), ((), ())), preferre...  119 us
    dot_general x6, matrix products, dot_first(): lax.dot_general(first_arg, second_arg, (((0,), (0,)), ((), ())), preferre...  92.9 us
    pallas_call x1, Pallas kernels, attend_back(): pl.pallas_call(functools.partial(attend_back_kernel, scale, rows), grid=(...  70.5 us
    unnamed x284, local copies, waits for them, and re-layouts  66.2 us
    dot_general x1, matrix products, on_device(): jnp.dot(grad_gateup, gate_t, preferred_element_type=jnp.float32)  45.3 us
    ppermute x58, starting transfers between devices, swap_bit(): return lax.ppermute(values, 'dp', [(i, i ^ bit) for i in range(data_count)])  44.2 us
    all_to_all x1, waiting for transfers between devices, on_device(): early = lax.all_to_all(grad_attended[:, :tail], 'mp', 0, 0, tiled=True)  43.9 us
  transfers between devices with their start and end apart: 86, of which 31 were waited for; matrix products, arithmetic and copies ran while one was open for 46% of the time, Pallas kernels for 7%

profile of v3, /device:TPU:0, one launch (start us, length us, event | category | flops | bytes accessed | tf_op | source)
XLA Modules:
  0.0 1645.3 jit_solution(1820366014003397666)
XLA Ops:
  94.7 9.4 collective-permute-done.4
  110.4 8.8 collective-permute-done.7
  142.9 33.7 %all-to-all-done.1 = bf16[8,3,200,320]{3,2,1,0:T(8,128)(2,1)} async-done(((bf16[8,3,200,320]{3,2,1,0:T(8,128)(2,1)}), bf16[8,3,200,320]{3,2,1,0:T(8,128)(2,1)}, u32[]{:S(2)}, u32[]{:S(2)}) %all-to-all-start.1) | async-done | bytes 3072032 | tf_op jit(solution)/shard_map/all_to_all | solution.py:682
  234.7 15.5 collective-permute-done.10
  250.2 27.4 %collective-permute-done.11 = bf16[2,128,2560]{2,1,0:T(8,128)(2,1)} collective-permute-done((bf16[2,128,2560]{2,1,0:T(8,128)(2,1)}, bf16[2,128,2560]{2,1,0:T(8,128)(2,1)}, u32[]{:S(2)}, u32[]{:S(2)}) %collective-permute-start.11) | collective-permute-done | bytes 1310752 | tf_op jit(solution)/shard_map/ppermute | solution.py:184
  323.5 43.2 %shard_map.659 = (bf16[1024,1280]{1,0:T(8,128)(2,1)}, bf16[1024,2560]{1,0:T(8,128)(2,1)}, bf16[1024,2560]{1,0:T(8,128)(2,1)}, f32[10,16,128]{2,1,0:T(8,128)}) custom-call(bf16[1024,768]{1,0:T(8,128)(2,1)} %slice.309.query_latent_ref, bf16[1024,256]{1,0:T(8,128)(2,1)} %slice.310.keyval_latent_ref, bf16[768,2560]{1,0:T(8,128)(2,1)} %bitcast.529, ...), custom_call_target="tpu_custom_call" | custom-call | flops 21474836480 | bytes 20971520 | tf_op jit(solution)/shard_map/pallas_call | solution.py:552
  366.7 14.9 collective-permute-done.15
  434.1 40.0 %collective-permute-done.17 = bf16[512,2560]{1,0:T(8,128)(2,1)} collective-permute-done((bf16[512,2560]{1,0:T(8,128)(2,1)}, bf16[512,2560]{1,0:T(8,128)(2,1)}, u32[]{:S(2)}, u32[]{:S(2)}) %collective-permute-start.17) | collective-permute-done | bytes 2621472 | tf_op jit(solution)/shard_map/ppermute | solution.py:184
  493.2 10.4 multiply_reduce_fusion
  511.5 27.5 %collective-permute-done.22 = bf16[256,2560]{1,0:T(8,128)(2,1)} collective-permute-done((bf16[256,2560]{1,0:T(8,128)(2,1)S(1)}, bf16[256,2560]{1,0:T(8,128)(2,1)}, u32[]{:S(2)}, u32[]{:S(2)}) %collective-permute-start.22) | collective-permute-done | bytes 1310752 | tf_op jit(solution)/shard_map/ppermute | solution.py:184
  543.4 23.6 %collective-permute-done.23 = bf16[256,2560]{1,0:T(8,128)(2,1)} collective-permute-done((bf16[256,2560]{1,0:T(8,128)(2,1)S(1)}, bf16[256,2560]{1,0:T(8,128)(2,1)}, u32[]{:S(2)}, u32[]{:S(2)}) %collective-permute-start.23) | collective-permute-done | bytes 1310752 | tf_op jit(solution)/shard_map/ppermute | solution.py:184
  575.1 20.7 %collective-permute-done.30 = bf16[256,2560]{1,0:T(8,128)(2,1)S(1)} collective-permute-done((bf16[256,2560]{1,0:T(8,128)(2,1)}, bf16[256,2560]{1,0:T(8,128)(2,1)S(1)}, u32[]{:S(2)}, u32[]{:S(2)}) %collective-permute-start.30) | collective-permute-done | bytes 1310752 | tf_op jit(solution)/shard_map/ppermute | solution.py:184
  611.0 51.2 %fusion.37 = f32[4096,1792]{1,0:T(8,128)} fusion(bf16[4096,2560]{1,0:T(8,128)(2,1)} %constant_dynamic-update-slice_fusion, bf16[96,2560]{1,0:T(8,128)(2,1)S(1)} %broadcast_in_dim.245, bf16[800,2560]{1,0:T(8,128)(2,1)} %bitcast.584, bf16[800,2560]{1,0:T(8,128)(2,1)} %bitcast.582), kind=kOutput, calls=%fused_computation.112 | convolution fusion | flops 37617664000 | bytes 59015168 | tf_op jit(solution)/shard_map/dot_general | solution.py:105
  689.8 36.4 %multiply_convert_fusion.2 = (bf16[4096,896]{1,0:T(8,128)(2,1)}, bf16[4096,896]{1,0:T(8,128)(2,1)}, bf16[4096,896]{1,0:T(8,128)(2,1)}) fusion(f32[4096,1792]{1,0:T(8,128)} %fusion.37, bf16[4096,2560]{1,0:T(8,128)(2,1)} %constant_dynamic-update-slice_fusion.15, bf16[800,2560]{1,0:T(8,128)(2,1)} %all-gather.13.cloned.1.call-done), kind=kOutput, calls=%fused_computation.6 | convolution fusion | flops 18845532160 | bytes 76447744 | tf_op jit(solution)/shard_map/dot_general | solution.py:105
  726.3 45.3 %convolution_convert_fusion = bf16[4096,2560]{1,0:T(8,128)(2,1)} fusion(bf16[4096,896]{1,0:T(8,128)(2,1)} %get-tuple-element.557, bf16[4096,896]{1,0:T(8,128)(2,1)} %get-tuple-element.556, bf16[96,2560]{1,0:T(8,128)(2,1)S(1)} %broadcast_in_dim.245, bf16[800,2560]{1,0:T(8,128)(2,1)} %bitcast.585, bf16[800,2560]{1,0:T(8,128)(2,1)} %bitcast.583), kind=kOutput, calls=%fused_computation | convolution fusion | flops 37657509888 | bytes 44335104 | tf_op jit(solution)/shard_map/dot_general | solution.py:859
  783.5 22.1 %convolution_convert_fusion.5 = bf16[896,2560]{1,0:T(8,128)(2,1)S(1)} fusion(bf16[4096,896]{1,0:T(8,128)(2,1)S(1)} %copy-done.14, bf16[4096,2560]{1,0:T(8,128)(2,1)} %constant_dynamic-update-slice_fusion.15), kind=kOutput, calls=%fused_computation.27 | convolution fusion | flops 18792775680 | bytes 32899072 | tf_op jit(solution)/shard_map/dot_general | solution.py:99
  818.4 48.0 %convolution_convert_fusion.3 = bf16[1792,2560]{1,0:T(8,128)(2,1)} fusion(bf16[4096,2560]{1,0:T(8,128)(2,1)} %constant_dynamic-update-slice_fusion, bf16[4096,896]{1,0:T(8,128)(2,1)} %get-tuple-element.557, bf16[4096,896]{1,0:T(8,128)(2,1)} %get-tuple-element.556), kind=kOutput, calls=%fused_computation.11 | convolution fusion | flops 37614911488 | bytes 44826624 | tf_op jit(solution)/shard_map/dot_general | solution.py:99
  874.5 28.7 %collective-permute-done.51 = bf16[256,2560]{1,0:T(8,128)(2,1)S(1)} collective-permute-done((bf16[256,2560]{1,0:T(8,128)(2,1)S(1)}, bf16[256,2560]{1,0:T(8,128)(2,1)S(1)}, u32[]{:S(2)}, u32[]{:S(2)}) %collective-permute-start.51) | collective-permute-done | bytes 1310752 | tf_op jit(solution)/shard_map/ppermute | solution.py:184
  917.6 19.9 %collective-permute-done.52 = bf16[256,2560]{1,0:T(8,128)(2,1)} collective-permute-done((bf16[256,2560]{1,0:T(8,128)(2,1)}, bf16[256,2560]{1,0:T(8,128)(2,1)}, u32[]{:S(2)}, u32[]{:S(2)}) %collective-permute-start.52) | collective-permute-done | bytes 1310752 | tf_op jit(solution)/shard_map/ppermute | solution.py:184
  949.6 10.9 convolution_convert_fusion.2
  984.5 12.7 convolution_convert_fusion.7
  1022.0 9.3 fusion.1
  1031.3 43.9 %all-to-all-done.10 = bf16[4,64,2560]{2,1,0:T(8,128)(2,1)S(1)} async-done(((bf16[4,64,2560]{2,1,0:T(8,128)(2,1)}), bf16[4,64,2560]{2,1,0:T(8,128)(2,1)S(1)}, u32[]{:S(2)}, u32[]{:S(2)}) %all-to-all-start.10) | async-done | bytes 1310752 | tf_op jit(solution)/shard_map/all_to_all | solution.py:885
  1087.8 27.9 %convolution_convert_fusion.1 = bf16[4096,2560]{1,0:T(8,128)(2,1)} fusion(bf16[4096,896]{1,0:T(8,128)(2,1)} %bitcast.510, bf16[800,2560]{1,0:T(8,128)(2,1)S(1)} %copy-done.105), kind=kOutput, calls=%fused_computation.1 | convolution fusion | flops 18800967680 | bytes 32407552 | tf_op jit(solution)/shard_map/dot_general | solution.py:894
  1123.3 35.7 %collective-permute-done.55 = bf16[320,2560]{1,0:T(8,128)(2,1)} collective-permute-done((bf16[320,2560]{1,0:T(8,128)(2,1)}, bf16[320,2560]{1,0:T(8,128)(2,1)}, u32[]{:S(2)}, u32[]{:S(2)}) %collective-permute-start.55) | collective-permute-done | bytes 1638432 | tf_op jit(solution)/shard_map/ppermute | solution.py:184
  1182.8 70.5 %shard_map.660 = (bf16[1024,2560]{1,0:T(8,128)(2,1)}, bf16[1024,2560]{1,0:T(8,128)(2,1)}, f32[1024,128]{1,0:T(8,128)}) custom-call(bf16[1024,2560]{1,0:T(8,128)(2,1)} %get-tuple-element.163.query_ref, bf16[1024,2560]{1,0:T(8,128)(2,1)} %get-tuple-element.164.keyval_ref, bf16[1024,1280]{1,0:T(8,128)(2,1)} %bitcast.538, bf16[1024,128]{1,0:T(8,128)(2,1)} %pad.31.key_ref, ...), custom_call_target="tpu_custom_call" | custom-call | flops 42949672960 | bytes 20971520 | tf_op jit(solution)/shard_map/pallas_call | solution.py:586
  1359.0 9.0 fusion.21
  1372.3 22.0 %collective-permute-done.62 = bf16[256,2560]{1,0:T(8,128)(2,1)} collective-permute-done((bf16[256,2560]{1,0:T(8,128)(2,1)}, bf16[256,2560]{1,0:T(8,128)(2,1)}, u32[]{:S(2)}, u32[]{:S(2)}) %collective-permute-start.62) | collective-permute-done | bytes 1310752 | tf_op jit(solution)/shard_map/ppermute | solution.py:184
  1421.0 20.8 %all-to-all-done.20 = bf16[8,400,320]{2,1,0:T(8,128)(2,1)} async-done(((bf16[8,400,320]{2,1,0:T(8,128)(2,1)}), bf16[8,400,320]{2,1,0:T(8,128)(2,1)}, u32[]{:S(2)}, u32[]{:S(2)}) %all-to-all-start.20) | async-done | bytes 2048032 | tf_op jit(solution)/shard_map/all_to_all | solution.py:934
  1467.5 17.3 %add_divide_fusion.1 = (f32[320,2,1600]{2,1,0:T(2,128)}, f32[320,2,1600]{2,1,0:T(2,128)}, f32[320,2,1600]{2,1,0:T(2,128)}) fusion(f32[320,2,1600]{2,1,0:T(2,128)} %reshape.690, f32[320,2,1600]{2,1,0:T(2,128)} %param.60, f32[320,2,1600]{2,1,0:T(2,128)} %param.61), kind=kLoop, calls=%fused_computation.66 | loop fusion | flops 10240000 | bytes 24576000 | tf_op jit(solution)/shard_map/div | solution.py:121
  1511.4 8.9 fusion.137
  1582.4 10.3 all-to-all-done.17
  (785 shorter events, 801.6 us)
Async XLA Ops:
  9.3 60.6 %collective-permute-start = (bf16[320,264]{1,0:T(8,128)(2,1)}, bf16[320,264]{1,0:T(8,128)(2,1)}, u32[]{:S(2)}, u32[]{:S(2)}) collective-permute-start(bf16[320,264]{1,0:T(8,128)(2,1)} %copy.769), channel_id=1, source_target_pairs={{0,1},{1,2},{2,3},{3,0},{4,5},{5,6},{6,7},{7,4},{8,9},{9,10},{10,1... | collective-permute-start | bytes 506888 | tf_op jit(solution)/shard_map/ppermute | solution.py:263
  12.3 59.3 %collective-permute-start.1 = (bf16[320,264]{1,0:T(8,128)(2,1)}, bf16[320,264]{1,0:T(8,128)(2,1)}, u32[]{:S(2)}, u32[]{:S(2)}) collective-permute-start(bf16[320,264]{1,0:T(8,128)(2,1)} %copy.769), channel_id=1, source_target_pairs={{0,2},{1,3},{2,0},{3,1},{4,6},{5,7},{6,4},{7,5},{8,10},{9,11},{10,... | collective-permute-start | bytes 506888 | tf_op jit(solution)/shard_map/ppermute | solution.py:263
  14.9 58.5 %collective-permute-start.2 = (bf16[320,264]{1,0:T(8,128)(2,1)}, bf16[320,264]{1,0:T(8,128)(2,1)}, u32[]{:S(2)}, u32[]{:S(2)}) collective-permute-start(bf16[320,264]{1,0:T(8,128)(2,1)} %copy.769), channel_id=1, source_target_pairs={{0,3},{1,0},{2,1},{3,2},{4,7},{5,4},{6,5},{7,6},{8,11},{9,8},{10,9... | collective-permute-start | bytes 506888 | tf_op jit(solution)/shard_map/ppermute | solution.py:263
  22.5 274.5 %all-gather.11.cloned.1.call-start = ((), (), s32[]{:S(2)}) async-start(), calls=%async_computation.32 | async-start | bytes 2048000 | tf_op jit(solution)/shard_map/all_gather | solution.py:690
  132.9 177.2 %all-gather.7.cloned.1.call-start = ((), (), s32[]{:S(2)}) async-start(), calls=%async_computation.27 | async-start | bytes 5120000 | tf_op jit(solution)/shard_map/all_gather | solution.py:741
  213.6 64.0 %all-to-all-start.4 = ((bf16[4,128,1056]{1,2,0:T(8,128)(2,1)}), bf16[4,128,1056]{1,2,0:T(8,128)(2,1)}, u32[]{:S(2)}, u32[]{:S(2)}) async-start(bf16[4,128,1056]{1,2,0:T(8,128)(2,1)} %bitcast.525), calls=%async_computation.4 | async-start | bytes 2162688 | tf_op jit(solution)/shard_map/all_to_all | solution.py:737
  217.9 177.8 %all-gather.9.cloned.1.call-start = ((), (), s32[]{:S(2)}) async-start(), calls=%async_computation.28 | async-start | bytes 5120000 | tf_op jit(solution)/shard_map/all_gather | solution.py:748
  218.5 59.1 %collective-permute-start.11 = (bf16[2,128,2560]{2,1,0:T(8,128)(2,1)}, bf16[2,128,2560]{2,1,0:T(8,128)(2,1)}, u32[]{:S(2)}, u32[]{:S(2)}) collective-permute-start(bf16[2,128,2560]{2,1,0:T(8,128)(2,1)} %bitcast.517), channel_id=1, source_target_pairs={{0,16},{4,20},{8,24},{12,28},{16,0},{20,4},{24,8},{28,12},{1,17},{... | collective-permute-start | bytes 3932168 | tf_op jit(solution)/shard_map/ppermute | solution.py:184
  218.9 58.7 %collective-permute-start.12 = (bf16[2,128,2560]{2,1,0:T(8,128)(2,1)}, bf16[2,128,2560]{2,1,0:T(8,128)(2,1)}, u32[]{:S(2)}, u32[]{:S(2)}) collective-permute-start(bf16[2,128,2560]{2,1,0:T(8,128)(2,1)} %bitcast.518), channel_id=1, source_target_pairs={{0,24},{4,28},{8,16},{12,20},{16,8},{20,12},{24,0},{28,4},{1,25},{... | collective-permute-start | bytes 3932168 | tf_op jit(solution)/shard_map/ppermute | solution.py:184
  306.6 60.1 %collective-permute-start.14 = (bf16[320,2560]{1,0:T(8,128)(2,1)}, bf16[320,2560]{1,0:T(8,128)(2,1)}, u32[]{:S(2)}, u32[]{:S(2)}) collective-permute-start(bf16[320,2560]{1,0:T(8,128)(2,1)} %bitcast.245), channel_id=1, source_target_pairs={{0,8},{4,12},{8,0},{12,4},{16,24},{20,28},{24,16},{28,20},{1,9},{5... | collective-permute-start | bytes 4915208 | tf_op jit(solution)/shard_map/ppermute | solution.py:184
  308.3 73.3 %collective-permute-start.15 = (bf16[320,2560]{1,0:T(8,128)(2,1)}, bf16[320,2560]{1,0:T(8,128)(2,1)}, u32[]{:S(2)}, u32[]{:S(2)}) collective-permute-start(bf16[320,2560]{1,0:T(8,128)(2,1)} %bitcast.245), channel_id=1, source_target_pairs={{0,16},{4,20},{8,24},{12,28},{16,0},{20,4},{24,8},{28,12},{1,17},{... | collective-permute-start | bytes 4915208 | tf_op jit(solution)/shard_map/ppermute | solution.py:184
  308.5 73.1 %collective-permute-start.16 = (bf16[320,2560]{1,0:T(8,128)(2,1)}, bf16[320,2560]{1,0:T(8,128)(2,1)}, u32[]{:S(2)}, u32[]{:S(2)}) collective-permute-start(bf16[320,2560]{1,0:T(8,128)(2,1)} %bitcast.245), channel_id=1, source_target_pairs={{0,24},{4,28},{8,16},{12,20},{16,8},{20,12},{24,0},{28,4},{1,25},{... | collective-permute-start | bytes 4915208 | tf_op jit(solution)/shard_map/ppermute | solution.py:184
  395.7 90.6 %collective-permute-start.19 = (bf16[4,320,2560]{2,1,0:T(8,128)(2,1)}, bf16[4,320,2560]{2,1,0:T(8,128)(2,1)}, u32[]{:S(2)}, u32[]{:S(2)}) collective-permute-start(bf16[4,320,2560]{2,1,0:T(8,128)(2,1)} %bitcast_dynamic-update-slice_fusion.4), channel_id=1, source_target_pairs={{0,4},{4,0},{8,12},{12,8},{16,20},{20,16},{24,28},{28,24},{1,5},{5... | collective-permute-start | bytes 19660808 | tf_op jit(solution)/shard_map/ppermute | solution.py:184
  410.0 64.6 %all-to-all-start.7 = ((bf16[4,128,2560]{1,2,0:T(8,128)(2,1)}), bf16[4,128,2560]{1,2,0:T(8,128)(2,1)}, u32[]{:S(2)}, u32[]{:S(2)}) async-start(bf16[4,128,2560]{1,2,0:T(8,128)(2,1)} %bitcast.496), calls=%async_computation.7 | async-start | bytes 5242880 | tf_op jit(solution)/shard_map/all_to_all | solution.py:803
  414.7 275.1 %all-gather.13.cloned.1.call-start = ((), (), s32[]{:S(2)}) async-start(), calls=%async_computation.33 | async-start | bytes 5120000 | tf_op jit(solution)/shard_map/all_gather | solution.py:805
  414.9 59.2 %collective-permute-start.17 = (bf16[512,2560]{1,0:T(8,128)(2,1)}, bf16[512,2560]{1,0:T(8,128)(2,1)}, u32[]{:S(2)}, u32[]{:S(2)}) collective-permute-start(bf16[512,2560]{1,0:T(8,128)(2,1)} %fusion.9), channel_id=1, source_target_pairs={{0,8},{4,12},{8,0},{12,4},{16,24},{20,28},{24,16},{28,20},{1,9},{5... | collective-permute-start | bytes 7864328 | tf_op jit(solution)/shard_map/ppermute | solution.py:184
  415.4 58.8 %collective-permute-start.18 = (bf16[512,2560]{1,0:T(8,128)(2,1)}, bf16[512,2560]{1,0:T(8,128)(2,1)}, u32[]{:S(2)}, u32[]{:S(2)}) collective-permute-start(bf16[512,2560]{1,0:T(8,128)(2,1)} %fusion.9), channel_id=1, source_target_pairs={{0,16},{4,20},{8,24},{12,28},{16,0},{20,4},{24,8},{28,12},{1,17},{... | collective-permute-start | bytes 7864328 | tf_op jit(solution)/shard_map/ppermute | solution.py:184
  510.2 508.2 %reduce-scatter.6.cloned.1.call-start = ((), (), s32[]{:S(2)}) async-start(), calls=%async_computation.30 | async-start | bytes 5120000 | tf_op jit(solution)/shard_map/reduce_scatter | solution.py:868
  510.3 64.2 %collective-permute-start.26 = (bf16[256,2560]{1,0:T(8,128)(2,1)S(1)}, bf16[256,2560]{1,0:T(8,128)(2,1)S(1)}, u32[]{:S(2)}, u32[]{:S(2)}) collective-permute-start(bf16[256,2560]{1,0:T(8,128)(2,1)S(1)} %get-tuple-element.588), channel_id=1, source_target_pairs={{0,16},{4,20},{8,24},{12,28},{16,0},{20,4},{24,8},{28,12},{1,17},{... | collective-permute-start | bytes 3932168 | tf_op jit(solution)/shard_map/ppermute | solution.py:184
  609.3 61.8 %collective-permute-start.34 = (bf16[512,2560]{1,0:T(8,128)(2,1)S(1)}, bf16[512,2560]{1,0:T(8,128)(2,1)}, u32[]{:S(2)}, u32[]{:S(2)}) collective-permute-start(bf16[512,2560]{1,0:T(8,128)(2,1)S(1)} %copy-done.9), channel_id=1, source_target_pairs={{0,4},{4,0},{8,12},{12,8},{16,20},{20,16},{24,28},{28,24},{1,5},{5... | collective-permute-start | bytes 7864328 | tf_op jit(solution)/shard_map/ppermute | solution.py:184
  609.3 60.2 %collective-permute-start.37 = (bf16[512,2560]{1,0:T(8,128)(2,1)S(1)}, bf16[512,2560]{1,0:T(8,128)(2,1)S(1)}, u32[]{:S(2)}, u32[]{:S(2)}) collective-permute-start(bf16[512,2560]{1,0:T(8,128)(2,1)S(1)} %copy-done.9), channel_id=1, source_target_pairs={{0,24},{4,28},{8,16},{12,20},{16,8},{20,12},{24,0},{28,4},{1,25},{... | collective-permute-start | bytes 7864328 | tf_op jit(solution)/shard_map/ppermute | solution.py:184
  610.5 67.5 %collective-permute-start.35 = (bf16[512,2560]{1,0:T(8,128)(2,1)}, bf16[512,2560]{1,0:T(8,128)(2,1)}, u32[]{:S(2)}, u32[]{:S(2)}) collective-permute-start(bf16[512,2560]{1,0:T(8,128)(2,1)} %collective-permute-done.17), channel_id=1, source_target_pairs={{0,4},{4,0},{8,12},{12,8},{16,20},{20,16},{24,28},{28,24},{1,5},{5... | collective-permute-start | bytes 7864328 | tf_op jit(solution)/shard_map/ppermute | solution.py:184
  610.7 74.2 %collective-permute-start.36 = (bf16[512,2560]{1,0:T(8,128)(2,1)}, bf16[512,2560]{1,0:T(8,128)(2,1)S(1)}, u32[]{:S(2)}, u32[]{:S(2)}) collective-permute-start(bf16[512,2560]{1,0:T(8,128)(2,1)} %collective-permute-done.18), channel_id=1, source_target_pairs={{0,4},{4,0},{8,12},{12,8},{16,20},{20,16},{24,28},{28,24},{1,5},{5... | collective-permute-start | bytes 7864328 | tf_op jit(solution)/shard_map/ppermute | solution.py:184
  818.3 493.8 %reduce-scatter.8.cloned.1.call-start = ((), (), s32[]{:S(2)}) async-start(), calls=%async_computation.31 | async-start | bytes 10240000 | tf_op jit(solution)/shard_map/reduce_scatter | solution.py:879
  1004.9 70.3 %all-to-all-start.10 = ((bf16[4,64,2560]{2,1,0:T(8,128)(2,1)}), bf16[4,64,2560]{2,1,0:T(8,128)(2,1)S(1)}, u32[]{:S(2)}, u32[]{:S(2)}) async-start(bf16[4,64,2560]{2,1,0:T(8,128)(2,1)} %get-tuple-element.585), calls=%async_computation.10 | async-start | bytes 2621440 | tf_op jit(solution)/shard_map/all_to_all | solution.py:885
  1075.3 88.1 %all-to-all-start.11 = ((bf16[4,64,2560]{2,1,0:T(8,128)(2,1)}), bf16[4,64,2560]{2,1,0:T(8,128)(2,1)}, u32[]{:S(2)}, u32[]{:S(2)}) async-start(bf16[4,64,2560]{2,1,0:T(8,128)(2,1)} %get-tuple-element.166), calls=%async_computation.12 | async-start | bytes 2621440 | tf_op jit(solution)/shard_map/all_to_all | solution.py:893
  1079.6 552.8 %reduce-scatter.4.cloned.1.call-start = ((), (), s32[]{:S(2)}) async-start(), calls=%async_computation.29 | async-start | bytes 23592960 | tf_op jit(solution)/shard_map/reduce_scatter | solution.py:897
  1085.5 73.5 %collective-permute-start.55 = (bf16[320,2560]{1,0:T(8,128)(2,1)}, bf16[320,2560]{1,0:T(8,128)(2,1)}, u32[]{:S(2)}, u32[]{:S(2)}) collective-permute-start(bf16[320,2560]{1,0:T(8,128)(2,1)} %get-tuple-element.575), channel_id=1, source_target_pairs={{0,16},{4,20},{8,24},{12,28},{16,0},{20,4},{24,8},{28,12},{1,17},{... | collective-permute-start | bytes 4915208 | tf_op jit(solution)/shard_map/ppermute | solution.py:184
  1086.9 72.0 %collective-permute-start.56 = (bf16[320,2560]{1,0:T(8,128)(2,1)S(1)}, bf16[320,2560]{1,0:T(8,128)(2,1)}, u32[]{:S(2)}, u32[]{:S(2)}) collective-permute-start(bf16[320,2560]{1,0:T(8,128)(2,1)S(1)} %get-tuple-element.574), channel_id=1, source_target_pairs={{0,24},{4,28},{8,16},{12,20},{16,8},{20,12},{24,0},{28,4},{1,25},{... | collective-permute-start | bytes 4915208 | tf_op jit(solution)/shard_map/ppermute | solution.py:184
  1175.6 92.9 %all-to-all-start.13 = ((bf16[8,200,320]{2,1,0:T(8,128)(2,1)}), bf16[8,200,320]{2,1,0:T(8,128)(2,1)}, u32[]{:S(2)}, u32[]{:S(2)}) async-start(bf16[8,200,320]{2,1,0:T(8,128)(2,1)} %copy.814), calls=%async_computation.15 | async-start | bytes 2457600 | tf_op jit(solution)/shard_map/all_to_all | solution.py:912
  1359.0 161.3 %collective-permute-start.57 = (bf16[4,320,1056]{2,1,0:T(8,128)(2,1)}, bf16[4,320,1056]{2,1,0:T(8,128)(2,1)}, u32[]{:S(2)}, u32[]{:S(2)}) collective-permute-start(bf16[4,320,1056]{2,1,0:T(8,128)(2,1)} %dynamic-slice_bitcast_fusion.1), channel_id=1, source_target_pairs={{0,4},{4,0},{8,12},{12,8},{16,20},{20,16},{24,28},{28,24},{1,5},{5... | collective-permute-start | bytes 8110088 | tf_op jit(solution)/shard_map/ppermute | solution.py:184
  1441.9 86.0 %all-to-all-start.19 = ((bf16[4,128,1280]{1,2,0:T(8,128)(2,1)}), bf16[4,128,1280]{1,2,0:T(8,128)(2,1)}, u32[]{:S(2)}, u32[]{:S(2)}) async-start(bf16[4,128,1280]{1,2,0:T(8,128)(2,1)} %bitcast.143), calls=%async_computation.22 | async-start | bytes 2621440 | tf_op jit(solution)/shard_map/all_to_all | solution.py:353
  (170 other events, 3861.3 us)
Sparse Core Ops, SparseCore 0:
  25.5 37.5 all-gather.10
  184.8 99.6 all-gather.6
  286.6 77.5 all-gather.8
  510.4 79.5 all-gather.12
  818.4 75.0 reduce-scatter.5
  917.7 162.0 reduce-scatter.7
  1115.9 150.1 reduce-scatter.3

commit v4 on v3

--- a/solution.py
+++ b/solution.py
@@ -320,16 +320,21 @@
     return lax.optimization_barrier(values)
 
 
+def far_shares(parts, group_size, data_count, data_index):
+    own = data_index // group_size
+    shares = []
+    for far in range(data_count // group_size):
+        part = lax.dynamic_index_in_dim(parts, own ^ far, 0, keepdims=False)
+        shares.append(swap_bit(part, far * group_size, data_count) if far else part)
+    return shares
+
+
+def sum_of(shares):
+    return sum((share.astype(jnp.float32) for share in shares[1:]), shares[0].astype(jnp.float32))
+
+
 def far_sum(parts, group_size, data_count, data_index):
-    own = data_index // group_size
-
-    def part_of(far):
-        return lax.dynamic_index_in_dim(parts, own ^ far, 0, keepdims=False)
-
-    total = part_of(0).astype(jnp.float32)
-    for far in range(1, data_count // group_size):
-        total = total + swap_bit(part_of(far), far * group_size, data_count).astype(jnp.float32)
-    return total
+    return sum_of(far_shares(parts, group_size, data_count, data_index))
 
 
 def near_sum(grad_w, group_size, data_count, data_index):
@@ -709,11 +714,10 @@
     )
     units = exchange_units(units)
     lat_w = far_parts(row_major(columns(lat_w)), group, data_count)
-    both_w, *lat_w = tie(columns(both_w), *lat_w)
+    both_w, units, *lat_w = tie(columns(both_w), units, *lat_w)
     both_w = both_w.reshape(query_rows + keyval_rows, group, -1)
     both_w = lax.all_to_all(both_w, "dp", 1, 0, axis_index_groups=near)
-    both_w, units = tie(row_major(both_w), units)
-    both_parts = far_parts(both_w, group, data_count)
+    both_parts = far_parts(row_major(both_w), group, data_count)
     lat_w = rows_of(lat_w, group, data_count, data_index)
     gain_all = gain_all.reshape(-1).astype(jnp.float32)
     gain_one = gain_all[:WIDTH]
@@ -791,19 +795,22 @@
         return parts.reshape(length, -1)
 
     grad_out = cotangent.reshape(micro * share, WIDTH).astype(jnp.float32)
-    mixed_own, attended, *output_parts = tie(
-        (RESIDUAL * grad_out).astype(bf16), attended, *output_parts
-    )
-    output_w = rows_of(output_parts, group, data_count, data_index)
+    mixed_own, attended = tie((RESIDUAL * grad_out).astype(bf16), attended)
     mixed_parts = [mixed_own] + [
         swap_bit(mixed_own, bit, data_count) for bit in bits_of(group, data_count)
     ]
     attended, gate_halves[1] = tie(attended, gate_halves[1])
-    attended = heads_near(attended)
-    attended = lax.all_to_all(attended, "mp", 0, 0, tiled=True)
-    down_t, attended, *mixed_parts = tie(units[2], attended, *mixed_parts)
+    attended, *output_parts = tie(heads_near(attended), *output_parts)
+    middle = attended.shape[1] // 2
+    early = lax.all_to_all(attended[:, :middle], "mp", 0, 0, tiled=True)
+    late, early, *output_parts = tie(attended[:, middle:], early, *output_parts)
+    late = lax.all_to_all(late, "mp", 0, 0, tiled=True)
+    output_w = rows_of(output_parts, group, data_count, data_index)
+    attended = jnp.concatenate([early, late], axis=1)
+    down_t, attended = tie(units[2], attended)
     down_t = lax.all_gather(down_t, "mp", axis=0).reshape(hidden_units, WIDTH)
     attended_own = to_owners(attended, group, near).reshape(micro * share, -1)
+    attended_own, *mixed_parts = tie(attended_own, *mixed_parts)
     branch = dot_last(attended_own, output_w)
     hidden = tok + RESIDUAL * branch
     normed_two, inverse_two = rms_parts(hidden, gain_two)
@@ -828,10 +835,10 @@
 
     down_t = jnp.concatenate([down_t, gate_pad], axis=0)
     normed_full, *mixed_parts = tie(joined(normed_two), *mixed_parts)
-    early = [0] + [bit // group for bit in bits_of(group, data_count)]
+    sent_far = [0] + [bit // group for bit in bits_of(group, data_count)]
     mixed_parts = [
-        mixed_parts[early.index(far)]
-        if far in early
+        mixed_parts[sent_far.index(far)]
+        if far in sent_far
         else swap_bit(mixed_parts[0], far * group, data_count)
         for far in range(far_count)
     ]
@@ -878,8 +885,8 @@
     ).reshape(model_count, 2 * unit_count, WIDTH)
     gate_sum = lax.psum_scatter(gate_sum, "mp", scatter_dimension=0, tiled=True)
     grad_attended = jnp.dot(grad_branch, output_w, preferred_element_type=jnp.float32)
-    grad_attended = near_parts(
-        grad_attended.astype(bf16).reshape(micro, share, -1), group, near
+    grad_attended, grad_branch = tie(
+        near_parts(grad_attended.astype(bf16).reshape(micro, share, -1), group, near), grad_branch
     )
     tail = grad_attended.shape[1] // 2
     early = lax.all_to_all(grad_attended[:, :tail], "mp", 0, 0, tiled=True)
@@ -898,10 +905,12 @@
         mixed_out.reshape(data_count, -1, WIDTH), "dp", scatter_dimension=0, tiled=True
     ).reshape(hidden.shape)
     grad_attended = heads_in(jnp.concatenate([early, late], axis=1))
-    project_sum = far_sum(project_sum, group, data_count, data_index)
+    project_shares = far_shares(project_sum, group, data_count, data_index)
     grad_query_all, grad_keyval, grad_shared = attend_back(
         queries, keyval, grad_attended, key_lanes, bias, tables, scale_attn, rows_attn
     )
+    grad_query_all, *project_shares = tie(grad_query_all, *project_shares)
+    project_sum = sum_of(project_shares)
     grad_shared = rotate_back(
         grad_shared[:, NOPE_DIM : NOPE_DIM + ROPE_DIM], cosine, sine_part
     )

time: 1660 us -> 1650 us (level)
  waiting for transfers between devices: 451 us -> 335 us
  local copies, waits for them, and re-layouts: 386 us -> 431 us
  blocking collectives: 56.5 us -> 87.4 us
  other arithmetic: 164 us -> 182 us
    ppermute x58, waiting for transfers between devices: 319 us -> 251 us  [swap_bit(): return lax.ppermute(values, 'dp', [(i, i ^ bit) for i in range(data_count)])]
    all_to_all x1, waiting for transfers between devices: 33.7 us -> 0.01 us  [exchange_units(): return lax.all_to_all(values, 'dp', 0, 0, tiled=True)]
    all_to_all x1, blocking collectives: 6.82 us -> 35.6 us  [on_device(): early = lax.all_to_all(attended[:, :middle], 'mp', 0, 0, tiled=True)]
    all_to_all x1, waiting for transfers between devices: 20.8 us -> 0.01 us  [on_device(): gate_sum = lax.all_to_all(gate_sum, 'dp', 0, 0, tiled=True)]
    unnamed x284 -> x260, local copies, waits for them, and re-layouts: 66.2 us -> 85.5 us
  transfers between devices with their start and end apart: 86 -> 87, of which waited for: 31 -> 27; matrix products, arithmetic and copies ran while one was open for 46% -> 48% of each run, Pallas kernels for 7% -> 7%
where the time goes in v4:
time: 1650 us; the launch traced here: 1630 us
  local copies, waits for them, and re-layouts  431 us (26%)
  waiting for transfers between devices  335 us (20%)
  matrix products  335 us (20%)
  other arithmetic  182 us (11%)
  starting transfers between devices  129 us (8%)
  Pallas kernels  117 us (7%)
  blocking collectives  87.4 us (5%)
  between operations  17.1 us (1%)
    ppermute x58, waiting for transfers between devices, swap_bit(): return lax.ppermute(values, 'dp', [(i, i ^ bit) for i in range(data_count)])  251 us
    dot_general x6, matrix products, dot_last(): lax.dot_general(first_arg, second_arg, (((1,), (1,)), ((), ())), preferre...  116 us
    dot_general x6, matrix products, dot_first(): lax.dot_general(first_arg, second_arg, (((0,), (0,)), ((), ())), preferre...  93.2 us
    unnamed x260, local copies, waits for them, and re-layouts  85.5 us
    pallas_call x1, Pallas kernels, attend_back(): pl.pallas_call(functools.partial(attend_back_kernel, scale, rows), grid=(...  72 us
    ppermute x58, starting transfers between devices, swap_bit(): return lax.ppermute(values, 'dp', [(i, i ^ bit) for i in range(data_count)])  45.6 us
    dot_general x1, matrix products, on_device(): jnp.dot(grad_gateup, gate_t, preferred_element_type=jnp.float32)  45.5 us
    all_to_all x1, waiting for transfers between devices, on_device(): early = lax.all_to_all(grad_attended[:, :tail], 'mp', 0, 0, tiled=True)  44 us
  transfers between devices with their start and end apart: 87, of which 27 were waited for; matrix products, arithmetic and copies ran while one was open for 48% of the time, Pallas kernels for 7%

profile of v4, /device:TPU:0, one launch (start us, length us, event | category | flops | bytes accessed | tf_op | source)
XLA Modules:
  0.0 1634.4 jit_solution(8941191542835118219)
XLA Ops:
  97.7 8.8 collective-permute-done.4
  115.4 10.8 collective-permute-done.6
  126.3 16.3 collective-permute-done.8
  219.1 15.5 collective-permute-done.10
  234.6 27.6 %collective-permute-done.11 = bf16[2,128,2560]{2,1,0:T(8,128)(2,1)} collective-permute-done((bf16[2,128,2560]{2,1,0:T(8,128)(2,1)}, bf16[2,128,2560]{2,1,0:T(8,128)(2,1)}, u32[]{:S(2)}, u32[]{:S(2)}) %collective-permute-start.11) | collective-permute-done | bytes 1310752 | tf_op jit(solution)/shard_map/ppermute | solution.py:184
  309.5 43.3 %shard_map.659 = (bf16[1024,1280]{1,0:T(8,128)(2,1)}, bf16[1024,2560]{1,0:T(8,128)(2,1)}, bf16[1024,2560]{1,0:T(8,128)(2,1)}, f32[10,16,128]{2,1,0:T(8,128)}) custom-call(bf16[1024,768]{1,0:T(8,128)(2,1)} %slice.317.query_latent_ref, bf16[1024,256]{1,0:T(8,128)(2,1)} %slice.318.keyval_latent_ref, bf16[768,2560]{1,0:T(8,128)(2,1)} %bitcast.529, ...), custom_call_target="tpu_custom_call" | custom-call | flops 21474836480 | bytes 20971520 | tf_op jit(solution)/shard_map/pallas_call | solution.py:557
  374.7 35.6 %all_to_all.213 = bf16[4,64,2560]{2,1,0:T(8,128)(2,1)} all-to-all(bf16[4,64,2560]{2,1,0:T(8,128)(2,1)} %copy.804), channel_id=1, replica_groups=mesh['dp'=8,'mp'=4] {'mp'}, dimensions={0} | all-to-all | bytes 2621440 | tf_op jit(solution)/shard_map/all_to_all | solution.py:805
  452.4 14.3 all-to-all-done.8
  493.0 11.1 multiply_reduce_fusion
  512.0 27.2 %collective-permute-done.22 = bf16[256,2560]{1,0:T(8,128)(2,1)} collective-permute-done((bf16[256,2560]{1,0:T(8,128)(2,1)S(1)}, bf16[256,2560]{1,0:T(8,128)(2,1)}, u32[]{:S(2)}, u32[]{:S(2)}) %collective-permute-start.22) | collective-permute-done | bytes 1310752 | tf_op jit(solution)/shard_map/ppermute | solution.py:184
  543.8 23.4 %collective-permute-done.23 = bf16[256,2560]{1,0:T(8,128)(2,1)} collective-permute-done((bf16[256,2560]{1,0:T(8,128)(2,1)S(1)}, bf16[256,2560]{1,0:T(8,128)(2,1)}, u32[]{:S(2)}, u32[]{:S(2)}) %collective-permute-start.23) | collective-permute-done | bytes 1310752 | tf_op jit(solution)/shard_map/ppermute | solution.py:184
  575.3 20.8 %collective-permute-done.30 = bf16[256,2560]{1,0:T(8,128)(2,1)S(1)} collective-permute-done((bf16[256,2560]{1,0:T(8,128)(2,1)}, bf16[256,2560]{1,0:T(8,128)(2,1)S(1)}, u32[]{:S(2)}, u32[]{:S(2)}) %collective-permute-start.30) | collective-permute-done | bytes 1310752 | tf_op jit(solution)/shard_map/ppermute | solution.py:184
  611.7 51.1 %fusion.35 = f32[4096,1792]{1,0:T(8,128)} fusion(bf16[4096,2560]{1,0:T(8,128)(2,1)} %constant_dynamic-update-slice_fusion, bf16[96,2560]{1,0:T(8,128)(2,1)S(1)} %broadcast_in_dim.245, bf16[800,2560]{1,0:T(8,128)(2,1)} %bitcast.584, bf16[800,2560]{1,0:T(8,128)(2,1)} %bitcast.582), kind=kOutput, calls=%fused_computation.111 | convolution fusion | flops 37617664000 | bytes 59015168 | tf_op jit(solution)/shard_map/dot_general | solution.py:105
  690.3 36.4 %multiply_convert_fusion.2 = (bf16[4096,896]{1,0:T(8,128)(2,1)}, bf16[4096,896]{1,0:T(8,128)(2,1)}, bf16[4096,896]{1,0:T(8,128)(2,1)}) fusion(f32[4096,1792]{1,0:T(8,128)} %fusion.35, bf16[4096,2560]{1,0:T(8,128)(2,1)} %constant_dynamic-update-slice_fusion.15, bf16[800,2560]{1,0:T(8,128)(2,1)} %all-gather.13.cloned.1.call-done), kind=kOutput, calls=%fused_computation.6 | convolution fusion | flops 18845532160 | bytes 76447744 | tf_op jit(solution)/shard_map/dot_general | solution.py:105
  726.7 45.5 %convolution_convert_fusion = bf16[4096,2560]{1,0:T(8,128)(2,1)} fusion(bf16[4096,896]{1,0:T(8,128)(2,1)} %get-tuple-element.585, bf16[4096,896]{1,0:T(8,128)(2,1)} %get-tuple-element.584, bf16[96,2560]{1,0:T(8,128)(2,1)S(1)} %broadcast_in_dim.245, bf16[800,2560]{1,0:T(8,128)(2,1)} %bitcast.585, bf16[800,2560]{1,0:T(8,128)(2,1)} %bitcast.583), kind=kOutput, calls=%fused_computation | convolution fusion | flops 37657509888 | bytes 44335104 | tf_op jit(solution)/shard_map/dot_general | solution.py:866
  784.2 22.1 %convolution_convert_fusion.5 = bf16[896,2560]{1,0:T(8,128)(2,1)S(1)} fusion(bf16[4096,896]{1,0:T(8,128)(2,1)S(1)} %copy-done.18, bf16[4096,2560]{1,0:T(8,128)(2,1)} %constant_dynamic-update-slice_fusion.15), kind=kOutput, calls=%fused_computation.27 | convolution fusion | flops 18792775680 | bytes 32899072 | tf_op jit(solution)/shard_map/dot_general | solution.py:99
  819.0 47.9 %convolution_convert_fusion.3 = bf16[1792,2560]{1,0:T(8,128)(2,1)} fusion(bf16[4096,2560]{1,0:T(8,128)(2,1)} %constant_dynamic-update-slice_fusion, bf16[4096,896]{1,0:T(8,128)(2,1)} %get-tuple-element.585, bf16[4096,896]{1,0:T(8,128)(2,1)} %get-tuple-element.584), kind=kOutput, calls=%fused_computation.11 | convolution fusion | flops 37614911488 | bytes 44826624 | tf_op jit(solution)/shard_map/dot_general | solution.py:99
  875.6 28.3 %collective-permute-done.51 = bf16[256,2560]{1,0:T(8,128)(2,1)S(1)} collective-permute-done((bf16[256,2560]{1,0:T(8,128)(2,1)S(1)}, bf16[256,2560]{1,0:T(8,128)(2,1)S(1)}, u32[]{:S(2)}, u32[]{:S(2)}) %collective-permute-start.51) | collective-permute-done | bytes 1310752 | tf_op jit(solution)/shard_map/ppermute | solution.py:184
  918.3 19.9 %collective-permute-done.52 = bf16[256,2560]{1,0:T(8,128)(2,1)} collective-permute-done((bf16[256,2560]{1,0:T(8,128)(2,1)}, bf16[256,2560]{1,0:T(8,128)(2,1)}, u32[]{:S(2)}, u32[]{:S(2)}) %collective-permute-start.52) | collective-permute-done | bytes 1310752 | tf_op jit(solution)/shard_map/ppermute | solution.py:184
  951.0 10.0 convolution_convert_fusion.7
  1020.7 9.3 fusion.1
  1030.0 44.0 %all-to-all-done.11 = bf16[4,64,2560]{2,1,0:T(8,128)(2,1)S(1)} async-done(((bf16[4,64,2560]{2,1,0:T(8,128)(2,1)}), bf16[4,64,2560]{2,1,0:T(8,128)(2,1)S(1)}, u32[]{:S(2)}, u32[]{:S(2)}) %all-to-all-start.11) | async-done | bytes 1310752 | tf_op jit(solution)/shard_map/all_to_all | solution.py:892
  1087.8 28.0 %convolution_convert_fusion.1 = bf16[4096,2560]{1,0:T(8,128)(2,1)} fusion(bf16[4096,896]{1,0:T(8,128)(2,1)} %bitcast.514, bf16[800,2560]{1,0:T(8,128)(2,1)S(1)} %copy-done.96), kind=kOutput, calls=%fused_computation.1 | convolution fusion | flops 18800967680 | bytes 32407552 | tf_op jit(solution)/shard_map/dot_general | solution.py:901
  1136.8 72.0 %shard_map.660 = (bf16[1024,2560]{1,0:T(8,128)(2,1)}, bf16[1024,2560]{1,0:T(8,128)(2,1)}, f32[1024,128]{1,0:T(8,128)}) custom-call(bf16[1024,2560]{1,0:T(8,128)(2,1)} %get-tuple-element.186.query_ref, bf16[1024,2560]{1,0:T(8,128)(2,1)} %get-tuple-element.187.keyval_ref, bf16[1024,1280]{1,0:T(8,128)(2,1)} %bitcast.537, bf16[1024,128]{1,0:T(8,128)(2,1)} %pad.31.key_ref, ...), custom_call_target="tpu_custom_call" | custom-call | flops 42949672960 | bytes 20971520 | tf_op jit(solution)/shard_map/pallas_call | solution.py:591
  1307.8 9.0 fusion.21
  1321.5 23.6 %collective-permute-done.62 = bf16[256,2560]{1,0:T(8,128)(2,1)} collective-permute-done((bf16[256,2560]{1,0:T(8,128)(2,1)}, bf16[256,2560]{1,0:T(8,128)(2,1)}, u32[]{:S(2)}, u32[]{:S(2)}) %collective-permute-start.62) | collective-permute-done | bytes 1310752 | tf_op jit(solution)/shard_map/ppermute | solution.py:184
  1375.1 8.6 copy.828
  1419.2 17.3 %add_divide_fusion.1 = (f32[320,2,1600]{2,1,0:T(2,128)}, f32[320,2,1600]{2,1,0:T(2,128)}, f32[320,2,1600]{2,1,0:T(2,128)}) fusion(f32[320,2,1600]{2,1,0:T(2,128)} %reshape.688, f32[320,2,1600]{2,1,0:T(2,128)} %param.60, f32[320,2,1600]{2,1,0:T(2,128)} %param.61), kind=kLoop, calls=%fused_computation.66 | loop fusion | flops 10240000 | bytes 24576000 | tf_op jit(solution)/shard_map/div | solution.py:121
  1467.9 8.5 fusion.133
  1509.0 9.1 collective-permute-done.59
  1545.0 7.9 all-to-all-done.18
  1616.6 10.7 fusion.18
  (763 shorter events, 853.3 us)
Async XLA Ops:
  9.2 63.0 %collective-permute-start = (bf16[320,264]{1,0:T(8,128)(2,1)}, bf16[320,264]{1,0:T(8,128)(2,1)}, u32[]{:S(2)}, u32[]{:S(2)}) collective-permute-start(bf16[320,264]{1,0:T(8,128)(2,1)} %copy.774), channel_id=1, source_target_pairs={{0,1},{1,2},{2,3},{3,0},{4,5},{5,6},{6,7},{7,4},{8,9},{9,10},{10,1... | collective-permute-start | bytes 506888 | tf_op jit(solution)/shard_map/ppermute | solution.py:263
  12.2 61.8 %collective-permute-start.1 = (bf16[320,264]{1,0:T(8,128)(2,1)}, bf16[320,264]{1,0:T(8,128)(2,1)}, u32[]{:S(2)}, u32[]{:S(2)}) collective-permute-start(bf16[320,264]{1,0:T(8,128)(2,1)} %copy.774), channel_id=1, source_target_pairs={{0,2},{1,3},{2,0},{3,1},{4,6},{5,7},{6,4},{7,5},{8,10},{9,11},{10,... | collective-permute-start | bytes 506888 | tf_op jit(solution)/shard_map/ppermute | solution.py:263
  14.8 60.9 %collective-permute-start.2 = (bf16[320,264]{1,0:T(8,128)(2,1)}, bf16[320,264]{1,0:T(8,128)(2,1)}, u32[]{:S(2)}, u32[]{:S(2)}) collective-permute-start(bf16[320,264]{1,0:T(8,128)(2,1)} %copy.774), channel_id=1, source_target_pairs={{0,3},{1,0},{2,1},{3,2},{4,7},{5,4},{6,5},{7,6},{8,11},{9,8},{10,9... | collective-permute-start | bytes 506888 | tf_op jit(solution)/shard_map/ppermute | solution.py:263
  22.4 260.6 %all-gather.11.cloned.1.call-start = ((), (), s32[]{:S(2)}) async-start(), calls=%async_computation.33 | async-start | bytes 2048000 | tf_op jit(solution)/shard_map/all_gather | solution.py:695
  62.7 79.8 %all-to-all-start = ((bf16[8,3,200,320]{3,2,1,0:T(8,128)(2,1)}), bf16[8,3,200,320]{3,2,1,0:T(8,128)(2,1)}, u32[]{:S(2)}, u32[]{:S(2)}) async-start(bf16[8,3,200,320]{3,2,1,0:T(8,128)(2,1)} %copy.784), calls=%async_computation | async-start | bytes 7372800 | tf_op jit(solution)/shard_map/all_to_all | solution.py:687
  67.2 228.9 %all-gather.7.cloned.1.call-start = ((), (), s32[]{:S(2)}) async-start(), calls=%async_computation.28 | async-start | bytes 5120000 | tf_op jit(solution)/shard_map/all_gather | solution.py:745
  197.9 64.3 %all-to-all-start.3 = ((bf16[4,128,1056]{1,2,0:T(8,128)(2,1)}), bf16[4,128,1056]{1,2,0:T(8,128)(2,1)}, u32[]{:S(2)}, u32[]{:S(2)}) async-start(bf16[4,128,1056]{1,2,0:T(8,128)(2,1)} %bitcast.526), calls=%async_computation.3 | async-start | bytes 2162688 | tf_op jit(solution)/shard_map/all_to_all | solution.py:741
  202.2 150.6 %all-gather.9.cloned.1.call-start = ((), (), s32[]{:S(2)}) async-start(), calls=%async_computation.29 | async-start | bytes 5120000 | tf_op jit(solution)/shard_map/all_gather | solution.py:752
  203.2 58.9 %collective-permute-start.11 = (bf16[2,128,2560]{2,1,0:T(8,128)(2,1)}, bf16[2,128,2560]{2,1,0:T(8,128)(2,1)}, u32[]{:S(2)}, u32[]{:S(2)}) collective-permute-start(bf16[2,128,2560]{2,1,0:T(8,128)(2,1)} %bitcast.36), channel_id=1, source_target_pairs={{0,16},{4,20},{8,24},{12,28},{16,0},{20,4},{24,8},{28,12},{1,17},{... | collective-permute-start | bytes 3932168 | tf_op jit(solution)/shard_map/ppermute | solution.py:184
  292.6 71.9 %collective-permute-start.14 = (bf16[320,2560]{1,0:T(8,128)(2,1)}, bf16[320,2560]{1,0:T(8,128)(2,1)}, u32[]{:S(2)}, u32[]{:S(2)}) collective-permute-start(bf16[320,2560]{1,0:T(8,128)(2,1)} %bitcast.245), channel_id=1, source_target_pairs={{0,8},{4,12},{8,0},{12,4},{16,24},{20,28},{24,16},{28,20},{1,9},{5... | collective-permute-start | bytes 4915208 | tf_op jit(solution)/shard_map/ppermute | solution.py:184
  294.1 73.3 %collective-permute-start.15 = (bf16[320,2560]{1,0:T(8,128)(2,1)}, bf16[320,2560]{1,0:T(8,128)(2,1)}, u32[]{:S(2)}, u32[]{:S(2)}) collective-permute-start(bf16[320,2560]{1,0:T(8,128)(2,1)} %bitcast.245), channel_id=1, source_target_pairs={{0,16},{4,20},{8,24},{12,28},{16,0},{20,4},{24,8},{28,12},{1,17},{... | collective-permute-start | bytes 4915208 | tf_op jit(solution)/shard_map/ppermute | solution.py:184
  294.6 72.8 %collective-permute-start.16 = (bf16[320,2560]{1,0:T(8,128)(2,1)}, bf16[320,2560]{1,0:T(8,128)(2,1)}, u32[]{:S(2)}, u32[]{:S(2)}) collective-permute-start(bf16[320,2560]{1,0:T(8,128)(2,1)} %bitcast.245), channel_id=1, source_target_pairs={{0,24},{4,28},{8,16},{12,20},{16,8},{20,12},{24,0},{28,4},{1,25},{... | collective-permute-start | bytes 4915208 | tf_op jit(solution)/shard_map/ppermute | solution.py:184
  424.5 60.1 %collective-permute-start.19 = (bf16[4,320,2560]{2,1,0:T(8,128)(2,1)}, bf16[4,320,2560]{2,1,0:T(8,128)(2,1)}, u32[]{:S(2)}, u32[]{:S(2)}) collective-permute-start(bf16[4,320,2560]{2,1,0:T(8,128)(2,1)} %bitcast_dynamic-update-slice_fusion.4), channel_id=1, source_target_pairs={{0,4},{4,0},{8,12},{12,8},{16,20},{20,16},{24,28},{28,24},{1,5},{5... | collective-permute-start | bytes 19660808 | tf_op jit(solution)/shard_map/ppermute | solution.py:184
  424.5 59.6 %collective-permute-start.17 = (bf16[512,2560]{1,0:T(8,128)(2,1)}, bf16[512,2560]{1,0:T(8,128)(2,1)}, u32[]{:S(2)}, u32[]{:S(2)}) collective-permute-start(bf16[512,2560]{1,0:T(8,128)(2,1)} %fusion.9), channel_id=1, source_target_pairs={{0,8},{4,12},{8,0},{12,4},{16,24},{20,28},{24,16},{28,20},{1,9},{5... | collective-permute-start | bytes 7864328 | tf_op jit(solution)/shard_map/ppermute | solution.py:184
  425.3 59.3 %collective-permute-start.18 = (bf16[512,2560]{1,0:T(8,128)(2,1)}, bf16[512,2560]{1,0:T(8,128)(2,1)}, u32[]{:S(2)}, u32[]{:S(2)}) collective-permute-start(bf16[512,2560]{1,0:T(8,128)(2,1)} %fusion.9), channel_id=1, source_target_pairs={{0,16},{4,20},{8,24},{12,28},{16,0},{20,4},{24,8},{28,12},{1,17},{... | collective-permute-start | bytes 7864328 | tf_op jit(solution)/shard_map/ppermute | solution.py:184
  434.9 255.4 %all-gather.13.cloned.1.call-start = ((), (), s32[]{:S(2)}) async-start(), calls=%async_computation.34 | async-start | bytes 5120000 | tf_op jit(solution)/shard_map/all_gather | solution.py:811
  511.1 505.9 %reduce-scatter.6.cloned.1.call-start = ((), (), s32[]{:S(2)}) async-start(), calls=%async_computation.31 | async-start | bytes 5120000 | tf_op jit(solution)/shard_map/reduce_scatter | solution.py:875
  511.1 63.6 %collective-permute-start.26 = (bf16[256,2560]{1,0:T(8,128)(2,1)S(1)}, bf16[256,2560]{1,0:T(8,128)(2,1)S(1)}, u32[]{:S(2)}, u32[]{:S(2)}) collective-permute-start(bf16[256,2560]{1,0:T(8,128)(2,1)S(1)} %get-tuple-element.619), channel_id=1, source_target_pairs={{0,16},{4,20},{8,24},{12,28},{16,0},{20,4},{24,8},{28,12},{1,17},{... | collective-permute-start | bytes 3932168 | tf_op jit(solution)/shard_map/ppermute | solution.py:184
  609.6 63.8 %collective-permute-start.34 = (bf16[512,2560]{1,0:T(8,128)(2,1)}, bf16[512,2560]{1,0:T(8,128)(2,1)}, u32[]{:S(2)}, u32[]{:S(2)}) collective-permute-start(bf16[512,2560]{1,0:T(8,128)(2,1)} %fusion.9), channel_id=1, source_target_pairs={{0,4},{4,0},{8,12},{12,8},{16,20},{20,16},{24,28},{28,24},{1,5},{5... | collective-permute-start | bytes 7864328 | tf_op jit(solution)/shard_map/ppermute | solution.py:184
  609.6 60.4 %collective-permute-start.37 = (bf16[512,2560]{1,0:T(8,128)(2,1)}, bf16[512,2560]{1,0:T(8,128)(2,1)S(1)}, u32[]{:S(2)}, u32[]{:S(2)}) collective-permute-start(bf16[512,2560]{1,0:T(8,128)(2,1)} %fusion.9), channel_id=1, source_target_pairs={{0,24},{4,28},{8,16},{12,20},{16,8},{20,12},{24,0},{28,4},{1,25},{... | collective-permute-start | bytes 7864328 | tf_op jit(solution)/shard_map/ppermute | solution.py:184
  611.2 69.0 %collective-permute-start.35 = (bf16[512,2560]{1,0:T(8,128)(2,1)}, bf16[512,2560]{1,0:T(8,128)(2,1)S(1)}, u32[]{:S(2)}, u32[]{:S(2)}) collective-permute-start(bf16[512,2560]{1,0:T(8,128)(2,1)} %collective-permute-done.17), channel_id=1, source_target_pairs={{0,4},{4,0},{8,12},{12,8},{16,20},{20,16},{24,28},{28,24},{1,5},{5... | collective-permute-start | bytes 7864328 | tf_op jit(solution)/shard_map/ppermute | solution.py:184
  611.4 73.9 %collective-permute-start.36 = (bf16[512,2560]{1,0:T(8,128)(2,1)}, bf16[512,2560]{1,0:T(8,128)(2,1)S(1)}, u32[]{:S(2)}, u32[]{:S(2)}) collective-permute-start(bf16[512,2560]{1,0:T(8,128)(2,1)} %collective-permute-done.18), channel_id=1, source_target_pairs={{0,4},{4,0},{8,12},{12,8},{16,20},{20,16},{24,28},{28,24},{1,5},{5... | collective-permute-start | bytes 7864328 | tf_op jit(solution)/shard_map/ppermute | solution.py:184
  819.0 455.3 %reduce-scatter.8.cloned.1.call-start = ((), (), s32[]{:S(2)}) async-start(), calls=%async_computation.32 | async-start | bytes 10240000 | tf_op jit(solution)/shard_map/reduce_scatter | solution.py:886
  1004.6 69.3 %all-to-all-start.11 = ((bf16[4,64,2560]{2,1,0:T(8,128)(2,1)}), bf16[4,64,2560]{2,1,0:T(8,128)(2,1)S(1)}, u32[]{:S(2)}, u32[]{:S(2)}) async-start(bf16[4,64,2560]{2,1,0:T(8,128)(2,1)} %get-tuple-element.616), calls=%async_computation.11 | async-start | bytes 2621440 | tf_op jit(solution)/shard_map/all_to_all | solution.py:892
  1078.3 538.3 %reduce-scatter.4.cloned.1.call-start = ((), (), s32[]{:S(2)}) async-start(), calls=%async_computation.30 | async-start | bytes 23592960 | tf_op jit(solution)/shard_map/reduce_scatter | solution.py:904
  1084.3 124.5 %collective-permute-start.54 = (bf16[320,2560]{1,0:T(8,128)(2,1)}, bf16[320,2560]{1,0:T(8,128)(2,1)}, u32[]{:S(2)}, u32[]{:S(2)}) collective-permute-start(bf16[320,2560]{1,0:T(8,128)(2,1)} %get-tuple-element.603), channel_id=1, source_target_pairs={{0,8},{4,12},{8,0},{12,4},{16,24},{20,28},{24,16},{28,20},{1,9},{5... | collective-permute-start | bytes 4915208 | tf_op jit(solution)/shard_map/ppermute | solution.py:184
  1085.8 123.0 %collective-permute-start.55 = (bf16[320,2560]{1,0:T(8,128)(2,1)}, bf16[320,2560]{1,0:T(8,128)(2,1)}, u32[]{:S(2)}, u32[]{:S(2)}) collective-permute-start(bf16[320,2560]{1,0:T(8,128)(2,1)} %get-tuple-element.602), channel_id=1, source_target_pairs={{0,16},{4,20},{8,24},{12,28},{16,0},{20,4},{24,8},{28,12},{1,17},{... | collective-permute-start | bytes 4915208 | tf_op jit(solution)/shard_map/ppermute | solution.py:184
  1087.3 121.6 %collective-permute-start.56 = (bf16[320,2560]{1,0:T(8,128)(2,1)}, bf16[320,2560]{1,0:T(8,128)(2,1)}, u32[]{:S(2)}, u32[]{:S(2)}) collective-permute-start(bf16[320,2560]{1,0:T(8,128)(2,1)} %get-tuple-element.601), channel_id=1, source_target_pairs={{0,24},{4,28},{8,16},{12,20},{16,8},{20,12},{24,0},{28,4},{1,25},{... | collective-permute-start | bytes 4915208 | tf_op jit(solution)/shard_map/ppermute | solution.py:184
  1129.8 99.2 %all-to-all-start.14 = ((bf16[8,200,320]{2,1,0:T(8,128)(2,1)}), bf16[8,200,320]{2,1,0:T(8,128)(2,1)}, u32[]{:S(2)}, u32[]{:S(2)}) async-start(bf16[8,200,320]{2,1,0:T(8,128)(2,1)} %copy.820), calls=%async_computation.16 | async-start | bytes 2457600 | tf_op jit(solution)/shard_map/all_to_all | solution.py:921
  1286.3 58.9 %collective-permute-start.62 = (bf16[256,2560]{1,0:T(8,128)(2,1)}, bf16[256,2560]{1,0:T(8,128)(2,1)}, u32[]{:S(2)}, u32[]{:S(2)}) collective-permute-start(bf16[256,2560]{1,0:T(8,128)(2,1)} %get-tuple-element.607), channel_id=1, source_target_pairs={{0,16},{4,20},{8,24},{12,28},{16,0},{20,4},{24,8},{28,12},{1,17},{... | collective-permute-start | bytes 3932168 | tf_op jit(solution)/shard_map/ppermute | solution.py:184
  1387.3 89.0 %collective-permute-start.57 = (bf16[4,320,1056]{2,1,0:T(8,128)(2,1)}, bf16[4,320,1056]{2,1,0:T(8,128)(2,1)}, u32[]{:S(2)}, u32[]{:S(2)}) collective-permute-start(bf16[4,320,1056]{2,1,0:T(8,128)(2,1)} %dynamic-slice_bitcast_fusion.1), channel_id=1, source_target_pairs={{0,4},{4,0},{8,12},{12,8},{16,20},{20,16},{24,28},{28,24},{1,5},{5... | collective-permute-start | bytes 8110088 | tf_op jit(solution)/shard_map/ppermute | solution.py:184
  1391.6 94.0 %all-to-all-start.20 = ((bf16[4,128,1280]{1,2,0:T(8,128)(2,1)}), bf16[4,128,1280]{1,2,0:T(8,128)(2,1)}, u32[]{:S(2)}, u32[]{:S(2)}) async-start(bf16[4,128,1280]{1,2,0:T(8,128)(2,1)} %bitcast.520), calls=%async_computation.23 | async-start | bytes 2621440 | tf_op jit(solution)/shard_map/all_to_all | solution.py:358
  (159 other events, 3800.5 us)
Sparse Core Ops, SparseCore 0:
  25.4 37.5 all-gather.10
  159.8 98.7 all-gather.6
  260.7 77.5 all-gather.8
  511.2 77.0 all-gather.12
  819.1 73.4 reduce-scatter.5
  918.4 160.4 reduce-scatter.7
  1115.9 150.5 reduce-scatter.3

commit v5 on v4

--- a/solution.py
+++ b/solution.py
@@ -883,7 +883,6 @@
     gate_sum = jnp.transpose(
         gate_sum.reshape(2, model_count, unit_count, WIDTH), (1, 0, 2, 3)
     ).reshape(model_count, 2 * unit_count, WIDTH)
-    gate_sum = lax.psum_scatter(gate_sum, "mp", scatter_dimension=0, tiled=True)
     grad_attended = jnp.dot(grad_branch, output_w, preferred_element_type=jnp.float32)
     grad_attended, grad_branch = tie(
         near_parts(grad_attended.astype(bf16).reshape(micro, share, -1), group, near), grad_branch
@@ -904,7 +903,10 @@
     mixed_out = lax.psum_scatter(
         mixed_out.reshape(data_count, -1, WIDTH), "dp", scatter_dimension=0, tiled=True
     ).reshape(hidden.shape)
-    grad_attended = heads_in(jnp.concatenate([early, late], axis=1))
+    grad_attended, gate_sum = tie(
+        heads_in(jnp.concatenate([early, late], axis=1)), gate_sum
+    )
+    gate_sum = lax.psum_scatter(gate_sum, "mp", scatter_dimension=0, tiled=True)
     project_shares = far_shares(project_sum, group, data_count, data_index)
     grad_query_all, grad_keyval, grad_shared = attend_back(
         queries, keyval, grad_attended, key_lanes, bias, tables, scale_attn, rows_attn
@@ -937,11 +939,8 @@
         axis=2,
     )
     gate_sum = jnp.transpose(gate_sum.reshape(2 * unit_count, data_count, -1), (1, 0, 2))
-    parts, grad_both, gate_sum = tie(
-        lax.all_to_all(parts, "mp", 0, 0, tiled=True), grad_both, gate_sum
-    )
+    parts, grad_both = tie(lax.all_to_all(parts, "mp", 0, 0, tiled=True), grad_both)
     gate_sum = lax.all_to_all(gate_sum, "dp", 0, 0, tiled=True)
-    project_sum, gate_sum = tie(project_sum, gate_sum)
     gate_sum = jnp.transpose(
         gate_sum.reshape(data_count, 2, unit_count, -1), (3, 1, 0, 2)
     ).reshape(gateup_weight.shape)

time: 1650 us -> 1750 us (1.061)
  waiting for transfers between devices: 335 us -> 433 us
    ppermute x58, waiting for transfers between devices: 251 us -> 289 us  [swap_bit(): return lax.ppermute(values, 'dp', [(i, i ^ bit) for i in range(data_count)])]
    all_to_all x2, waiting for transfers between devices: 14.3 us -> 48.7 us  [on_device(): late = lax.all_to_all(late, 'mp', 0, 0, tiled=True)]
    unnamed x260 -> x276, local copies, waits for them, and re-layouts: 85.5 us -> 84.2 us
  transfers between devices with their start and end apart: 87 -> 87, of which waited for: 27 -> 30; matrix products, arithmetic and copies ran while one was open for 48% -> 43% of each run, Pallas kernels for 7% -> 7%
where the time goes in v5:
time: 1750 us; the launch traced here: 1730 us
  local copies, waits for them, and re-layouts  437 us (25%)
  waiting for transfers between devices  433 us (25%)
  matrix products  335 us (19%)
  other arithmetic  179 us (10%)
  starting transfers between devices  129 us (7%)
  Pallas kernels  116 us (7%)
  blocking collectives  86.3 us (5%)
    ppermute x58, waiting for transfers between devices, swap_bit(): return lax.ppermute(values, 'dp', [(i, i ^ bit) for i in range(data_count)])  289 us
    dot_general x6, matrix products, dot_last(): lax.dot_general(first_arg, second_arg, (((1,), (1,)), ((), ())), preferre...  117 us
    dot_general x6, matrix products, dot_first(): lax.dot_general(first_arg, second_arg, (((0,), (0,)), ((), ())), preferre...  92.1 us
    unnamed x276, local copies, waits for them, and re-layouts  84.2 us
    pallas_call x1, Pallas kernels, attend_back(): pl.pallas_call(functools.partial(attend_back_kernel, scale, rows), grid=(...  70.3 us
    all_to_all x1, waiting for transfers between devices, on_device(): early = lax.all_to_all(grad_attended[:, :tail], 'mp', 0, 0, tiled=True)  50.4 us
    all_to_all x2, waiting for transfers between devices, on_device(): late = lax.all_to_all(late, 'mp', 0, 0, tiled=True)  48.7 us
    dot_general x1, matrix products, on_device(): jnp.dot(grad_gateup, gate_t, preferred_element_type=jnp.float32)  45.6 us
  transfers between devices with their start and end apart: 87, of which 30 were waited for; matrix products, arithmetic and copies ran while one was open for 43% of the time, Pallas kernels for 7%

profile of v5, /device:TPU:0, one launch (start us, length us, event | category | flops | bytes accessed | tf_op | source)
XLA Modules:
  0.0 1732.3 jit_solution(5750381069475261541)
XLA Ops:
  115.5 10.8 collective-permute-done.6
  126.3 16.3 collective-permute-done.8
  219.0 15.5 collective-permute-done.10
  234.5 27.6 %collective-permute-done.11 = bf16[2,128,2560]{2,1,0:T(8,128)(2,1)} collective-permute-done((bf16[2,128,2560]{2,1,0:T(8,128)(2,1)}, bf16[2,128,2560]{2,1,0:T(8,128)(2,1)}, u32[]{:S(2)}, u32[]{:S(2)}) %collective-permute-start.11) | collective-permute-done | bytes 1310752 | tf_op jit(solution)/shard_map/ppermute | solution.py:184
  309.4 43.3 %shard_map.659 = (bf16[1024,1280]{1,0:T(8,128)(2,1)}, bf16[1024,2560]{1,0:T(8,128)(2,1)}, bf16[1024,2560]{1,0:T(8,128)(2,1)}, f32[10,16,128]{2,1,0:T(8,128)}) custom-call(bf16[1024,768]{1,0:T(8,128)(2,1)} %slice.317.query_latent_ref, bf16[1024,256]{1,0:T(8,128)(2,1)} %slice.318.keyval_latent_ref, bf16[768,2560]{1,0:T(8,128)(2,1)} %bitcast.530, ...), custom_call_target="tpu_custom_call" | custom-call | flops 21474836480 | bytes 20971520 | tf_op jit(solution)/shard_map/pallas_call | solution.py:557
  374.7 35.6 %all_to_all.213 = bf16[4,64,2560]{2,1,0:T(8,128)(2,1)} all-to-all(bf16[4,64,2560]{2,1,0:T(8,128)(2,1)} %copy.804), channel_id=1, replica_groups=mesh['dp'=8,'mp'=4] {'mp'}, dimensions={0} | all-to-all | bytes 2621440 | tf_op jit(solution)/shard_map/all_to_all | solution.py:805
  452.3 14.3 all-to-all-done.8
  492.9 11.1 multiply_reduce_fusion
  511.9 27.2 %collective-permute-done.22 = bf16[256,2560]{1,0:T(8,128)(2,1)} collective-permute-done((bf16[256,2560]{1,0:T(8,128)(2,1)S(1)}, bf16[256,2560]{1,0:T(8,128)(2,1)}, u32[]{:S(2)}, u32[]{:S(2)}) %collective-permute-start.22) | collective-permute-done | bytes 1310752 | tf_op jit(solution)/shard_map/ppermute | solution.py:184
  543.8 23.4 %collective-permute-done.23 = bf16[256,2560]{1,0:T(8,128)(2,1)} collective-permute-done((bf16[256,2560]{1,0:T(8,128)(2,1)S(1)}, bf16[256,2560]{1,0:T(8,128)(2,1)}, u32[]{:S(2)}, u32[]{:S(2)}) %collective-permute-start.23) | collective-permute-done | bytes 1310752 | tf_op jit(solution)/shard_map/ppermute | solution.py:184
  575.3 20.8 %collective-permute-done.30 = bf16[256,2560]{1,0:T(8,128)(2,1)S(1)} collective-permute-done((bf16[256,2560]{1,0:T(8,128)(2,1)}, bf16[256,2560]{1,0:T(8,128)(2,1)S(1)}, u32[]{:S(2)}, u32[]{:S(2)}) %collective-permute-start.30) | collective-permute-done | bytes 1310752 | tf_op jit(solution)/shard_map/ppermute | solution.py:184
  611.7 51.1 %fusion.35 = f32[4096,1792]{1,0:T(8,128)} fusion(bf16[4096,2560]{1,0:T(8,128)(2,1)} %constant_dynamic-update-slice_fusion, bf16[96,2560]{1,0:T(8,128)(2,1)S(1)} %broadcast_in_dim.245, bf16[800,2560]{1,0:T(8,128)(2,1)} %bitcast.586, bf16[800,2560]{1,0:T(8,128)(2,1)} %bitcast.584), kind=kOutput, calls=%fused_computation.111 | convolution fusion | flops 37617664000 | bytes 59015168 | tf_op jit(solution)/shard_map/dot_general | solution.py:105
  690.3 36.4 %multiply_convert_fusion.2 = (bf16[4096,896]{1,0:T(8,128)(2,1)}, bf16[4096,896]{1,0:T(8,128)(2,1)}, bf16[4096,896]{1,0:T(8,128)(2,1)}) fusion(f32[4096,1792]{1,0:T(8,128)} %fusion.35, bf16[4096,2560]{1,0:T(8,128)(2,1)} %constant_dynamic-update-slice_fusion.15, bf16[800,2560]{1,0:T(8,128)(2,1)} %all-gather.13.cloned.1.call-done), kind=kOutput, calls=%fused_computation.6 | convolution fusion | flops 18845532160 | bytes 76447744 | tf_op jit(solution)/shard_map/dot_general | solution.py:105
  726.7 45.6 %convolution_convert_fusion = bf16[4096,2560]{1,0:T(8,128)(2,1)} fusion(bf16[4096,896]{1,0:T(8,128)(2,1)} %get-tuple-element.583, bf16[4096,896]{1,0:T(8,128)(2,1)} %get-tuple-element.582, bf16[96,2560]{1,0:T(8,128)(2,1)S(1)} %broadcast_in_dim.245, bf16[800,2560]{1,0:T(8,128)(2,1)} %bitcast.587, bf16[800,2560]{1,0:T(8,128)(2,1)} %bitcast.585), kind=kOutput, calls=%fused_computation | convolution fusion | flops 37657509888 | bytes 44335104 | tf_op jit(solution)/shard_map/dot_general | solution.py:866
  784.3 23.1 %convolution_convert_fusion.5 = bf16[896,2560]{1,0:T(8,128)(2,1)} fusion(bf16[4096,896]{1,0:T(8,128)(2,1)S(1)} %copy-done.17, bf16[4096,2560]{1,0:T(8,128)(2,1)} %constant_dynamic-update-slice_fusion.15), kind=kOutput, calls=%fused_computation.27 | convolution fusion | flops 18792775680 | bytes 32899072 | tf_op jit(solution)/shard_map/dot_general | solution.py:99
  817.8 47.1 %convolution_convert_fusion.3 = bf16[1792,2560]{1,0:T(8,128)(2,1)} fusion(bf16[4096,2560]{1,0:T(8,128)(2,1)} %constant_dynamic-update-slice_fusion, bf16[4096,896]{1,0:T(8,128)(2,1)} %get-tuple-element.583, bf16[4096,896]{1,0:T(8,128)(2,1)} %get-tuple-element.582), kind=kOutput, calls=%fused_computation.11 | convolution fusion | flops 37614911488 | bytes 44826624 | tf_op jit(solution)/shard_map/dot_general | solution.py:99
  876.8 28.3 %collective-permute-done.51 = bf16[256,2560]{1,0:T(8,128)(2,1)S(1)} collective-permute-done((bf16[256,2560]{1,0:T(8,128)(2,1)S(1)}, bf16[256,2560]{1,0:T(8,128)(2,1)S(1)}, u32[]{:S(2)}, u32[]{:S(2)}) %collective-permute-start.51) | collective-permute-done | bytes 1310752 | tf_op jit(solution)/shard_map/ppermute | solution.py:184
  910.3 27.5 %collective-permute-done.52 = bf16[256,2560]{1,0:T(8,128)(2,1)S(1)} collective-permute-done((bf16[256,2560]{1,0:T(8,128)(2,1)S(1)}, bf16[256,2560]{1,0:T(8,128)(2,1)S(1)}, u32[]{:S(2)}, u32[]{:S(2)}) %collective-permute-start.52) | collective-permute-done | bytes 1310752 | tf_op jit(solution)/shard_map/ppermute | solution.py:184
  1003.8 9.2 fusion.1
  1013.0 50.4 %all-to-all-done.11 = bf16[4,64,2560]{2,1,0:T(8,128)(2,1)S(1)} async-done(((bf16[4,64,2560]{2,1,0:T(8,128)(2,1)}), bf16[4,64,2560]{2,1,0:T(8,128)(2,1)S(1)}, u32[]{:S(2)}, u32[]{:S(2)}) %all-to-all-start.11) | async-done | bytes 1310752 | tf_op jit(solution)/shard_map/all_to_all | solution.py:891
  1075.8 34.3 %all-to-all-done.12 = bf16[4,64,2560]{2,1,0:T(8,128)(2,1)} async-done(((bf16[4,64,2560]{2,1,0:T(8,128)(2,1)}), bf16[4,64,2560]{2,1,0:T(8,128)(2,1)}, u32[]{:S(2)}, u32[]{:S(2)}) %all-to-all-start.12) | async-done | bytes 1310752 | tf_op jit(solution)/shard_map/all_to_all | solution.py:899
  1152.5 28.2 %convolution_convert_fusion.1 = bf16[4096,2560]{1,0:T(8,128)(2,1)} fusion(bf16[4096,896]{1,0:T(8,128)(2,1)} %bitcast.514, bf16[800,2560]{1,0:T(8,128)(2,1)S(1)} %copy-done.102), kind=kOutput, calls=%fused_computation.1 | convolution fusion | flops 18800967680 | bytes 32407552 | tf_op jit(solution)/shard_map/dot_general | solution.py:900
  1180.8 70.3 %shard_map.660 = (bf16[1024,2560]{1,0:T(8,128)(2,1)}, bf16[1024,2560]{1,0:T(8,128)(2,1)}, f32[1024,128]{1,0:T(8,128)}) custom-call(bf16[1024,2560]{1,0:T(8,128)(2,1)} %get-tuple-element.185.query_ref, bf16[1024,2560]{1,0:T(8,128)(2,1)} %get-tuple-element.186.keyval_ref, bf16[1024,1280]{1,0:T(8,128)(2,1)} %bitcast.539, bf16[1024,128]{1,0:T(8,128)(2,1)} %pad.31.key_ref, ...), custom_call_target="tpu_custom_call" | custom-call | flops 42949672960 | bytes 20971520 | tf_op jit(solution)/shard_map/pallas_call | solution.py:591
  1340.9 9.1 fusion.21
  1389.3 8.8 copy.827
  1414.2 19.1 %collective-permute-done.61 = bf16[256,2560]{1,0:T(8,128)(2,1)} collective-permute-done((bf16[256,2560]{1,0:T(8,128)(2,1)}, bf16[256,2560]{1,0:T(8,128)(2,1)}, u32[]{:S(2)}, u32[]{:S(2)}) %collective-permute-start.61) | collective-permute-done | bytes 1310752 | tf_op jit(solution)/shard_map/ppermute | solution.py:184
  1433.3 28.8 %collective-permute-done.63 = bf16[256,2560]{1,0:T(8,128)(2,1)} collective-permute-done((bf16[256,2560]{1,0:T(8,128)(2,1)}, bf16[256,2560]{1,0:T(8,128)(2,1)}, u32[]{:S(2)}, u32[]{:S(2)}) %collective-permute-start.63) | collective-permute-done | bytes 1310752 | tf_op jit(solution)/shard_map/ppermute | solution.py:184
  1497.5 12.1 all-to-all-done.20
  1514.6 12.9 collective-permute-done.59
  1579.9 13.1 all-to-all-done.22
  1628.7 17.3 add_divide_fusion.1
  1714.6 10.7 fusion.18
  (779 shorter events, 885.8 us)
Async XLA Ops:
  9.2 63.1 %collective-permute-start = (bf16[320,264]{1,0:T(8,128)(2,1)}, bf16[320,264]{1,0:T(8,128)(2,1)}, u32[]{:S(2)}, u32[]{:S(2)}) collective-permute-start(bf16[320,264]{1,0:T(8,128)(2,1)} %copy.774), channel_id=1, source_target_pairs={{0,1},{1,2},{2,3},{3,0},{4,5},{5,6},{6,7},{7,4},{8,9},{9,10},{10,1... | collective-permute-start | bytes 506888 | tf_op jit(solution)/shard_map/ppermute | solution.py:263
  12.2 61.8 %collective-permute-start.1 = (bf16[320,264]{1,0:T(8,128)(2,1)}, bf16[320,264]{1,0:T(8,128)(2,1)}, u32[]{:S(2)}, u32[]{:S(2)}) collective-permute-start(bf16[320,264]{1,0:T(8,128)(2,1)} %copy.774), channel_id=1, source_target_pairs={{0,2},{1,3},{2,0},{3,1},{4,6},{5,7},{6,4},{7,5},{8,10},{9,11},{10,... | collective-permute-start | bytes 506888 | tf_op jit(solution)/shard_map/ppermute | solution.py:263
  14.8 61.0 %collective-permute-start.2 = (bf16[320,264]{1,0:T(8,128)(2,1)}, bf16[320,264]{1,0:T(8,128)(2,1)}, u32[]{:S(2)}, u32[]{:S(2)}) collective-permute-start(bf16[320,264]{1,0:T(8,128)(2,1)} %copy.774), channel_id=1, source_target_pairs={{0,3},{1,0},{2,1},{3,2},{4,7},{5,4},{6,5},{7,6},{8,11},{9,8},{10,9... | collective-permute-start | bytes 506888 | tf_op jit(solution)/shard_map/ppermute | solution.py:263
  22.4 260.5 %all-gather.11.cloned.1.call-start = ((), (), s32[]{:S(2)}) async-start(), calls=%async_computation.33 | async-start | bytes 2048000 | tf_op jit(solution)/shard_map/all_gather | solution.py:695
  62.7 79.8 %all-to-all-start = ((bf16[8,3,200,320]{3,2,1,0:T(8,128)(2,1)}), bf16[8,3,200,320]{3,2,1,0:T(8,128)(2,1)}, u32[]{:S(2)}, u32[]{:S(2)}) async-start(bf16[8,3,200,320]{3,2,1,0:T(8,128)(2,1)} %copy.784), calls=%async_computation | async-start | bytes 7372800 | tf_op jit(solution)/shard_map/all_to_all | solution.py:687
  67.2 228.9 %all-gather.7.cloned.1.call-start = ((), (), s32[]{:S(2)}) async-start(), calls=%async_computation.28 | async-start | bytes 5120000 | tf_op jit(solution)/shard_map/all_gather | solution.py:745
  197.9 64.2 %all-to-all-start.3 = ((bf16[4,128,1056]{1,2,0:T(8,128)(2,1)}), bf16[4,128,1056]{1,2,0:T(8,128)(2,1)}, u32[]{:S(2)}, u32[]{:S(2)}) async-start(bf16[4,128,1056]{1,2,0:T(8,128)(2,1)} %bitcast.527), calls=%async_computation.3 | async-start | bytes 2162688 | tf_op jit(solution)/shard_map/all_to_all | solution.py:741
  202.1 150.6 %all-gather.9.cloned.1.call-start = ((), (), s32[]{:S(2)}) async-start(), calls=%async_computation.29 | async-start | bytes 5120000 | tf_op jit(solution)/shard_map/all_gather | solution.py:752
  203.2 58.9 %collective-permute-start.11 = (bf16[2,128,2560]{2,1,0:T(8,128)(2,1)}, bf16[2,128,2560]{2,1,0:T(8,128)(2,1)}, u32[]{:S(2)}, u32[]{:S(2)}) collective-permute-start(bf16[2,128,2560]{2,1,0:T(8,128)(2,1)} %bitcast.36), channel_id=1, source_target_pairs={{0,16},{4,20},{8,24},{12,28},{16,0},{20,4},{24,8},{28,12},{1,17},{... | collective-permute-start | bytes 3932168 | tf_op jit(solution)/shard_map/ppermute | solution.py:184
  292.6 71.8 %collective-permute-start.14 = (bf16[320,2560]{1,0:T(8,128)(2,1)}, bf16[320,2560]{1,0:T(8,128)(2,1)}, u32[]{:S(2)}, u32[]{:S(2)}) collective-permute-start(bf16[320,2560]{1,0:T(8,128)(2,1)} %bitcast.245), channel_id=1, source_target_pairs={{0,8},{4,12},{8,0},{12,4},{16,24},{20,28},{24,16},{28,20},{1,9},{5... | collective-permute-start | bytes 4915208 | tf_op jit(solution)/shard_map/ppermute | solution.py:184
  294.1 73.3 %collective-permute-start.15 = (bf16[320,2560]{1,0:T(8,128)(2,1)}, bf16[320,2560]{1,0:T(8,128)(2,1)}, u32[]{:S(2)}, u32[]{:S(2)}) collective-permute-start(bf16[320,2560]{1,0:T(8,128)(2,1)} %bitcast.245), channel_id=1, source_target_pairs={{0,16},{4,20},{8,24},{12,28},{16,0},{20,4},{24,8},{28,12},{1,17},{... | collective-permute-start | bytes 4915208 | tf_op jit(solution)/shard_map/ppermute | solution.py:184
  294.6 72.8 %collective-permute-start.16 = (bf16[320,2560]{1,0:T(8,128)(2,1)}, bf16[320,2560]{1,0:T(8,128)(2,1)}, u32[]{:S(2)}, u32[]{:S(2)}) collective-permute-start(bf16[320,2560]{1,0:T(8,128)(2,1)} %bitcast.245), channel_id=1, source_target_pairs={{0,24},{4,28},{8,16},{12,20},{16,8},{20,12},{24,0},{28,4},{1,25},{... | collective-permute-start | bytes 4915208 | tf_op jit(solution)/shard_map/ppermute | solution.py:184
  424.5 60.1 %collective-permute-start.19 = (bf16[4,320,2560]{2,1,0:T(8,128)(2,1)}, bf16[4,320,2560]{2,1,0:T(8,128)(2,1)}, u32[]{:S(2)}, u32[]{:S(2)}) collective-permute-start(bf16[4,320,2560]{2,1,0:T(8,128)(2,1)} %bitcast_dynamic-update-slice_fusion.4), channel_id=1, source_target_pairs={{0,4},{4,0},{8,12},{12,8},{16,20},{20,16},{24,28},{28,24},{1,5},{5... | collective-permute-start | bytes 19660808 | tf_op jit(solution)/shard_map/ppermute | solution.py:184
  424.5 59.6 %collective-permute-start.17 = (bf16[512,2560]{1,0:T(8,128)(2,1)}, bf16[512,2560]{1,0:T(8,128)(2,1)}, u32[]{:S(2)}, u32[]{:S(2)}) collective-permute-start(bf16[512,2560]{1,0:T(8,128)(2,1)} %fusion.9), channel_id=1, source_target_pairs={{0,8},{4,12},{8,0},{12,4},{16,24},{20,28},{24,16},{28,20},{1,9},{5... | collective-permute-start | bytes 7864328 | tf_op jit(solution)/shard_map/ppermute | solution.py:184
  425.2 59.3 %collective-permute-start.18 = (bf16[512,2560]{1,0:T(8,128)(2,1)}, bf16[512,2560]{1,0:T(8,128)(2,1)}, u32[]{:S(2)}, u32[]{:S(2)}) collective-permute-start(bf16[512,2560]{1,0:T(8,128)(2,1)} %fusion.9), channel_id=1, source_target_pairs={{0,16},{4,20},{8,24},{12,28},{16,0},{20,4},{24,8},{28,12},{1,17},{... | collective-permute-start | bytes 7864328 | tf_op jit(solution)/shard_map/ppermute | solution.py:184
  434.9 255.4 %all-gather.13.cloned.1.call-start = ((), (), s32[]{:S(2)}) async-start(), calls=%async_computation.34 | async-start | bytes 5120000 | tf_op jit(solution)/shard_map/all_gather | solution.py:811
  511.1 624.6 %reduce-scatter.6.cloned.1.call-start = ((), (), s32[]{:S(2)}) async-start(), calls=%async_computation.31 | async-start | bytes 5120000 | tf_op jit(solution)/shard_map/reduce_scatter | solution.py:875
  511.1 63.6 %collective-permute-start.26 = (bf16[256,2560]{1,0:T(8,128)(2,1)S(1)}, bf16[256,2560]{1,0:T(8,128)(2,1)S(1)}, u32[]{:S(2)}, u32[]{:S(2)}) collective-permute-start(bf16[256,2560]{1,0:T(8,128)(2,1)S(1)} %get-tuple-element.617), channel_id=1, source_target_pairs={{0,16},{4,20},{8,24},{12,28},{16,0},{20,4},{24,8},{28,12},{1,17},{... | collective-permute-start | bytes 3932168 | tf_op jit(solution)/shard_map/ppermute | solution.py:184
  609.6 63.8 %collective-permute-start.34 = (bf16[512,2560]{1,0:T(8,128)(2,1)}, bf16[512,2560]{1,0:T(8,128)(2,1)}, u32[]{:S(2)}, u32[]{:S(2)}) collective-permute-start(bf16[512,2560]{1,0:T(8,128)(2,1)} %fusion.9), channel_id=1, source_target_pairs={{0,4},{4,0},{8,12},{12,8},{16,20},{20,16},{24,28},{28,24},{1,5},{5... | collective-permute-start | bytes 7864328 | tf_op jit(solution)/shard_map/ppermute | solution.py:184
  609.6 60.4 %collective-permute-start.37 = (bf16[512,2560]{1,0:T(8,128)(2,1)}, bf16[512,2560]{1,0:T(8,128)(2,1)S(1)}, u32[]{:S(2)}, u32[]{:S(2)}) collective-permute-start(bf16[512,2560]{1,0:T(8,128)(2,1)} %fusion.9), channel_id=1, source_target_pairs={{0,24},{4,28},{8,16},{12,20},{16,8},{20,12},{24,0},{28,4},{1,25},{... | collective-permute-start | bytes 7864328 | tf_op jit(solution)/shard_map/ppermute | solution.py:184
  611.2 69.0 %collective-permute-start.35 = (bf16[512,2560]{1,0:T(8,128)(2,1)}, bf16[512,2560]{1,0:T(8,128)(2,1)S(1)}, u32[]{:S(2)}, u32[]{:S(2)}) collective-permute-start(bf16[512,2560]{1,0:T(8,128)(2,1)} %collective-permute-done.17), channel_id=1, source_target_pairs={{0,4},{4,0},{8,12},{12,8},{16,20},{20,16},{24,28},{28,24},{1,5},{5... | collective-permute-start | bytes 7864328 | tf_op jit(solution)/shard_map/ppermute | solution.py:184
  611.4 73.9 %collective-permute-start.36 = (bf16[512,2560]{1,0:T(8,128)(2,1)}, bf16[512,2560]{1,0:T(8,128)(2,1)S(1)}, u32[]{:S(2)}, u32[]{:S(2)}) collective-permute-start(bf16[512,2560]{1,0:T(8,128)(2,1)} %collective-permute-done.18), channel_id=1, source_target_pairs={{0,4},{4,0},{8,12},{12,8},{16,20},{20,16},{24,28},{28,24},{1,5},{5... | collective-permute-start | bytes 7864328 | tf_op jit(solution)/shard_map/ppermute | solution.py:184
  991.0 72.4 %all-to-all-start.11 = ((bf16[4,64,2560]{2,1,0:T(8,128)(2,1)}), bf16[4,64,2560]{2,1,0:T(8,128)(2,1)S(1)}, u32[]{:S(2)}, u32[]{:S(2)}) async-start(bf16[4,64,2560]{2,1,0:T(8,128)(2,1)} %get-tuple-element.614), calls=%async_computation.11 | async-start | bytes 2621440 | tf_op jit(solution)/shard_map/all_to_all | solution.py:891
  1067.7 481.8 %reduce-scatter.8.cloned.1.call-start = ((), (), s32[]{:S(2)}) async-start(), calls=%async_computation.32 | async-start | bytes 10240000 | tf_op jit(solution)/shard_map/reduce_scatter | solution.py:909
  1139.3 132.1 %all-to-all-start.14 = ((bf16[8,200,320]{2,1,0:T(8,128)(2,1)}), bf16[8,200,320]{2,1,0:T(8,128)(2,1)S(1)}, u32[]{:S(2)}, u32[]{:S(2)}) async-start(bf16[8,200,320]{2,1,0:T(8,128)(2,1)} %copy.821), calls=%async_computation.16 | async-start | bytes 2457600 | tf_op jit(solution)/shard_map/all_to_all | solution.py:923
  1142.9 571.6 %reduce-scatter.4.cloned.1.call-start = ((), (), s32[]{:S(2)}) async-start(), calls=%async_computation.30 | async-start | bytes 23592960 | tf_op jit(solution)/shard_map/reduce_scatter | solution.py:903
  1149.0 102.0 %collective-permute-start.54 = (bf16[320,2560]{1,0:T(8,128)(2,1)}, bf16[320,2560]{1,0:T(8,128)(2,1)S(1)}, u32[]{:S(2)}, u32[]{:S(2)}) collective-permute-start(bf16[320,2560]{1,0:T(8,128)(2,1)} %get-tuple-element.601), channel_id=1, source_target_pairs={{0,8},{4,12},{8,0},{12,4},{16,24},{20,28},{24,16},{28,20},{1,9},{5... | collective-permute-start | bytes 4915208 | tf_op jit(solution)/shard_map/ppermute | solution.py:184
  1151.0 100.0 %collective-permute-start.55 = (bf16[320,2560]{1,0:T(8,128)(2,1)}, bf16[320,2560]{1,0:T(8,128)(2,1)}, u32[]{:S(2)}, u32[]{:S(2)}) collective-permute-start(bf16[320,2560]{1,0:T(8,128)(2,1)} %get-tuple-element.600), channel_id=1, source_target_pairs={{0,16},{4,20},{8,24},{12,28},{16,0},{20,4},{24,8},{28,12},{1,17},{... | collective-permute-start | bytes 4915208 | tf_op jit(solution)/shard_map/ppermute | solution.py:184
  1152.5 98.6 %collective-permute-start.56 = (bf16[320,2560]{1,0:T(8,128)(2,1)}, bf16[320,2560]{1,0:T(8,128)(2,1)}, u32[]{:S(2)}, u32[]{:S(2)}) collective-permute-start(bf16[320,2560]{1,0:T(8,128)(2,1)} %get-tuple-element.599), channel_id=1, source_target_pairs={{0,24},{4,28},{8,16},{12,20},{16,8},{20,12},{24,0},{28,4},{1,25},{... | collective-permute-start | bytes 4915208 | tf_op jit(solution)/shard_map/ppermute | solution.py:184
  1383.4 78.7 %collective-permute-start.63 = (bf16[256,2560]{1,0:T(8,128)(2,1)}, bf16[256,2560]{1,0:T(8,128)(2,1)}, u32[]{:S(2)}, u32[]{:S(2)}) collective-permute-start(bf16[256,2560]{1,0:T(8,128)(2,1)} %get-tuple-element.604), channel_id=1, source_target_pairs={{0,24},{4,28},{8,16},{12,20},{16,8},{20,12},{24,0},{28,4},{1,25},{... | collective-permute-start | bytes 3932168 | tf_op jit(solution)/shard_map/ppermute | solution.py:184
  1401.8 84.6 %collective-permute-start.57 = (bf16[4,320,1056]{2,1,0:T(8,128)(2,1)}, bf16[4,320,1056]{2,1,0:T(8,128)(2,1)}, u32[]{:S(2)}, u32[]{:S(2)}) collective-permute-start(bf16[4,320,1056]{2,1,0:T(8,128)(2,1)} %dynamic-slice_bitcast_fusion.1), channel_id=1, source_target_pairs={{0,4},{4,0},{8,12},{12,8},{16,20},{20,16},{24,28},{28,24},{1,5},{5... | collective-permute-start | bytes 8110088 | tf_op jit(solution)/shard_map/ppermute | solution.py:184
  1611.7 62.8 %all-to-all-start.24 = ((f32[4,92,256]{2,1,0:T(8,128)}), f32[4,92,256]{2,1,0:T(8,128)S(1)}, u32[]{:S(2)}, u32[]{:S(2)}) async-start(f32[4,92,256]{2,1,0:T(8,128)} %broadcast_in_dim.250), calls=%async_computation.27 | async-start | bytes 786432 | tf_op jit(solution)/shard_map/all_to_all | solution.py:173
  (167 other events, 4016.2 us)
Sparse Core Ops, SparseCore 0:
  25.4 37.5 all-gather.10
  159.8 98.7 all-gather.6
  260.7 77.5 all-gather.8
  511.2 77.0 all-gather.12
  980.9 105.7 reduce-scatter.5
  1125.1 140.3 reduce-scatter.7
  1269.1 159.0 reduce-scatter.3
